TPU v7x, 128 devices: a whole 4x4x4 slice. The times are simulated.
128 devices in a mesh: wall: 8 (over z_lo, y), gas: 16 (over x, z_hi, core).
Axes of the slice: x: 4, y: 4, z: 4 (z_hi: 2, z_lo: 2; z = z_hi * 2 + z_lo), core: 2. Of those that a mesh axis runs over, the one named last changes fastest.
Arguments:
- gas_state: float32 [3, 4, 1024, 8192], P(None, None, 'wall', 'gas'), may hold values from -8 to 8
- wall_flags: int32 [1024, 64], P('wall', 'gas'), may hold values from 0 to 128
- film_state: float32 [4, 1024, 8192], P(None, 'wall', 'gas'), may hold values from -12 to 12, as said below
- deposit: float32 [1024, 8192], P('wall', 'gas'), may hold values from 0.05 to 1
- owner_map: int32 [8, 16], replicated, may hold values from 0 to 15, each once within a row
Outputs:
- film_out: float32 [4, 1024, 8192], P(None, ('wall', 'gas'))
- cfl: float32 [], replicated
Inputs may be any that keep to these rules, and one draw needn't show every extreme that they name: film_state[0] is positive. `owner_map`: each row is a permutation of 0 to 16 - 1.
All inputs are finite; a program needn't handle non-finite values.
Results may differ from a plain program's by a relative error of at most 0.00002.
Values sent between devices are 32-bit elements; how exact they have to be, the bound alone decides.
No kernel may reach another device: no remote copies, remote signals or barrier semaphores. Data moves between devices by JAX's collectives and lax.ppermute only.
A program may use at most 64 MiB of HBM per device.

v0:
```python
import jax
import jax.numpy as jnp
from jax import lax
from jax.sharding import PartitionSpec as P

SUBSTEPS = 4


LAYER_WEIGHTS = (0.1, 0.2, 0.3, 0.4)
KAPPA = 0.41
HEIGHT_RATIO = 20.0
SPEED_FLOOR = 0.5
PRANDTL_TURB = 0.85
PRANDTL_JUMP = 3.0
LAMINAR_SHEAR = 0.3
LAMINAR_HEAT = 0.2
FILM_SPREAD = 0.24
FILM_FLOOR = 0.3
FRICTION = 0.5
GRAVITY = 1.0
COURANT = 6.0


def with_halo(value, sides, width):
    for axis, dim in sides:
        size, length = (lax.axis_size(axis), value.shape[dim])
        up = [(i, (i + 1) % size) for i in range(size)]
        down = [(j, i) for i, j in up]
        last = lax.slice_in_dim(value, length - width, length, axis=dim)
        leading = lax.slice_in_dim(value, 0, width, axis=dim)
        before = lax.ppermute(last, axis, up)
        after = lax.ppermute(leading, axis, down)
        value = jnp.concatenate([before, value, after], axis=dim)
    return value


def reichardt(scaled_height):
    return jnp.log1p(KAPPA * scaled_height) / KAPPA + 7.8 * (
        1.0 - jnp.exp(-scaled_height / 11.0) - scaled_height / 11.0 * jnp.exp(-scaled_height / 3.0)
    )


def surface_forcing(filtered, film_heat, attached, deposit):
    along, across, gas_heat = (filtered[0], filtered[1], filtered[2])
    wall_speed = jnp.sqrt(along * along + across * across + SPEED_FLOOR * SPEED_FLOOR)
    scaled_height = jnp.sqrt(HEIGHT_RATIO * wall_speed)
    scaled_speed = reichardt(scaled_height)
    factor = wall_speed / (scaled_speed * scaled_speed)
    contrast = gas_heat - film_heat
    shear_along = jnp.where(attached, factor * along, LAMINAR_SHEAR * along)
    shear_across = jnp.where(attached, factor * across, LAMINAR_SHEAR * across)
    heat_flux = jnp.where(
        attached,
        wall_speed * contrast / (PRANDTL_TURB * scaled_speed + PRANDTL_JUMP),
        LAMINAR_HEAT * contrast,
    )
    return jnp.stack([shear_along, shear_across, heat_flux, deposit])


def peak_speed(film_now):
    thickness = jnp.sqrt(film_now[0] * film_now[0] + FILM_FLOOR * FILM_FLOOR)
    moving = jnp.sqrt(film_now[1] * film_now[1] + film_now[2] * film_now[2])
    return jnp.max(moving / thickness + jnp.sqrt(GRAVITY * thickness))


def advance(padded, forcing, time_step):
    centre = padded[:, 1:-1, 1:-1]
    north_side = padded[:, :-2, 1:-1]
    south_side = padded[:, 2:, 1:-1]
    west_side = padded[:, 1:-1, :-2]
    east_side = padded[:, 1:-1, 2:]
    spread = north_side + south_side + west_side + east_side - 4.0 * centre
    height = centre[0]
    thickness = jnp.sqrt(height * height + FILM_FLOOR * FILM_FLOOR)
    divergence = 0.5 * (east_side[1] - west_side[1]) + 0.5 * (south_side[2] - north_side[2])
    slope_along = 0.5 * (east_side[0] - west_side[0])
    slope_across = 0.5 * (south_side[0] - north_side[0])
    new_height = height + FILM_SPREAD * spread[0] + time_step * (forcing[3] - divergence)
    new_along = (
        centre[1]
        + FILM_SPREAD * spread[1]
        + time_step
        * (forcing[0] - FRICTION * centre[1] / thickness - GRAVITY * height * slope_along)
    )
    new_across = (
        centre[2]
        + FILM_SPREAD * spread[2]
        + time_step
        * (forcing[1] - FRICTION * centre[2] / thickness - GRAVITY * height * slope_across)
    )
    new_heat = centre[3] + FILM_SPREAD * spread[3] + time_step * forcing[2] / thickness
    return jnp.stack([new_height, new_along, new_across, new_heat])


def per_device(gas_state, wall_flags, film_state, deposit, owner_map):
    tile_rows, tile_cols = (film_state.shape[1], film_state.shape[2])
    gas_count = lax.axis_size("gas")
    strip_rows = tile_rows // gas_count
    sampled = LAYER_WEIGHTS[0] * gas_state[:, 0]
    for layer in range(1, gas_state.shape[1]):
        sampled = sampled + LAYER_WEIGHTS[layer] * gas_state[:, layer]
    padded = with_halo(sampled, (("wall", 1), ("gas", 2)), 1)
    row_sum = padded[:, :-2] + padded[:, 1:-1] + padded[:, 2:]
    filtered = (row_sum[:, :, :-2] + row_sum[:, :, 1:-1] + row_sum[:, :, 2:]) / 9.0
    position = lax.broadcasted_iota(jnp.int32, (1, 1, 128), 2)
    attached = (position < wall_flags[:, :, None]).reshape(tile_rows, tile_cols)
    forcing = surface_forcing(filtered, film_state[3], attached, deposit)
    time_step = COURANT / lax.pmax(peak_speed(film_state), ("wall", "gas"))
    own_map = owner_map[lax.axis_index("wall")]
    slots = jnp.arange(gas_count, dtype=jnp.int32)
    inverse_row = jnp.sum(
        slots[None, :] * (own_map[None, :] == slots[:, None]).astype(jnp.int32), axis=1
    )
    bundle = jnp.concatenate([film_state, forcing], axis=0)
    extended = with_halo(bundle, (("wall", 1),), SUBSTEPS)
    window = jnp.arange(strip_rows + 2 * SUBSTEPS, dtype=jnp.int32)
    row_index = inverse_row[:, None] * strip_rows + window[None, :]
    pieces = extended[:, row_index]
    arrived = lax.all_to_all(pieces, "gas", split_axis=1, concat_axis=3, tiled=True)[:, 0]
    film_now = arrived[:4]
    pulled = arrived[4:]
    total = arrived.shape[1]
    for substep in range(SUBSTEPS):
        wrapped = jnp.concatenate([film_now[:, :, -1:], film_now, film_now[:, :, :1]], axis=2)
        film_now = advance(wrapped, pulled[:, substep + 1 : total - substep - 1], time_step)
    cfl = time_step * lax.pmax(peak_speed(film_now), ("wall", "gas"))
    return (film_now, cfl)


def solution(mesh):
    return jax.shard_map(
        per_device,
        mesh=mesh,
        in_specs=(
            P(None, None, "wall", "gas"),
            P("wall", "gas"),
            P(None, "wall", "gas"),
            P("wall", "gas"),
            P(),
        ),
        out_specs=(P(None, ("wall", "gas"), None), P()),
        check_vma=False,
    )
```

profile of v0, /device:TPU:1, one launch (start us, length us, event | category | flops | bytes accessed | tf_op | source)
XLA Modules:
  0.0 269.7 jit_solution(3725248022279518884)
XLA Ops:
  0.6 0.0 copy-start
  0.7 2.3 fusion.16
  2.9 0.0 copy-start.4
  3.0 2.2 collective-permute-start
  5.2 2.9 %collective-permute-start.1 = (f32[3,1,512]{2,1,0:T(1,128)S(1)}, f32[3,1,512]{2,1,0:T(1,128)S(1)}, u32[]{:S(2)}, u32[]{:S(2)}) collective-permute-start(f32[3,1,512]{2,1,0:T(1,128)S(1)} %get-tuple-element.36), channel_id=1, source_target_pairs={{16,0},{32,16},{48,32},{64,48},{80,64},{96,80},{112,96},{0,112},{1... | collective-permute-start | bytes 18440 | tf_op jit(solution)/shard_map/ppermute | solution.py:32
  8.0 0.1 select_reduce_fusion
  8.2 0.1 compare_select_fusion
  8.2 0.7 collective-permute-done
  9.0 0.8 pad_maximum_fusion.28
  9.8 4.8 %collective-permute-start.2 = (f32[3,130,1]{2,1,0:T(8,128)}, f32[3,130,1]{2,1,0:T(8,128)}, u32[]{:S(2)}, u32[]{:S(2)}) collective-permute-start(f32[3,130,1]{2,1,0:T(8,128)} %get-tuple-element.33), channel_id=1, source_target_pairs={{0,1},{1,2},{2,3},{3,4},{4,5},{5,6},{6,7},{7,8},{8,9},{9,10},{10,1... | collective-permute-start | bytes 4688 | tf_op jit(solution)/shard_map/ppermute | solution.py:31
  14.6 0.1 reshape.169
  14.7 0.1 copy.31
  14.8 0.2 lt.48
  15.0 0.1 lt.49
  15.1 0.2 stack.10
  15.3 0.7 copy.36
  16.0 1.7 collective-permute-done.2
  17.7 4.4 %collective-permute-done.3 = f32[3,130,1]{2,1,0:T(8,128)} collective-permute-done((f32[3,130,1]{2,1,0:T(8,128)}, f32[3,130,1]{2,1,0:T(8,128)}, u32[]{:S(2)}, u32[]{:S(2)}) %collective-permute-start.3) | collective-permute-done | bytes 1592 | tf_op jit(solution)/shard_map/ppermute | solution.py:32
  22.0 1.5 pad_maximum_fusion.23
  23.5 0.2 slice_add_fusion.10
  23.7 0.5 fusion.14
  24.2 1.3 multiply_select_fusion
  25.5 0.5 multiply_select_fusion.1
  26.0 1.0 copy.39
  27.0 1.0 copy.38
  27.9 1.0 copy.37
  28.9 4.4 %concatenate.42 = f32[8,128,512]{2,0,1:T(8,128)S(1)} concatenate(f32[4,128,512]{2,0,1:T(4,128)S(1)} %copy.36, f32[1,128,512]{2,0,1:T(1,128)} %copy.37, f32[1,128,512]{2,0,1:T(1,128)} %copy.38, f32[1,128,512]{2,0,1:T(1,128)} %copy.39, f32[1,128,512]{2,0,1:T(1,128)S(1)} %stack.10), dimensions={0} | concatenate | bytes 4194304 | tf_op jit(solution)/shard_map/concatenate | solution.py:114
  33.3 0.6 collective-permute-start.4
  33.9 3.5 %collective-permute-start.5 = (f32[8,4,512]{2,0,1:T(8,128)S(1)}, f32[8,4,512]{2,0,1:T(8,128)S(1)}, u32[]{:S(2)}, u32[]{:S(2)}) collective-permute-start(f32[8,4,512]{2,0,1:T(8,128)S(1)} %get-tuple-element.29), channel_id=1, source_target_pairs={{16,0},{32,16},{48,32},{64,48},{80,64},{96,80},{112,96},{0,112},{1... | collective-permute-start | bytes 196616 | tf_op jit(solution)/shard_map/ppermute | solution.py:32
  37.4 1.6 collective-permute-done.4
  39.0 1.8 pad_maximum_fusion
  40.8 3.0 %gather_fusion = f32[256,8,512]{2,1,0:T(8,128)} fusion(f32[8,136,512]{2,0,1:T(8,128)S(1)} %pad_maximum_fusion, s32[1024]{0:T(1024)S(1)} %pad_clamp_fusion), kind=kCustom, calls=%fused_computation | custom fusion | bytes 8389632 | tf_op jit(solution)/shard_map/gather | solution.py:118
  43.8 6.8 %all-to-all-start = ((f32[8,16,16,512]{3,0,2,1:T(8,128)}), f32[8,16,16,512]{3,0,2,1:T(8,128)}, u32[]{:S(2)}, u32[]{:S(2)}) async-start(f32[8,16,16,512]{3,0,2,1:T(8,128)} %bitcast.44), calls=%async_computation | async-start | bytes 8388608 | tf_op jit(solution)/shard_map/all_to_all | solution.py:119
  50.6 118.0 %pmax.14 = f32[]{:T(128)} all-reduce(f32[]{:T(128)} %get-tuple-element.30), channel_id=1, replica_groups=mesh['wall'=8,'gas'=16] {'wall','gas'}, use_global_device_ids=true, to_apply=%region_2.3 | all-reduce | flops 1 | bytes 8 | tf_op jit(solution)/shard_map/pmax | solution.py:108
  169.3 6.0 %fusion.104 = (f32[4,1,16,16,512]{4,0,2,3,1:T(4,128)S(1)}, f32[4,1,16,16,512]{4,0,2,3,1:T(4,128)}) fusion(f32[8,1,16,16,512]{4,0,2,3,1:T(8,128)} %bitcast.6), kind=kLoop, calls=%fused_computation.225 | loop fusion | bytes 8388608 | tf_op jit(solution)/shard_map/slice | solution.py:120
  175.3 2.6 copy.40
  177.8 1.7 slice.537
  179.6 0.1 fusion.105
  179.7 4.2 %copy.41 = f32[4,1,16,16,512]{4,3,2,0,1:T(8,128)} copy(f32[4,1,16,16,512]{4,0,2,3,1:T(4,128)} %get-tuple-element.16) | data formatting | bytes 4194304 | tf_op jit(solution)/shard_map/slice | solution.py:121
  183.8 2.7 %slice.551 = f32[4,16,8192]{2,1,0:T(8,128)} reshape(f32[4,1,16,16,512]{4,3,2,0,1:T(8,128)} %copy.41) | data formatting | bytes 4194304 | tf_op jit(solution)/shard_map/slice | solution.py:121
  186.6 1.2 fusion.8
  187.8 0.4 copy-done.2
  188.2 0.8 fusion.25
  188.9 0.5 fusion.76
  189.5 0.1 pad_maximum_fusion.19
  189.6 1.4 fusion.5
  191.0 1.0 fusion.12
  192.0 0.5 fusion.67
  192.5 0.6 fusion.61
  193.1 0.5 fusion.55
  193.6 0.1 pad_maximum_fusion.20
  193.8 1.6 fusion.3
  195.4 1.0 fusion.11
  196.4 0.6 fusion.40
  197.0 0.5 fusion.46
  197.5 0.5 fusion.34
  198.0 0.1 pad_maximum_fusion.21
  198.2 1.4 fusion.1
  199.6 0.5 fusion.13
  200.1 2.1 add_reduce_fusion
  202.2 62.7 %pmax.15 = f32[]{:T(128)} all-reduce(f32[]{:T(128)} %get-tuple-element.2), channel_id=1, replica_groups=mesh['wall'=8,'gas'=16] {'wall','gas'}, use_global_device_ids=true, to_apply=%region_4.5 | all-reduce | flops 1 | bytes 8 | tf_op jit(solution)/shard_map/pmax | solution.py:126
  265.5 0.0 copy-start.5
  265.6 1.9 multiply_add_fusion.1
  267.5 1.0 pad_maximum_fusion.22
  (22 shorter events, 0.1 us)
Async XLA Ops:
  0.6 7.4 %copy-start = (s32[8,16]{1,0:T(8,128)S(1)}, s32[8,16]{1,0:T(8,128)}, u32[]{:S(2)}) copy-start(s32[8,16]{1,0:T(8,128)} %param.9) | copy-start | bytes 1540
  0.6 14.0 %copy-start.7 = (s32[128,4]{0,1:T(4,128)S(1)}, s32[128,4]{0,1:T(4,128)}, u32[]{:S(2)}) copy-start(s32[128,4]{0,1:T(4,128)} %param.6) | copy-start | bytes 6148
  0.7 14.4 %copy-start.6 = (f32[128,512]{1,0:T(8,128)S(1)}, f32[128,512]{1,0:T(8,128)}, u32[]{:S(2)}) copy-start(f32[128,512]{1,0:T(8,128)} %param.8) | copy-start | bytes 786436
  2.9 12.4 %copy-start.4 = (f32[4,128,512]{2,1,0:T(8,128)S(1)}, f32[4,128,512]{2,1,0:T(8,128)}, u32[]{:S(2)}) copy-start(f32[4,128,512]{2,1,0:T(8,128)} %param.7) | copy-start | bytes 3145732
  3.0 6.0 %collective-permute-start = (f32[3,1,512]{2,1,0:T(1,128)S(1)}, f32[3,1,512]{2,1,0:T(1,128)S(1)}, u32[]{:S(2)}, u32[]{:S(2)}) collective-permute-start(f32[3,1,512]{2,1,0:T(1,128)S(1)} %get-tuple-element.35), channel_id=1, source_target_pairs={{0,16},{16,32},{32,48},{48,64},{64,80},{80,96},{96,112},{112,0},{1... | collective-permute-start | bytes 18440 | tf_op jit(solution)/shard_map/ppermute | solution.py:31
  5.2 3.8 %collective-permute-start.1 = (f32[3,1,512]{2,1,0:T(1,128)S(1)}, f32[3,1,512]{2,1,0:T(1,128)S(1)}, u32[]{:S(2)}, u32[]{:S(2)}) collective-permute-start(f32[3,1,512]{2,1,0:T(1,128)S(1)} %get-tuple-element.36), channel_id=1, source_target_pairs={{16,0},{32,16},{48,32},{64,48},{80,64},{96,80},{112,96},{0,112},{1... | collective-permute-start | bytes 18440 | tf_op jit(solution)/shard_map/ppermute | solution.py:32
  9.8 7.9 %collective-permute-start.2 = (f32[3,130,1]{2,1,0:T(8,128)}, f32[3,130,1]{2,1,0:T(8,128)}, u32[]{:S(2)}, u32[]{:S(2)}) collective-permute-start(f32[3,130,1]{2,1,0:T(8,128)} %get-tuple-element.33), channel_id=1, source_target_pairs={{0,1},{1,2},{2,3},{3,4},{4,5},{5,6},{6,7},{7,8},{8,9},{9,10},{10,1... | collective-permute-start | bytes 4688 | tf_op jit(solution)/shard_map/ppermute | solution.py:31
  14.6 7.5 %collective-permute-start.3 = (f32[3,130,1]{2,1,0:T(8,128)}, f32[3,130,1]{2,1,0:T(8,128)}, u32[]{:S(2)}, u32[]{:S(2)}) collective-permute-start(f32[3,130,1]{2,1,0:T(8,128)} %get-tuple-element.34), channel_id=1, source_target_pairs={{1,0},{2,1},{3,2},{4,3},{5,4},{6,5},{7,6},{8,7},{9,8},{10,9},{11,1... | collective-permute-start | bytes 4688 | tf_op jit(solution)/shard_map/ppermute | solution.py:32
  33.3 5.7 %copy-start.3 = (f32[8,128,512]{2,0,1:T(8,128)}, f32[8,128,512]{2,0,1:T(8,128)S(1)}, u32[]{:S(2)}) copy-start(f32[8,128,512]{2,0,1:T(8,128)S(1)} %concatenate.42) | copy-start | bytes 6291460
  33.3 5.7 %collective-permute-start.4 = (f32[8,4,512]{2,0,1:T(8,128)S(1)}, f32[8,4,512]{2,0,1:T(8,128)S(1)}, u32[]{:S(2)}, u32[]{:S(2)}) collective-permute-start(f32[8,4,512]{2,0,1:T(8,128)S(1)} %get-tuple-element.28), channel_id=1, source_target_pairs={{0,16},{16,32},{32,48},{48,64},{64,80},{80,96},{96,112},{112,0},{1... | collective-permute-start | bytes 196616 | tf_op jit(solution)/shard_map/ppermute | solution.py:31
  33.9 5.1 %collective-permute-start.5 = (f32[8,4,512]{2,0,1:T(8,128)S(1)}, f32[8,4,512]{2,0,1:T(8,128)S(1)}, u32[]{:S(2)}, u32[]{:S(2)}) collective-permute-start(f32[8,4,512]{2,0,1:T(8,128)S(1)} %get-tuple-element.29), channel_id=1, source_target_pairs={{16,0},{32,16},{48,32},{64,48},{80,64},{96,80},{112,96},{0,112},{1... | collective-permute-start | bytes 196616 | tf_op jit(solution)/shard_map/ppermute | solution.py:32
  43.8 125.5 %all-to-all-start = ((f32[8,16,16,512]{3,0,2,1:T(8,128)}), f32[8,16,16,512]{3,0,2,1:T(8,128)}, u32[]{:S(2)}, u32[]{:S(2)}) async-start(f32[8,16,16,512]{3,0,2,1:T(8,128)} %bitcast.44), calls=%async_computation | async-start | bytes 8388608 | tf_op jit(solution)/shard_map/all_to_all | solution.py:119
  186.6 1.6 copy-start.2
  265.5 2.0 copy-start.5
  265.6 3.0 %copy-start.1 = (s32[8,16]{1,0:T(8,128)S(1)}, s32[8,16]{1,0:T(8,128)}, u32[]{:S(2)}) copy-start(s32[8,16]{1,0:T(8,128)} %param.9) | copy-start | bytes 1540
where the time goes:
time: 271 us; the launch traced here: 270 us
  blocking collectives  181 us (67%)
  local copies, waits for them, and re-layouts  29.4 us (11%)
  other arithmetic  27.1 us (10%)
  starting transfers between devices  20.7 us (8%)
  waiting for transfers between devices  8.35 us (3%)
  between operations  3.38 us (1%)
    pmax x1, blocking collectives, per_device(): time_step = COURANT / lax.pmax(peak_speed(film_state), ('wall', 'gas'))  118 us
    pmax x1, blocking collectives, per_device(): cfl = time_step * lax.pmax(peak_speed(film_now), ('wall', 'gas'))  62.7 us
    slice x3, local copies, waits for them, and re-layouts, per_device(): film_now = arrived[:4]  10.3 us
    ppermute x3, starting transfers between devices, with_halo(): before = lax.ppermute(last, axis, up)  7.56 us
    slice x2, local copies, waits for them, and re-layouts, per_device(): pulled = arrived[4:]  6.9 us
    all_to_all x1, starting transfers between devices, per_device(): lax.all_to_all(pieces, 'gas', split_axis=1, concat_axis=3, tiled=True)[:, 0]  6.76 us
    ppermute x3, starting transfers between devices, with_halo(): after = lax.ppermute(leading, axis, down)  6.36 us
  transfers between devices with their start and end apart: 7, of which 4 were waited for; matrix products, arithmetic and copies ran while one was open for 1% of the time, Pallas kernels for 0%

commit v1 on v0

v1 whole, which is shorter than its diff:
```python
import functools

import jax
import jax.numpy as jnp
from jax import lax
from jax.experimental import pallas as pl
from jax.experimental.pallas import tpu as pltpu
from jax.sharding import PartitionSpec as P

SUBSTEPS = 4
LAYER_WEIGHTS = (0.1, 0.2, 0.3, 0.4)
KAPPA = 0.41
HEIGHT_RATIO = 20.0
SPEED_FLOOR = 0.5
PRANDTL_TURB = 0.85
PRANDTL_JUMP = 3.0
LAMINAR_SHEAR = 0.3
LAMINAR_HEAT = 0.2
FILM_SPREAD = 0.24
FILM_FLOOR = 0.3
FRICTION = 0.5
COURANT = 6.0

ROWS = 128
COLS = 512
LANES = 128
TILES = COLS // LANES
HALO = SUBSTEPS
FIELDS = 9
STRIP = 8
RING = ROWS + 16
VMEM_LIMIT = 48 * 1024 * 1024


def lane_iota(shape):
    return lax.broadcasted_iota(jnp.int32, shape, len(shape) - 1)


def film_speed(height, along, across):
    square = height * height + FILM_FLOOR * FILM_FLOOR
    thickness = jnp.sqrt(square)
    moving = jnp.sqrt(along * along + across * across)
    return moving / thickness + jnp.sqrt(thickness)


def pack_columns(rows_of, count, left):
    lane = lane_iota((count, LANES))
    packed = jnp.zeros((count, LANES), jnp.float32)
    for field in range(FIELDS):
        shift = (4 * field) if left else (4 * field + 4)
        value = rows_of(field)
        if shift:
            value = pltpu.roll(value, shift, 1)
        packed = jnp.where((lane >= 4 * field) & (lane < 4 * field + 4), value, packed)
    return packed


def edges_kernel(
    gas, flags, film, deposit, sampled, to_north, to_south, core_pack, chip_pack, peak
):
    lane8 = lane_iota((STRIP, LANES))
    best = jnp.zeros((STRIP, LANES), jnp.float32)
    for tile in range(TILES):
        cols = slice(tile * LANES, (tile + 1) * LANES)
        for field in range(3):
            value = LAYER_WEIGHTS[0] * gas[field, 0, :, cols]
            for layer in range(1, 4):
                value = value + LAYER_WEIGHTS[layer] * gas[field, layer, :, cols]
            sampled[field, :, cols] = value
        speed = film_speed(film[0, :, cols], film[1, :, cols], film[2, :, cols])
        for row in range(0, ROWS, STRIP):
            best = jnp.maximum(best, speed[row : row + STRIP])
    peak[...] = jnp.broadcast_to(jnp.max(best, keepdims=True), (ROWS, LANES))

    def attached(rows, tile):
        count = flags[rows, tile : tile + 1]
        return jnp.where(lane_iota((count.shape[0], LANES)) < count, 1.0, 0.0)

    def value_of(field, rows, tile):
        cols = slice(tile * LANES, (tile + 1) * LANES)
        if field < 4:
            return film[field, rows, cols]
        if field < 7:
            return sampled[field - 4, rows, cols]
        if field == 7:
            return deposit[rows, cols]
        return attached(rows, tile)

    for field in range(FIELDS):
        for tile in range(TILES):
            cols = slice(tile * LANES, (tile + 1) * LANES)
            out = slice(4 * field, 4 * field + 4)
            to_north[out, cols] = value_of(field, slice(0, 4), tile)
            to_south[out, cols] = value_of(field, slice(ROWS - 4, ROWS), tile)

    even = lax.rem(lax.axis_index("gas"), 2) == 0
    every = slice(0, ROWS)
    west = pack_columns(lambda f: value_of(f, every, 0), ROWS, True)
    east = pack_columns(lambda f: value_of(f, every, TILES - 1), ROWS, False)
    core_pack[4 : 4 + ROWS, :] = jnp.where(even, east, west)
    chip_pack[4 : 4 + ROWS, :] = jnp.where(even, west, east)


def corners_kernel(from_north, from_south, core_in, chip_in, core_pack, chip_pack):
    even = lax.rem(lax.axis_index("gas"), 2) == 0
    core_pack[4 : 4 + ROWS, :] = core_in[4 : 4 + ROWS, :]
    chip_pack[4 : 4 + ROWS, :] = chip_in[4 : 4 + ROWS, :]
    for source, start in ((from_north, 0), (from_south, 4 + ROWS)):
        west = pack_columns(lambda f: source[4 * f : 4 * f + 4, 0:LANES], 4, True)
        east = pack_columns(
            lambda f: source[4 * f : 4 * f + 4, COLS - LANES : COLS], 4, False
        )
        core_pack[start : start + 4, :] = jnp.where(even, east, west)
        chip_pack[start : start + 4, :] = jnp.where(even, west, east)


def shifted_lanes(tiles):
    lane = lane_iota(tiles[0].shape)
    plus = [pltpu.roll(t, 1, 1) for t in tiles]
    minus = [pltpu.roll(t, LANES - 1, 1) for t in tiles]
    count = len(tiles)
    west = [jnp.where(lane == 0, plus[i - 1], plus[i]) for i in range(count)]
    east = [
        jnp.where(lane == LANES - 1, minus[(i + 1) % count], minus[i])
        for i in range(count)
    ]
    return west, east


def film_kernel(
    owner_map,
    film,
    sampled,
    flags,
    deposit,
    from_north,
    from_south,
    core_pack,
    chip_pack,
    peaks,
    out,
    peak,
    ring_a,
    ring_b,
    gas_ring,
    force,
):
    count = TILES + 1
    inner = slice(8, 8 + ROWS)
    even = lax.rem(lax.axis_index("gas"), 2) == 0
    wall = lax.axis_index("wall")
    step = COURANT / jnp.max(peaks[...])

    refs = [ring_a.at[f] for f in range(4)] + [gas_ring.at[f] for f in range(3)]
    refs += [force.at[3], force.at[0]]
    for field in range(FIELDS):
        ref = refs[field]
        for tile in range(TILES):
            cols = slice(tile * LANES, (tile + 1) * LANES)
            if field < 4:
                ref[tile, inner, :] = film[field, :, cols]
            elif field < 7:
                ref[tile, inner, :] = sampled[field - 4, :, cols]
            elif field == 7:
                ref[tile, inner, :] = deposit[:, cols]
            else:
                ref[tile, inner, :] = jnp.where(
                    lane_iota((ROWS, LANES)) < flags[:, tile : tile + 1], 1.0, 0.0
                )
            ref[tile, 4:8, :] = from_north[4 * field : 4 * field + 4, cols]
            ref[tile, 8 + ROWS : 12 + ROWS, :] = from_south[
                4 * field : 4 * field + 4, cols
            ]
    lane = lane_iota((ROWS + 8, LANES))
    core, chip = core_pack[...], chip_pack[...]
    east_side = jnp.where(even, core, chip)
    west_side = jnp.where(even, chip, core)
    for field in range(FIELDS):
        value = jnp.where(
            lane < LANES // 2,
            pltpu.roll(east_side, (LANES - 4 * field) % LANES, 1),
            pltpu.roll(west_side, (LANES - 4 - 4 * field) % LANES, 1),
        )
        refs[field][TILES, 4 : 12 + ROWS, :] = value

    def forcing_rows(index, carry):
        row = 4 + 8 * index
        here = pl.ds(row, STRIP)
        filtered = []
        for field in range(3):
            summed = [
                gas_ring[field, t, pl.ds(row - 1, STRIP), :]
                + gas_ring[field, t, here, :]
                + gas_ring[field, t, pl.ds(row + 1, STRIP), :]
                for t in range(count)
            ]
            west, east = shifted_lanes(summed)
            filtered.append(
                [(west[t] + summed[t] + east[t]) * (1.0 / 9.0) for t in range(count)]
            )
        for t in range(count):
            along, across = filtered[0][t], filtered[1][t]
            contrast = filtered[2][t] - ring_a[3, t, here, :]
            on_wall = force[0, t, here, :] > 0.5
            speed = jnp.sqrt(along * along + across * across + SPEED_FLOOR * SPEED_FLOOR)
            scaled = jnp.sqrt(HEIGHT_RATIO * speed)
            uplus = jnp.log(1.0 + KAPPA * scaled) * (1.0 / KAPPA) + 7.8 * (
                1.0
                - jnp.exp(scaled * (-1.0 / 11.0))
                - scaled * (1.0 / 11.0) * jnp.exp(scaled * (-1.0 / 3.0))
            )
            factor = jnp.where(on_wall, speed / (uplus * uplus), LAMINAR_SHEAR)
            heat = jnp.where(
                on_wall, speed / (PRANDTL_TURB * uplus + PRANDTL_JUMP), LAMINAR_HEAT
            )
            force[0, t, here, :] = step * (factor * along)
            force[1, t, here, :] = step * (factor * across)
            force[2, t, here, :] = step * (heat * contrast)
            force[3, t, here, :] = step * force[3, t, here, :]
        return carry

    lax.fori_loop(0, 17, forcing_rows, 0)

    half = 0.5 * step

    def advance(source, row):
        here = pl.ds(row, STRIP)
        centre, total, wests, easts, norths, souths = [], [], [], [], [], []
        for field in range(4):
            middle = [source[field, t, here, :] for t in range(count)]
            north = [source[field, t, pl.ds(row - 1, STRIP), :] for t in range(count)]
            south = [source[field, t, pl.ds(row + 1, STRIP), :] for t in range(count)]
            west, east = shifted_lanes(middle)
            centre.append(middle)
            wests.append(west)
            easts.append(east)
            norths.append(north)
            souths.append(south)
        news = []
        for t in range(count):
            spread = [
                (1.0 - 4.0 * FILM_SPREAD) * centre[f][t]
                + FILM_SPREAD
                * ((norths[f][t] + souths[f][t]) + (wests[f][t] + easts[f][t]))
                for f in range(4)
            ]
            height = centre[0][t]
            inverse = lax.rsqrt(height * height + FILM_FLOOR * FILM_FLOOR)
            drag = (FRICTION * step) * inverse
            slope = half * height
            height_new = (
                spread[0]
                + force[3, t, here, :]
                - half * ((easts[1][t] - wests[1][t]) + (souths[2][t] - norths[2][t]))
            )
            along_new = (
                spread[1]
                + force[0, t, here, :]
                - drag * centre[1][t]
                - slope * (easts[0][t] - wests[0][t])
            )
            across_new = (
                spread[2]
                + force[1, t, here, :]
                - drag * centre[2][t]
                - slope * (souths[0][t] - norths[0][t])
            )
            heat_new = spread[3] + force[2, t, here, :] * inverse
            news.append((height_new, along_new, across_new, heat_new))
        return news

    def middle_rows(source, target):
        def body(index, carry):
            row = 4 + 8 * index
            news = advance(source, row)
            for t in range(count):
                for field in range(4):
                    target[field, t, pl.ds(row, STRIP), :] = news[t][field]
            return carry

        lax.fori_loop(0, 17, body, 0)

    middle_rows(ring_a, ring_b)
    middle_rows(ring_b, ring_a)
    middle_rows(ring_a, ring_b)

    def last_rows(index, best):
        row = pl.multiple_of(8 + 8 * index, 8)
        news = advance(ring_b, row)
        place = pl.multiple_of(owner_map[wall, index] * STRIP, STRIP)
        for t in range(TILES):
            for field in range(4):
                out[field, pl.ds(place, STRIP), t * LANES : (t + 1) * LANES] = news[t][
                    field
                ]
            best = jnp.maximum(best, film_speed(*news[t][:3]))
        return best

    best = lax.fori_loop(0, 16, last_rows, jnp.zeros((STRIP, LANES), jnp.float32))
    peak[...] = jnp.broadcast_to(step * jnp.max(best, keepdims=True), (ROWS, LANES))


def vmem(count):
    return [pl.BlockSpec(memory_space=pltpu.VMEM)] * count


def shape(*dims):
    return jax.ShapeDtypeStruct(dims, jnp.float32)


def per_device(gas_state, wall_flags, film_state, deposit, owner_map):
    params = pltpu.CompilerParams(vmem_limit_bytes=VMEM_LIMIT)
    sampled, to_north, to_south, core_main, chip_main, peak = pl.pallas_call(
        edges_kernel,
        out_shape=(
            shape(3, ROWS, COLS),
            shape(4 * FIELDS, COLS),
            shape(4 * FIELDS, COLS),
            shape(ROWS + 8, LANES),
            shape(ROWS + 8, LANES),
            shape(ROWS, LANES),
        ),
        in_specs=vmem(4),
        out_specs=tuple(vmem(6)),
        compiler_params=params,
        name="edges",
    )(gas_state, wall_flags, film_state, deposit)

    walls, gases = lax.axis_size("wall"), lax.axis_size("gas")
    both = ("wall", "gas")
    peaks = lax.all_to_all(peak, both, split_axis=0, concat_axis=0, tiled=True)
    down = [(i, (i + 1) % walls) for i in range(walls)]
    up = [(j, i) for i, j in down]
    from_north = lax.ppermute(to_south, "wall", down)
    from_south = lax.ppermute(to_north, "wall", up)
    core_pack, chip_pack = pl.pallas_call(
        corners_kernel,
        out_shape=(shape(ROWS + 8, LANES), shape(ROWS + 8, LANES)),
        in_specs=vmem(4),
        out_specs=tuple(vmem(2)),
        compiler_params=params,
        name="corners",
    )(from_north, from_south, core_main, chip_main)
    partner = [(i, i ^ 1) for i in range(gases)]
    outer = [(i, (i + 1) % gases if i % 2 else (i - 1) % gases) for i in range(gases)]
    core_pack = lax.ppermute(core_pack, "gas", partner)
    chip_pack = lax.ppermute(chip_pack, "gas", outer)

    ring = (4, TILES + 1, RING, LANES)
    film, local = pl.pallas_call(
        film_kernel,
        out_shape=(shape(4, ROWS, COLS), shape(ROWS, LANES)),
        in_specs=[pl.BlockSpec(memory_space=pltpu.SMEM)] + vmem(9),
        out_specs=tuple(vmem(2)),
        scratch_shapes=[
            pltpu.VMEM(ring, jnp.float32),
            pltpu.VMEM(ring, jnp.float32),
            pltpu.VMEM((3,) + ring[1:], jnp.float32),
            pltpu.VMEM(ring, jnp.float32),
        ],
        compiler_params=params,
        name="film",
    )(
        owner_map,
        film_state,
        sampled,
        wall_flags,
        deposit,
        from_north,
        from_south,
        core_pack,
        chip_pack,
        peaks,
    )
    film_out = lax.all_to_all(film, "gas", split_axis=1, concat_axis=2, tiled=True)
    cfl = jnp.max(lax.all_to_all(local, both, split_axis=0, concat_axis=0, tiled=True))
    return film_out, cfl


def solution(mesh):
    return jax.shard_map(
        per_device,
        mesh=mesh,
        in_specs=(
            P(None, None, "wall", "gas"),
            P("wall", "gas"),
            P(None, "wall", "gas"),
            P("wall", "gas"),
            P(),
        ),
        out_specs=(P(None, ("wall", "gas"), None), P()),
        check_vma=False,
    )
```

time: 271 us -> 85.3 us (0.31)
  blocking collectives: 181 us -> 17.3 us
  other arithmetic: 27.1 us -> 0.73 us
  local copies, waits for them, and re-layouts: 29.4 us -> 7.8 us
  waiting for transfers between devices: 8.35 us -> 26.1 us
  Pallas kernels: 0 us -> 13.6 us
    pmax x2 -> x0, blocking collectives: 181 us -> none  [the longest x1 118 us: per_device(): time_step = COURANT / lax.pmax(peak_speed(film_state), ('wall', 'gas'))]
    all_to_all x1 -> x2, waiting for transfers between devices: 0.01 us -> 24 us  [the longest x1 16.2 us: per_device(): lax.all_to_all(film, 'gas', split_axis=1, concat_axis=2, tiled=True)]
    all_to_all x0 -> x1, blocking collectives: none -> 17.3 us  [per_device(): peaks = lax.all_to_all(peak, both, split_axis=0, concat_axis=0, tiled=True)]
    slice x8 -> x0, local copies, waits for them, and re-layouts: 17.3 us -> none  [the longest x3 10.3 us: per_device(): film_now = arrived[:4]]
    pallas_call x0 -> x3, Pallas kernels: none -> 13.6 us  [the longest x1 12.5 us: per_device(): pl.pallas_call(film_kernel, out_shape=(shape(4, ROWS, COLS), shape(ROWS,...]
    add x11 -> x0, other arithmetic: 8.96 us -> none  [the longest x3 3.2 us: advance(): centre[1] + FILM_SPREAD * spread[1]]
    concatenate x5 -> x0, other arithmetic: 7.61 us -> none  [the longest x3 4.36 us: per_device(): jnp.concatenate([film_now[:, :, -1:], film_now, film_now[:, :, :1]], axis=2)]
    ppermute x6 -> x4, waiting for transfers between devices: 8.35 us -> 2.07 us  [the longest x1 2.07 us: per_device(): from_north = lax.ppermute(to_south, 'wall', down)]
  transfers between devices with their start and end apart: 7 -> 6, of which waited for: 4 -> 3; matrix products, arithmetic and copies ran while one was open for 1% -> 3% of each run, Pallas kernels for 0% -> 0%
where the time goes in v1:
time: 85.3 us; the launch traced here: 84.9 us
  waiting for transfers between devices  26.1 us (31%)
  starting transfers between devices  18.7 us (22%)
  blocking collectives  17.3 us (20%)
  Pallas kernels  13.6 us (16%)
  local copies, waits for them, and re-layouts  7.8 us (9%)
    all_to_all x1, blocking collectives, per_device(): peaks = lax.all_to_all(peak, both, split_axis=0, concat_axis=0, tiled=True)  17.3 us
    all_to_all x1, waiting for transfers between devices, per_device(): lax.all_to_all(film, 'gas', split_axis=1, concat_axis=2, tiled=True)  16.2 us
    pallas_call x1, Pallas kernels, per_device(): pl.pallas_call(film_kernel, out_shape=(shape(4, ROWS, COLS), shape(ROWS,...  12.5 us
    all_to_all x1, waiting for transfers between devices, per_device(): lax.all_to_all(local, both, split_axis=0, concat_axis=0, tiled=True)  7.83 us
    unnamed x11, local copies, waits for them, and re-layouts  4.86 us
    all_to_all x1, starting transfers between devices, per_device(): lax.all_to_all(local, both, split_axis=0, concat_axis=0, tiled=True)  4.55 us
    all_to_all x1, starting transfers between devices, per_device(): lax.all_to_all(film, 'gas', split_axis=1, concat_axis=2, tiled=True)  4.4 us
    ppermute x1, starting transfers between devices, per_device(): chip_pack = lax.ppermute(chip_pack, 'gas', outer)  3.31 us
  transfers between devices with their start and end apart: 6, of which 3 were waited for; matrix products, arithmetic and copies ran while one was open for 3% of the time, Pallas kernels for 0%

profile of v1, /device:TPU:1, one launch (start us, length us, event | category | flops | bytes accessed | tf_op | source)
XLA Modules:
  0.0 84.9 jit_solution(13113482716160559998)
XLA Ops:
  0.6 0.0 copy-start.4
  0.6 0.8 copy.9.flags
  1.4 0.0 copy-start
  1.4 1.2 %copy-done = f32[4,128,512]{2,1,0:T(8,128)S(1)} copy-done((f32[4,128,512]{2,1,0:T(8,128)S(1)}, f32[4,128,512]{2,1,0:T(8,128)}, u32[]{:S(2)}) %copy-start) | copy-done | bytes 1048600
  2.7 0.0 copy-start.2
  2.7 1.9 %copy-done.2 = f32[3,4,128,512]{3,2,1,0:T(8,128)S(1)} copy-done((f32[3,4,128,512]{3,2,1,0:T(8,128)S(1)}, f32[3,4,128,512]{3,2,1,0:T(8,128)}, u32[]{:S(2)}) %copy-start.2) | copy-done | bytes 3145752
  4.5 0.0 copy-start.3
  4.6 0.9 %copy-done.3 = f32[128,512]{1,0:T(8,128)S(1)} copy-done((f32[128,512]{1,0:T(8,128)S(1)}, f32[128,512]{1,0:T(8,128)}, u32[]{:S(2)}) %copy-start.3) | copy-done | bytes 262168
  5.5 0.0 copy-start.1
  5.5 1.0 %edges.1 = (f32[3,128,512]{2,1,0:T(8,128)S(1)}, f32[36,512]{1,0:T(8,128)S(1)}, f32[36,512]{1,0:T(8,128)S(1)}, f32[136,128]{1,0:T(8,128)S(1)}, f32[136,128]{1,0:T(8,128)S(1)}, /*index=5*/f32[128,128]{1,0:T(8,128)S(1)}) custom-call(f32[3,4,128,512]{3,2,1,0:T(8,128)S(1)} %copy-done.2, s32[128,4]{1,0:T(8,128)S(1)} %copy.9.flags, f32[4,128,512]{2,1,0:T(8,128)S(1)} %copy-done, ...), custom_call_target="tpu_custom_call" | custom-call | tf_op jit(solution)/shard_map/edges/pallas_call | solution.py:313
  6.5 2.2 %collective-permute-start = (f32[36,512]{1,0:T(8,128)S(1)}, f32[36,512]{1,0:T(8,128)S(1)}, u32[]{:S(2)}, u32[]{:S(2)}) collective-permute-start(f32[36,512]{1,0:T(8,128)S(1)} %get-tuple-element.13), channel_id=1, source_target_pairs={{0,16},{16,32},{32,48},{48,64},{64,80},{80,96},{96,112},{112,0},{1... | collective-permute-start | bytes 221192 | tf_op jit(solution)/shard_map/ppermute | solution.py:334
  8.6 2.9 %collective-permute-start.1 = (f32[36,512]{1,0:T(8,128)S(1)}, f32[36,512]{1,0:T(8,128)S(1)}, u32[]{:S(2)}, u32[]{:S(2)}) collective-permute-start(f32[36,512]{1,0:T(8,128)S(1)} %get-tuple-element.14), channel_id=1, source_target_pairs={{16,0},{32,16},{48,32},{64,48},{80,64},{96,80},{112,96},{0,112},{1... | collective-permute-start | bytes 221192 | tf_op jit(solution)/shard_map/ppermute | solution.py:335
  11.5 2.1 %collective-permute-done.from_north = f32[36,512]{1,0:T(8,128)S(1)} collective-permute-done((f32[36,512]{1,0:T(8,128)S(1)}, f32[36,512]{1,0:T(8,128)S(1)}, u32[]{:S(2)}, u32[]{:S(2)}) %collective-permute-start) | collective-permute-done | bytes 73760 | tf_op jit(solution)/shard_map/ppermute | solution.py:334
  13.6 0.0 collective-permute-done.1.from_south
  13.6 0.1 corners.1
  13.7 1.3 %collective-permute-start.2 = (f32[136,128]{1,0:T(8,128)S(1)}, f32[136,128]{1,0:T(8,128)S(1)}, u32[]{:S(2)}, u32[]{:S(2)}) collective-permute-start(f32[136,128]{1,0:T(8,128)S(1)} %get-tuple-element.17), channel_id=1, source_target_pairs={{0,1},{1,0},{2,3},{3,2},{4,5},{5,4},{6,7},{7,6},{8,9},{9,8},{10,11... | collective-permute-start | bytes 208904 | tf_op jit(solution)/shard_map/ppermute | solution.py:346
  15.0 3.3 %collective-permute-start.3 = (f32[136,128]{1,0:T(8,128)S(1)}, f32[136,128]{1,0:T(8,128)S(1)}, u32[]{:S(2)}, u32[]{:S(2)}) collective-permute-start(f32[136,128]{1,0:T(8,128)S(1)} %get-tuple-element.18), channel_id=1, source_target_pairs={{0,15},{1,2},{2,1},{3,4},{4,3},{5,6},{6,5},{7,8},{8,7},{9,10},{10,... | collective-permute-start | bytes 208904 | tf_op jit(solution)/shard_map/ppermute | solution.py:347
  18.3 17.3 %all_to_all.38 = f32[128,1,128]{2,1,0:T(1,128)S(1)} all-to-all(f32[128,1,128]{2,1,0:T(1,128)S(1)} %bitcast.12), channel_id=1, replica_groups=mesh['wall'=8,'gas'=16] {'wall','gas'}, dimensions={0} | all-to-all | bytes 131072 | tf_op jit(solution)/shard_map/all_to_all | solution.py:331
  35.7 0.0 collective-permute-done.2.core_pack
  35.7 0.0 collective-permute-done.3.chip_pack
  35.7 0.0 copy-done.4
  35.7 0.0 copy-done.1
  35.7 12.5 %film.4 = (f32[4,128,512]{2,1,0:T(8,128)S(1)}, f32[128,128]{1,0:T(8,128)}) custom-call(s32[8,16]{1,0:T(8,128)S(1)} %copy-done.4, f32[4,128,512]{2,1,0:T(8,128)S(1)} %copy-done.1, f32[3,128,512]{2,1,0:T(8,128)S(1)} %get-tuple-element.12.sampled, s32[128,4]{1,0:T(8,128)S(1)} %copy.9.flags, f32[128,512]{1,0:T(8,128)S(1)} %copy-done.3, ...), custom_call_target="tpu_custom_call" | custom-call | tf_op jit(solution)/shard_map/film/pallas_call | solution.py:350
  48.2 4.5 %all-to-all-start.2 = ((f32[128,1,128]{2,1,0:T(1,128)}), f32[128,1,128]{2,1,0:T(1,128)S(1)}, u32[]{:S(2)}, u32[]{:S(2)}) async-start(f32[128,1,128]{2,1,0:T(1,128)} %bitcast.7), calls=%async_computation.2 | async-start | bytes 131072 | tf_op jit(solution)/shard_map/all_to_all | solution.py:376
  52.8 1.6 %copy.12 = f32[4,128,512]{2,0,1:T(4,128)} copy(f32[4,128,512]{2,1,0:T(8,128)S(1)} %get-tuple-element.20) | data formatting | bytes 2097152 | tf_op jit(solution)/shard_map/film/pallas_call | solution.py:350
  54.4 7.8 %all-to-all-done.2 = f32[128,1,128]{2,1,0:T(1,128)S(1)} async-done(((f32[128,1,128]{2,1,0:T(1,128)}), f32[128,1,128]{2,1,0:T(1,128)S(1)}, u32[]{:S(2)}, u32[]{:S(2)}) %all-to-all-start.2) | async-done | bytes 65568 | tf_op jit(solution)/shard_map/all_to_all | solution.py:376
  62.3 4.4 %all-to-all-start.1 = ((f32[4,128,512]{2,0,1:T(4,128)}), f32[4,128,512]{2,0,1:T(4,128)S(1)}, u32[]{:S(2)}, u32[]{:S(2)}) async-start(f32[4,128,512]{2,0,1:T(4,128)} %copy.12), calls=%async_computation.1 | async-start | bytes 2097152 | tf_op jit(solution)/shard_map/all_to_all | solution.py:375
  66.7 0.7 reduce_max.9
  67.4 16.2 %all-to-all-done.1 = f32[4,128,512]{2,0,1:T(4,128)S(1)} async-done(((f32[4,128,512]{2,0,1:T(4,128)}), f32[4,128,512]{2,0,1:T(4,128)S(1)}, u32[]{:S(2)}, u32[]{:S(2)}) %all-to-all-start.1) | async-done | bytes 1048608 | tf_op jit(solution)/shard_map/all_to_all | solution.py:375
  83.6 1.3 %copy.13 = f32[4,8,16,512]{3,1,2,0:T(8,128)} copy(f32[4,8,16,512]{3,0,1,2:T(4,128)S(1)} %bitcast.13) | data formatting | bytes 2097152 | tf_op jit(solution)/shard_map/all_to_all | solution.py:375
Async XLA Ops:
  0.6 35.0 %copy-start.4 = (s32[8,16]{1,0:T(8,128)S(1)}, s32[8,16]{1,0:T(8,128)}, u32[]{:S(2)}) copy-start(s32[8,16]{1,0:T(8,128)} %owner_map.1) | copy-start | bytes 1540
  1.4 1.2 %copy-start = (f32[4,128,512]{2,1,0:T(8,128)S(1)}, f32[4,128,512]{2,1,0:T(8,128)}, u32[]{:S(2)}) copy-start(f32[4,128,512]{2,1,0:T(8,128)} %film.5) | copy-start | bytes 3145732
  2.7 1.9 %copy-start.2 = (f32[3,4,128,512]{3,2,1,0:T(8,128)S(1)}, f32[3,4,128,512]{3,2,1,0:T(8,128)}, u32[]{:S(2)}) copy-start(f32[3,4,128,512]{3,2,1,0:T(8,128)} %gas.1) | copy-start | bytes 9437188
  4.5 0.9 %copy-start.3 = (f32[128,512]{1,0:T(8,128)S(1)}, f32[128,512]{1,0:T(8,128)}, u32[]{:S(2)}) copy-start(f32[128,512]{1,0:T(8,128)} %deposit.3) | copy-start | bytes 786436
  5.5 30.2 %copy-start.1 = (f32[4,128,512]{2,1,0:T(8,128)S(1)}, f32[4,128,512]{2,1,0:T(8,128)}, u32[]{:S(2)}) copy-start(f32[4,128,512]{2,1,0:T(8,128)} %film.5) | copy-start | bytes 3145732
  6.5 7.1 %collective-permute-start = (f32[36,512]{1,0:T(8,128)S(1)}, f32[36,512]{1,0:T(8,128)S(1)}, u32[]{:S(2)}, u32[]{:S(2)}) collective-permute-start(f32[36,512]{1,0:T(8,128)S(1)} %get-tuple-element.13), channel_id=1, source_target_pairs={{0,16},{16,32},{32,48},{48,64},{64,80},{80,96},{96,112},{112,0},{1... | collective-permute-start | bytes 221192 | tf_op jit(solution)/shard_map/ppermute | solution.py:334
  8.6 4.9 %collective-permute-start.1 = (f32[36,512]{1,0:T(8,128)S(1)}, f32[36,512]{1,0:T(8,128)S(1)}, u32[]{:S(2)}, u32[]{:S(2)}) collective-permute-start(f32[36,512]{1,0:T(8,128)S(1)} %get-tuple-element.14), channel_id=1, source_target_pairs={{16,0},{32,16},{48,32},{64,48},{80,64},{96,80},{112,96},{0,112},{1... | collective-permute-start | bytes 221192 | tf_op jit(solution)/shard_map/ppermute | solution.py:335
  13.7 22.0 %collective-permute-start.2 = (f32[136,128]{1,0:T(8,128)S(1)}, f32[136,128]{1,0:T(8,128)S(1)}, u32[]{:S(2)}, u32[]{:S(2)}) collective-permute-start(f32[136,128]{1,0:T(8,128)S(1)} %get-tuple-element.17), channel_id=1, source_target_pairs={{0,1},{1,0},{2,3},{3,2},{4,5},{5,4},{6,7},{7,6},{8,9},{9,8},{10,11... | collective-permute-start | bytes 208904 | tf_op jit(solution)/shard_map/ppermute | solution.py:346
  15.0 20.6 %collective-permute-start.3 = (f32[136,128]{1,0:T(8,128)S(1)}, f32[136,128]{1,0:T(8,128)S(1)}, u32[]{:S(2)}, u32[]{:S(2)}) collective-permute-start(f32[136,128]{1,0:T(8,128)S(1)} %get-tuple-element.18), channel_id=1, source_target_pairs={{0,15},{1,2},{2,1},{3,4},{4,3},{5,6},{6,5},{7,8},{8,7},{9,10},{10,... | collective-permute-start | bytes 208904 | tf_op jit(solution)/shard_map/ppermute | solution.py:347
  48.2 14.0 %all-to-all-start.2 = ((f32[128,1,128]{2,1,0:T(1,128)}), f32[128,1,128]{2,1,0:T(1,128)S(1)}, u32[]{:S(2)}, u32[]{:S(2)}) async-start(f32[128,1,128]{2,1,0:T(1,128)} %bitcast.7), calls=%async_computation.2 | async-start | bytes 131072 | tf_op jit(solution)/shard_map/all_to_all | solution.py:376
  62.3 21.4 %all-to-all-start.1 = ((f32[4,128,512]{2,0,1:T(4,128)}), f32[4,128,512]{2,0,1:T(4,128)S(1)}, u32[]{:S(2)}, u32[]{:S(2)}) async-start(f32[4,128,512]{2,0,1:T(4,128)} %copy.12), calls=%async_computation.1 | async-start | bytes 2097152 | tf_op jit(solution)/shard_map/all_to_all | solution.py:375

commit v2 on v1

--- a/solution.py
+++ b/solution.py
@@ -1,5 +1,3 @@
-import functools
-
 import jax
 import jax.numpy as jnp
 from jax import lax
@@ -7,7 +5,7 @@
 from jax.experimental.pallas import tpu as pltpu
 from jax.sharding import PartitionSpec as P
 
-SUBSTEPS = 4
+
 LAYER_WEIGHTS = (0.1, 0.2, 0.3, 0.4)
 KAPPA = 0.41
 HEIGHT_RATIO = 20.0
@@ -25,10 +23,9 @@
 COLS = 512
 LANES = 128
 TILES = COLS // LANES
-HALO = SUBSTEPS
 FIELDS = 9
 STRIP = 8
-RING = ROWS + 16
+RING = ROWS + 24
 VMEM_LIMIT = 48 * 1024 * 1024
 
 
@@ -139,7 +136,6 @@
     chip_pack,
     peaks,
     out,
-    peak,
     ring_a,
     ring_b,
     gas_ring,
@@ -219,13 +215,13 @@
             force[3, t, here, :] = step * force[3, t, here, :]
         return carry
 
-    lax.fori_loop(0, 17, forcing_rows, 0)
+    grouped(3, 18, forcing_rows, 0)
 
     half = 0.5 * step
 
     def advance(source, row):
         here = pl.ds(row, STRIP)
-        centre, total, wests, easts, norths, souths = [], [], [], [], [], []
+        centre, wests, easts, norths, souths = [], [], [], [], []
         for field in range(4):
             middle = [source[field, t, here, :] for t in range(count)]
             north = [source[field, t, pl.ds(row - 1, STRIP), :] for t in range(count)]
@@ -278,7 +274,7 @@
                     target[field, t, pl.ds(row, STRIP), :] = news[t][field]
             return carry
 
-        lax.fori_loop(0, 17, body, 0)
+        grouped(6, 18, body, 0)
 
     middle_rows(ring_a, ring_b)
     middle_rows(ring_b, ring_a)
@@ -287,17 +283,45 @@
     def last_rows(index, best):
         row = pl.multiple_of(8 + 8 * index, 8)
         news = advance(ring_b, row)
-        place = pl.multiple_of(owner_map[wall, index] * STRIP, STRIP)
+        place = owner_map[wall, index]
         for t in range(TILES):
             for field in range(4):
-                out[field, pl.ds(place, STRIP), t * LANES : (t + 1) * LANES] = news[t][
-                    field
-                ]
+                out[place, field * TILES + t] = news[t][field]
             best = jnp.maximum(best, film_speed(*news[t][:3]))
         return best
 
-    best = lax.fori_loop(0, 16, last_rows, jnp.zeros((STRIP, LANES), jnp.float32))
-    peak[...] = jnp.broadcast_to(step * jnp.max(best, keepdims=True), (ROWS, LANES))
+    best = grouped(4, 16, last_rows, jnp.zeros((STRIP, LANES), jnp.float32))
+    top = jnp.broadcast_to(step * jnp.max(best, keepdims=True), (STRIP, LANES))
+    for owner in range(ROWS // STRIP):
+        out[owner, 4 * TILES] = top
+
+
+def band_peak_kernel(pieces, peak):
+    best = pieces[0, 0]
+    for source in range(1, pieces.shape[0]):
+        best = jnp.maximum(best, pieces[source, 0])
+    peak[...] = best
+
+
+def strips_kernel(pieces, out):
+    for source in range(pieces.shape[0]):
+        for t in range(TILES):
+            start = source * COLS + t * LANES
+            out[0, :, start : start + LANES] = pieces[source, t]
+
+
+def grouped(unroll, total, body, carry):
+    whole = total // unroll
+
+    def many(index, carry):
+        for k in range(unroll):
+            carry = body(index * unroll + k, carry)
+        return carry
+
+    carry = lax.fori_loop(0, whole, many, carry)
+    for index in range(whole * unroll, total):
+        carry = body(index, carry)
+    return carry
 
 
 def vmem(count):
@@ -308,7 +332,7 @@
     return jax.ShapeDtypeStruct(dims, jnp.float32)
 
 
-def per_device(gas_state, wall_flags, film_state, deposit, owner_map):
+def coupling_step(gas_state, wall_flags, film_state, deposit, owner_map):
     params = pltpu.CompilerParams(vmem_limit_bytes=VMEM_LIMIT)
     sampled, to_north, to_south, core_main, chip_main, peak = pl.pallas_call(
         edges_kernel,
@@ -347,11 +371,11 @@
     chip_pack = lax.ppermute(chip_pack, "gas", outer)
 
     ring = (4, TILES + 1, RING, LANES)
-    film, local = pl.pallas_call(
+    pieces = pl.pallas_call(
         film_kernel,
-        out_shape=(shape(4, ROWS, COLS), shape(ROWS, LANES)),
+        out_shape=shape(gases, 4 * TILES + 1, STRIP, LANES),
         in_specs=[pl.BlockSpec(memory_space=pltpu.SMEM)] + vmem(9),
-        out_specs=tuple(vmem(2)),
+        out_specs=vmem(1)[0],
         scratch_shapes=[
             pltpu.VMEM(ring, jnp.float32),
             pltpu.VMEM(ring, jnp.float32),
@@ -372,14 +396,37 @@
         chip_pack,
         peaks,
     )
-    film_out = lax.all_to_all(film, "gas", split_axis=1, concat_axis=2, tiled=True)
-    cfl = jnp.max(lax.all_to_all(local, both, split_axis=0, concat_axis=0, tiled=True))
+    pieces = lax.all_to_all(pieces, "gas", split_axis=0, concat_axis=0, tiled=True)
+    band_peak = pl.pallas_call(
+        band_peak_kernel,
+        out_shape=shape(STRIP, LANES),
+        grid=(1,),
+        in_specs=[
+            pl.BlockSpec((gases, 1, STRIP, LANES), lambda i: (0, 4 * TILES, 0, 0))
+        ],
+        out_specs=pl.BlockSpec((STRIP, LANES), lambda i: (0, 0)),
+        name="band_peak",
+    )(pieces)
+    cfl = jnp.max(
+        lax.all_to_all(band_peak, "wall", split_axis=0, concat_axis=0, tiled=True)
+    )
+    film_out = pl.pallas_call(
+        strips_kernel,
+        out_shape=shape(4, STRIP, gases * COLS),
+        grid=(4,),
+        in_specs=[pl.BlockSpec((gases, TILES, STRIP, LANES), lambda i: (0, i, 0, 0))],
+        out_specs=pl.BlockSpec((1, STRIP, gases * COLS), lambda i: (i, 0, 0)),
+        cost_estimate=pl.CostEstimate(
+            flops=0, bytes_accessed=2 << 20, transcendentals=0
+        ),
+        name="strips",
+    )(pieces)
     return film_out, cfl
 
 
 def solution(mesh):
     return jax.shard_map(
-        per_device,
+        coupling_step,
         mesh=mesh,
         in_specs=(
             P(None, None, "wall", "gas"),

time: 85.3 us -> 76.5 us (0.90)
  blocking collectives: 17.3 us -> 40 us
  waiting for transfers between devices: 26.1 us -> 3.65 us
  starting transfers between devices: 18.7 us -> 13 us
  local copies, waits for them, and re-layouts: 7.8 us -> 4.85 us
    all_to_all x1 -> x2, blocking collectives: 17.3 us -> 40 us  [the longest x1 22.7 us: coupling_step(): lax.all_to_all(pieces, 'gas', split_axis=0, concat_axis=0, tiled=True)]
    all_to_all x2 -> x1, waiting for transfers between devices: 24 us -> 1.58 us  [coupling_step(): lax.all_to_all(band_peak, 'wall', split_axis=0, concat_axis=0, tiled=True)]
    all_to_all x2 -> x1, starting transfers between devices: 8.95 us -> 3.33 us  [coupling_step(): lax.all_to_all(band_peak, 'wall', split_axis=0, concat_axis=0, tiled=True)]
    pallas_call x1 -> x0, local copies, waits for them, and re-layouts: 1.65 us -> none  [per_device(): pl.pallas_call(film_kernel, out_shape=(shape(4, ROWS, COLS), shape(ROWS,...]
    all_to_all x1 -> x0, local copies, waits for them, and re-layouts: 1.29 us -> none  [per_device(): lax.all_to_all(film, 'gas', split_axis=1, concat_axis=2, tiled=True)]
    pallas_call x3 -> x5, Pallas kernels: 13.6 us -> 13.1 us  [the longest x1 7.17 us: coupling_step(): pl.pallas_call(film_kernel, out_shape=shape(gases, 4 * TILES + 1, STRIP,...]
  transfers between devices with their start and end apart: 6 -> 5, of which waited for: 3 -> 2; matrix products, arithmetic and copies ran while one was open for 3% -> 0% of each run, Pallas kernels for 0% -> 4%
where the time goes in v2:
time: 76.5 us; the launch traced here: 75.9 us
  blocking collectives  40 us (52%)
  Pallas kernels  13.1 us (17%)
  starting transfers between devices  13 us (17%)
  local copies, waits for them, and re-layouts  4.85 us (6%)
  waiting for transfers between devices  3.65 us (5%)
    all_to_all x1, blocking collectives, coupling_step(): lax.all_to_all(pieces, 'gas', split_axis=0, concat_axis=0, tiled=True)  22.7 us
    all_to_all x1, blocking collectives, coupling_step(): peaks = lax.all_to_all(peak, both, split_axis=0, concat_axis=0, tiled=True)  17.3 us
    pallas_call x1, Pallas kernels, coupling_step(): pl.pallas_call(film_kernel, out_shape=shape(gases, 4 * TILES + 1, STRIP,...  7.17 us
    unnamed x11, local copies, waits for them, and re-layouts  4.85 us
    pallas_call x1, Pallas kernels, coupling_step(): pl.pallas_call(strips_kernel, out_shape=shape(4, STRIP, gases * COLS), gr...  3.38 us
    all_to_all x1, starting transfers between devices, coupling_step(): lax.all_to_all(band_peak, 'wall', split_axis=0, concat_axis=0, tiled=True)  3.33 us
    ppermute x1, starting transfers between devices, coupling_step(): chip_pack = lax.ppermute(chip_pack, 'gas', outer)  3.31 us
    ppermute x1, starting transfers between devices, coupling_step(): from_south = lax.ppermute(to_north, 'wall', up)  2.87 us
  transfers between devices with their start and end apart: 5, of which 2 were waited for; matrix products, arithmetic and copies ran while one was open for 0% of the time, Pallas kernels for 4%

profile of v2, /device:TPU:1, one launch (start us, length us, event | category | flops | bytes accessed | tf_op | source)
XLA Modules:
  0.0 75.9 jit_solution(16974524151892524201)
XLA Ops:
  0.6 0.8 %copy.9.flags = s32[128,4]{1,0:T(8,128)S(1)} copy(s32[128,4]{0,1:T(4,128)} %param.6) | data formatting | bytes 4096 | tf_op args[1]
  1.4 0.0 copy-start
  1.4 1.2 %copy-done = f32[4,128,512]{2,1,0:T(8,128)S(1)} copy-done((f32[4,128,512]{2,1,0:T(8,128)S(1)}, f32[4,128,512]{2,1,0:T(8,128)}, u32[]{:S(2)}) %copy-start) | copy-done | bytes 1048600
  2.6 0.0 copy-start.2
  2.6 1.9 %copy-done.2 = f32[3,4,128,512]{3,2,1,0:T(8,128)S(1)} copy-done((f32[3,4,128,512]{3,2,1,0:T(8,128)S(1)}, f32[3,4,128,512]{3,2,1,0:T(8,128)}, u32[]{:S(2)}) %copy-start.2) | copy-done | bytes 3145752
  4.5 0.0 copy-start.3
  4.5 0.9 %copy-done.3 = f32[128,512]{1,0:T(8,128)S(1)} copy-done((f32[128,512]{1,0:T(8,128)S(1)}, f32[128,512]{1,0:T(8,128)}, u32[]{:S(2)}) %copy-start.3) | copy-done | bytes 262168
  5.5 0.0 copy-start.1
  5.5 0.0 copy-start.4
  5.5 1.0 %edges.1 = (f32[3,128,512]{2,1,0:T(8,128)S(1)}, f32[36,512]{1,0:T(8,128)S(1)}, f32[36,512]{1,0:T(8,128)S(1)}, f32[136,128]{1,0:T(8,128)S(1)}, f32[136,128]{1,0:T(8,128)S(1)}, /*index=5*/f32[128,128]{1,0:T(8,128)S(1)}) custom-call(f32[3,4,128,512]{3,2,1,0:T(8,128)S(1)} %copy-done.2, s32[128,4]{1,0:T(8,128)S(1)} %copy.9.flags, f32[4,128,512]{2,1,0:T(8,128)S(1)} %copy-done, ...), custom_call_target="tpu_custom_call" | custom-call | tf_op jit(solution)/shard_map/edges/pallas_call | solution.py:337
  6.5 2.2 %collective-permute-start = (f32[36,512]{1,0:T(8,128)S(1)}, f32[36,512]{1,0:T(8,128)S(1)}, u32[]{:S(2)}, u32[]{:S(2)}) collective-permute-start(f32[36,512]{1,0:T(8,128)S(1)} %get-tuple-element.11), channel_id=1, source_target_pairs={{0,16},{16,32},{32,48},{48,64},{64,80},{80,96},{96,112},{112,0},{1... | collective-permute-start | bytes 221192 | tf_op jit(solution)/shard_map/ppermute | solution.py:358
  8.6 2.9 %collective-permute-start.1 = (f32[36,512]{1,0:T(8,128)S(1)}, f32[36,512]{1,0:T(8,128)S(1)}, u32[]{:S(2)}, u32[]{:S(2)}) collective-permute-start(f32[36,512]{1,0:T(8,128)S(1)} %get-tuple-element.12), channel_id=1, source_target_pairs={{16,0},{32,16},{48,32},{64,48},{80,64},{96,80},{112,96},{0,112},{1... | collective-permute-start | bytes 221192 | tf_op jit(solution)/shard_map/ppermute | solution.py:359
  11.5 2.1 %collective-permute-done.from_north = f32[36,512]{1,0:T(8,128)S(1)} collective-permute-done((f32[36,512]{1,0:T(8,128)S(1)}, f32[36,512]{1,0:T(8,128)S(1)}, u32[]{:S(2)}, u32[]{:S(2)}) %collective-permute-start) | collective-permute-done | bytes 73760 | tf_op jit(solution)/shard_map/ppermute | solution.py:358
  13.6 0.0 collective-permute-done.1.from_south
  13.6 0.1 corners.1
  13.7 1.3 %collective-permute-start.2 = (f32[136,128]{1,0:T(8,128)S(1)}, f32[136,128]{1,0:T(8,128)S(1)}, u32[]{:S(2)}, u32[]{:S(2)}) collective-permute-start(f32[136,128]{1,0:T(8,128)S(1)} %get-tuple-element.15), channel_id=1, source_target_pairs={{0,1},{1,0},{2,3},{3,2},{4,5},{5,4},{6,7},{7,6},{8,9},{9,8},{10,11... | collective-permute-start | bytes 208904 | tf_op jit(solution)/shard_map/ppermute | solution.py:370
  15.0 3.3 %collective-permute-start.3 = (f32[136,128]{1,0:T(8,128)S(1)}, f32[136,128]{1,0:T(8,128)S(1)}, u32[]{:S(2)}, u32[]{:S(2)}) collective-permute-start(f32[136,128]{1,0:T(8,128)S(1)} %get-tuple-element.16), channel_id=1, source_target_pairs={{0,15},{1,2},{2,1},{3,4},{4,3},{5,6},{6,5},{7,8},{8,7},{9,10},{10,... | collective-permute-start | bytes 208904 | tf_op jit(solution)/shard_map/ppermute | solution.py:371
  18.3 17.3 %all_to_all.25 = f32[128,1,128]{2,1,0:T(1,128)S(1)} all-to-all(f32[128,1,128]{2,1,0:T(1,128)S(1)} %bitcast.8), channel_id=1, replica_groups=mesh['wall'=8,'gas'=16] {'wall','gas'}, dimensions={0} | all-to-all | bytes 131072 | tf_op jit(solution)/shard_map/all_to_all | solution.py:355
  35.7 0.0 collective-permute-done.2.core_pack
  35.7 0.0 collective-permute-done.3.chip_pack
  35.7 0.0 copy-done.1
  35.7 0.0 copy-done.4
  35.7 7.2 %film.4 = f32[16,17,8,128]{3,2,1,0:T(8,128)S(1)} custom-call(s32[8,16]{1,0:T(8,128)S(1)} %copy-done.4, f32[4,128,512]{2,1,0:T(8,128)S(1)} %copy-done.1, f32[3,128,512]{2,1,0:T(8,128)S(1)} %get-tuple-element.10.sampled, s32[128,4]{1,0:T(8,128)S(1)} %copy.9.flags, f32[128,512]{1,0:T(8,128)S(1)} %copy-done.3, f32[36,512]{1,0:T(8,128)S(1)} %collective-permute-done.from_north, ...), custom_call_target="tpu_custom_call" | custom-call | tf_op jit(solution)/shard_map/film/pallas_call | solution.py:374
  42.9 22.7 %all_to_all.26.pieces = f32[16,17,8,128]{3,2,1,0:T(8,128)} all-to-all(f32[16,17,8,128]{3,2,1,0:T(8,128)S(1)} %film.4), channel_id=1, replica_groups=mesh['wall'=8,'gas'=16] {'gas'}, dimensions={0} | all-to-all | bytes 2228224 | tf_op jit(solution)/shard_map/all_to_all | solution.py:399
  65.5 1.4 %band_peak.1 = f32[8,128]{1,0:T(8,128)} custom-call(f32[16,17,8,128]{3,2,1,0:T(8,128)} %all_to_all.26.pieces), custom_call_target="tpu_custom_call" | custom-call | tf_op jit(solution)/shard_map/band_peak/pallas_call | solution.py:400
  67.0 3.3 %all-to-all-start.2 = ((f32[8,1,128]{2,1,0:T(1,128)}), f32[8,1,128]{2,1,0:T(1,128)S(1)}, u32[]{:S(2)}, u32[]{:S(2)}) async-start(f32[8,1,128]{2,1,0:T(1,128)} %bitcast.9), calls=%async_computation.2 | async-start | bytes 8192 | tf_op jit(solution)/shard_map/all_to_all | solution.py:411
  70.3 3.4 %strips.1 = f32[4,8,8192]{2,1,0:T(8,128)} custom-call(f32[16,17,8,128]{3,2,1,0:T(8,128)} %all_to_all.26.pieces), custom_call_target="tpu_custom_call" | custom-call | bytes 2097152 | tf_op jit(solution)/shard_map/strips/pallas_call | solution.py:413
  73.7 1.6 %all-to-all-done.2 = f32[8,1,128]{2,1,0:T(1,128)S(1)} async-done(((f32[8,1,128]{2,1,0:T(1,128)}), f32[8,1,128]{2,1,0:T(1,128)S(1)}, u32[]{:S(2)}, u32[]{:S(2)}) %all-to-all-start.2) | async-done | bytes 4128 | tf_op jit(solution)/shard_map/all_to_all | solution.py:411
  75.3 0.6 reduce_max.9
Async XLA Ops:
  1.4 1.2 %copy-start = (f32[4,128,512]{2,1,0:T(8,128)S(1)}, f32[4,128,512]{2,1,0:T(8,128)}, u32[]{:S(2)}) copy-start(f32[4,128,512]{2,1,0:T(8,128)} %film.5) | copy-start | bytes 3145732
  2.6 1.9 %copy-start.2 = (f32[3,4,128,512]{3,2,1,0:T(8,128)S(1)}, f32[3,4,128,512]{3,2,1,0:T(8,128)}, u32[]{:S(2)}) copy-start(f32[3,4,128,512]{3,2,1,0:T(8,128)} %gas.1) | copy-start | bytes 9437188
  4.5 0.9 %copy-start.3 = (f32[128,512]{1,0:T(8,128)S(1)}, f32[128,512]{1,0:T(8,128)}, u32[]{:S(2)}) copy-start(f32[128,512]{1,0:T(8,128)} %deposit.3) | copy-start | bytes 786436
  5.5 30.2 %copy-start.1 = (f32[4,128,512]{2,1,0:T(8,128)S(1)}, f32[4,128,512]{2,1,0:T(8,128)}, u32[]{:S(2)}) copy-start(f32[4,128,512]{2,1,0:T(8,128)} %film.5) | copy-start | bytes 3145732
  5.5 30.2 %copy-start.4 = (s32[8,16]{1,0:T(8,128)S(1)}, s32[8,16]{1,0:T(8,128)}, u32[]{:S(2)}) copy-start(s32[8,16]{1,0:T(8,128)} %owner_map.1) | copy-start | bytes 1540
  6.5 7.1 %collective-permute-start = (f32[36,512]{1,0:T(8,128)S(1)}, f32[36,512]{1,0:T(8,128)S(1)}, u32[]{:S(2)}, u32[]{:S(2)}) collective-permute-start(f32[36,512]{1,0:T(8,128)S(1)} %get-tuple-element.11), channel_id=1, source_target_pairs={{0,16},{16,32},{32,48},{48,64},{64,80},{80,96},{96,112},{112,0},{1... | collective-permute-start | bytes 221192 | tf_op jit(solution)/shard_map/ppermute | solution.py:358
  8.6 4.9 %collective-permute-start.1 = (f32[36,512]{1,0:T(8,128)S(1)}, f32[36,512]{1,0:T(8,128)S(1)}, u32[]{:S(2)}, u32[]{:S(2)}) collective-permute-start(f32[36,512]{1,0:T(8,128)S(1)} %get-tuple-element.12), channel_id=1, source_target_pairs={{16,0},{32,16},{48,32},{64,48},{80,64},{96,80},{112,96},{0,112},{1... | collective-permute-start | bytes 221192 | tf_op jit(solution)/shard_map/ppermute | solution.py:359
  13.7 22.0 %collective-permute-start.2 = (f32[136,128]{1,0:T(8,128)S(1)}, f32[136,128]{1,0:T(8,128)S(1)}, u32[]{:S(2)}, u32[]{:S(2)}) collective-permute-start(f32[136,128]{1,0:T(8,128)S(1)} %get-tuple-element.15), channel_id=1, source_target_pairs={{0,1},{1,0},{2,3},{3,2},{4,5},{5,4},{6,7},{7,6},{8,9},{9,8},{10,11... | collective-permute-start | bytes 208904 | tf_op jit(solution)/shard_map/ppermute | solution.py:370
  15.0 20.6 %collective-permute-start.3 = (f32[136,128]{1,0:T(8,128)S(1)}, f32[136,128]{1,0:T(8,128)S(1)}, u32[]{:S(2)}, u32[]{:S(2)}) collective-permute-start(f32[136,128]{1,0:T(8,128)S(1)} %get-tuple-element.16), channel_id=1, source_target_pairs={{0,15},{1,2},{2,1},{3,4},{4,3},{5,6},{6,5},{7,8},{8,7},{9,10},{10,... | collective-permute-start | bytes 208904 | tf_op jit(solution)/shard_map/ppermute | solution.py:371
  67.0 8.3 %all-to-all-start.2 = ((f32[8,1,128]{2,1,0:T(1,128)}), f32[8,1,128]{2,1,0:T(1,128)S(1)}, u32[]{:S(2)}, u32[]{:S(2)}) async-start(f32[8,1,128]{2,1,0:T(1,128)} %bitcast.9), calls=%async_computation.2 | async-start | bytes 8192 | tf_op jit(solution)/shard_map/all_to_all | solution.py:411

commit v3 on v2

--- a/solution.py
+++ b/solution.py
@@ -26,7 +26,7 @@
 FIELDS = 9
 STRIP = 8
 RING = ROWS + 24
-VMEM_LIMIT = 48 * 1024 * 1024
+VMEM_LIMIT = 24 << 20
 
 
 def lane_iota(shape):
@@ -52,46 +52,84 @@
     return packed
 
 
+def sample(gas, field, rows, cols):
+    value = LAYER_WEIGHTS[0] * gas[field, 0, rows, cols]
+    for layer in range(1, 4):
+        value = value + LAYER_WEIGHTS[layer] * gas[field, layer, rows, cols]
+    return value
+
+
+def flag_columns(flags_by_row):
+    flags = flags_by_row.astype(jnp.float32)
+    return jnp.transpose(jnp.concatenate([flags, flags], axis=0))
+
+
+def attached_rows(columns, rows, tile):
+    count = columns[rows, tile : tile + 1]
+    lane = lane_iota((count.shape[0], LANES)).astype(jnp.float32)
+    return jnp.where(lane < count, 1.0, 0.0)
+
+
 def edges_kernel(
-    gas, flags, film, deposit, sampled, to_north, to_south, core_pack, chip_pack, peak
+    gas_hbm,
+    flags_hbm,
+    film_hbm,
+    deposit_hbm,
+    sampled,
+    to_north,
+    to_south,
+    core_pack,
+    chip_pack,
+    peak,
+    film,
+    gas,
+    deposit,
+    flags,
+    sems,
 ):
-    lane8 = lane_iota((STRIP, LANES))
+    copies = [
+        pltpu.make_async_copy(film_hbm, film, sems.at[0]),
+        pltpu.make_async_copy(gas_hbm.at[0], gas.at[0], sems.at[1]),
+        pltpu.make_async_copy(gas_hbm.at[1], gas.at[1], sems.at[2]),
+        pltpu.make_async_copy(gas_hbm.at[2], gas.at[2], sems.at[3]),
+        pltpu.make_async_copy(flags_hbm, flags, sems.at[4]),
+        pltpu.make_async_copy(deposit_hbm, deposit, sems.at[5]),
+    ]
+    for copy in copies:
+        copy.start()
+    tiles = [slice(tile * LANES, (tile + 1) * LANES) for tile in range(TILES)]
+    copies[0].wait()
     best = jnp.zeros((STRIP, LANES), jnp.float32)
-    for tile in range(TILES):
-        cols = slice(tile * LANES, (tile + 1) * LANES)
-        for field in range(3):
-            value = LAYER_WEIGHTS[0] * gas[field, 0, :, cols]
-            for layer in range(1, 4):
-                value = value + LAYER_WEIGHTS[layer] * gas[field, layer, :, cols]
-            sampled[field, :, cols] = value
+    for cols in tiles:
         speed = film_speed(film[0, :, cols], film[1, :, cols], film[2, :, cols])
         for row in range(0, ROWS, STRIP):
             best = jnp.maximum(best, speed[row : row + STRIP])
     peak[...] = jnp.broadcast_to(jnp.max(best, keepdims=True), (ROWS, LANES))
-
-    def attached(rows, tile):
-        count = flags[rows, tile : tile + 1]
-        return jnp.where(lane_iota((count.shape[0], LANES)) < count, 1.0, 0.0)
+    every = slice(0, ROWS)
+    for field in range(3):
+        copies[1 + field].wait()
+        for cols in tiles:
+            sampled[field, :, cols] = sample(gas, field, every, cols)
+    copies[4].wait()
+    copies[5].wait()
+    columns = flag_columns(flags[...])
 
     def value_of(field, rows, tile):
-        cols = slice(tile * LANES, (tile + 1) * LANES)
         if field < 4:
-            return film[field, rows, cols]
+            return film[field, rows, tiles[tile]]
         if field < 7:
-            return sampled[field - 4, rows, cols]
+            return sampled[field - 4, rows, tiles[tile]]
         if field == 7:
-            return deposit[rows, cols]
-        return attached(rows, tile)
+            return deposit[rows, tiles[tile]]
+        return attached_rows(columns, rows, tile)
 
     for field in range(FIELDS):
-        for tile in range(TILES):
-            cols = slice(tile * LANES, (tile + 1) * LANES)
-            out = slice(4 * field, 4 * field + 4)
-            to_north[out, cols] = value_of(field, slice(0, 4), tile)
-            to_south[out, cols] = value_of(field, slice(ROWS - 4, ROWS), tile)
+        for tile, cols in enumerate(tiles):
+            target = slice(4 * field, 4 * field + 4)
+            to_north[target, cols] = value_of(field, slice(0, 4), tile)
+            to_south[target, cols] = value_of(field, slice(ROWS - 4, ROWS), tile)
 
     even = lax.rem(lax.axis_index("gas"), 2) == 0
-    every = slice(0, ROWS)
     west = pack_columns(lambda f: value_of(f, every, 0), ROWS, True)
     east = pack_columns(lambda f: value_of(f, every, TILES - 1), ROWS, False)
     core_pack[4 : 4 + ROWS, :] = jnp.where(even, east, west)
@@ -124,31 +162,60 @@
     return west, east
 
 
-def film_kernel(
-    owner_map,
+def wall_forcing(filtered, film_heat, attached):
+    along, across, gas_heat = filtered
+    contrast = gas_heat - film_heat
+    on_wall = attached > 0.5
+    square = along * along + across * across + SPEED_FLOOR * SPEED_FLOOR
+    speed = square * lax.rsqrt(square)
+    height = HEIGHT_RATIO * speed
+    scaled = height * lax.rsqrt(height)
+    uplus = jnp.log(1.0 + KAPPA * scaled) * (1.0 / KAPPA) + 7.8 * (
+        1.0
+        - jnp.exp(scaled * (-1.0 / 11.0))
+        - scaled * (1.0 / 11.0) * jnp.exp(scaled * (-1.0 / 3.0))
+    )
+    factor = jnp.where(on_wall, speed / (uplus * uplus), LAMINAR_SHEAR)
+    heat = jnp.where(
+        on_wall, speed / (PRANDTL_TURB * uplus + PRANDTL_JUMP), LAMINAR_HEAT
+    )
+    return factor * along, factor * across, heat * contrast
+
+
+def inside_kernel(
+    sampled,
+    film_hbm,
+    flags_hbm,
+    deposit_hbm,
+    from_north,
+    from_south,
+    ring,
+    force,
+    seam,
+    gas_ring,
+    attached,
     film,
-    sampled,
     flags,
     deposit,
-    from_north,
-    from_south,
-    core_pack,
-    chip_pack,
-    peaks,
-    out,
-    ring_a,
-    ring_b,
-    gas_ring,
-    force,
+    sems,
 ):
-    count = TILES + 1
+    pairs = (
+        (flags_hbm, flags),
+        (film_hbm, film),
+        (deposit_hbm, deposit),
+    )
+    copies = [
+        pltpu.make_async_copy(source, target, sems.at[index])
+        for index, (source, target) in enumerate(pairs)
+    ]
+    for copy in copies:
+        copy.start()
+    for copy in copies:
+        copy.wait()
     inner = slice(8, 8 + ROWS)
-    even = lax.rem(lax.axis_index("gas"), 2) == 0
-    wall = lax.axis_index("wall")
-    step = COURANT / jnp.max(peaks[...])
-
-    refs = [ring_a.at[f] for f in range(4)] + [gas_ring.at[f] for f in range(3)]
-    refs += [force.at[3], force.at[0]]
+    columns = flag_columns(flags[...])
+    refs = [ring.at[f] for f in range(4)] + [gas_ring.at[f] for f in range(3)]
+    refs += [force.at[3], attached]
     for field in range(FIELDS):
         ref = refs[field]
         for tile in range(TILES):
@@ -160,24 +227,19 @@
             elif field == 7:
                 ref[tile, inner, :] = deposit[:, cols]
             else:
-                ref[tile, inner, :] = jnp.where(
-                    lane_iota((ROWS, LANES)) < flags[:, tile : tile + 1], 1.0, 0.0
-                )
+                ref[tile, inner, :] = attached_rows(columns, slice(0, ROWS), tile)
             ref[tile, 4:8, :] = from_north[4 * field : 4 * field + 4, cols]
             ref[tile, 8 + ROWS : 12 + ROWS, :] = from_south[
                 4 * field : 4 * field + 4, cols
             ]
+    every = slice(4, 12 + ROWS)
     lane = lane_iota((ROWS + 8, LANES))
-    core, chip = core_pack[...], chip_pack[...]
-    east_side = jnp.where(even, core, chip)
-    west_side = jnp.where(even, chip, core)
-    for field in range(FIELDS):
-        value = jnp.where(
-            lane < LANES // 2,
-            pltpu.roll(east_side, (LANES - 4 * field) % LANES, 1),
-            pltpu.roll(west_side, (LANES - 4 - 4 * field) % LANES, 1),
+    for index, ref in enumerate(refs[4:7] + [refs[3], attached]):
+        seam[index, every, :] = jnp.where(
+            lane < LANES // 4,
+            ref[0, every, :],
+            pltpu.roll(ref[TILES - 1, every, :], LANES // 2, 1),
         )
-        refs[field][TILES, 4 : 12 + ROWS, :] = value
 
     def forcing_rows(index, carry):
         row = 4 + 8 * index
@@ -188,44 +250,108 @@
                 gas_ring[field, t, pl.ds(row - 1, STRIP), :]
                 + gas_ring[field, t, here, :]
                 + gas_ring[field, t, pl.ds(row + 1, STRIP), :]
-                for t in range(count)
+                for t in range(TILES)
             ]
             west, east = shifted_lanes(summed)
             filtered.append(
-                [(west[t] + summed[t] + east[t]) * (1.0 / 9.0) for t in range(count)]
+                [(west[t] + summed[t] + east[t]) * (1.0 / 9.0) for t in range(TILES)]
             )
-        for t in range(count):
-            along, across = filtered[0][t], filtered[1][t]
-            contrast = filtered[2][t] - ring_a[3, t, here, :]
-            on_wall = force[0, t, here, :] > 0.5
-            speed = jnp.sqrt(along * along + across * across + SPEED_FLOOR * SPEED_FLOOR)
-            scaled = jnp.sqrt(HEIGHT_RATIO * speed)
-            uplus = jnp.log(1.0 + KAPPA * scaled) * (1.0 / KAPPA) + 7.8 * (
-                1.0
-                - jnp.exp(scaled * (-1.0 / 11.0))
-                - scaled * (1.0 / 11.0) * jnp.exp(scaled * (-1.0 / 3.0))
+        for t in range(TILES):
+            result = wall_forcing(
+                [filtered[f][t] for f in range(3)],
+                ring[3, t, here, :],
+                attached[t, here, :],
             )
-            factor = jnp.where(on_wall, speed / (uplus * uplus), LAMINAR_SHEAR)
-            heat = jnp.where(
-                on_wall, speed / (PRANDTL_TURB * uplus + PRANDTL_JUMP), LAMINAR_HEAT
+            for field in range(3):
+                force[field, t, here, :] = result[field]
+        return carry
+
+    grouped(3, 18, forcing_rows, 0)
+
+
+def film_kernel(
+    owner_map,
+    ring,
+    force_in,
+    seam_in,
+    core_pack,
+    chip_pack,
+    peaks,
+    out,
+    halo,
+    seam,
+    ring_a,
+    ring_b,
+    force,
+):
+    count = TILES + 1
+    even = lax.rem(lax.axis_index("gas"), 2) == 0
+    wall = lax.axis_index("wall")
+    step = COURANT / jnp.max(peaks[...])
+
+    every = slice(4, 12 + ROWS)
+    lane = lane_iota((ROWS + 8, LANES))
+    core, chip = core_pack[...], chip_pack[...]
+    east_side = jnp.where(even, core, chip)
+    west_side = jnp.where(even, chip, core)
+    for field in (0, 1, 2, 3, 7):
+        value = jnp.where(
+            lane < LANES // 2,
+            pltpu.roll(east_side, (LANES - 4 * field) % LANES, 1),
+            pltpu.roll(west_side, (LANES - 4 - 4 * field) % LANES, 1),
+        )
+        if field == 7:
+            force[3, TILES, every, :] = step * value
+        else:
+            halo[field, every, :] = value
+    for index, field in enumerate((4, 5, 6, 3, 8)):
+        east = pltpu.roll(east_side, (LANES // 2 - 4 * field) % LANES, 1)
+        west = pltpu.roll(west_side, (LANES - 4 - 4 * field) % LANES, 1)
+        value = jnp.where(
+            (lane >= LANES // 2) & (lane < LANES // 2 + 4), east, seam_in[index, every, :]
+        )
+        seam[index, every, :] = jnp.where(lane >= LANES - 4, west, value)
+
+    def seam_rows(index, carry):
+        row = 4 + 8 * index
+        here = pl.ds(row, STRIP)
+        lanes = lane_iota((STRIP, LANES))
+        filtered = []
+        for field in range(3):
+            summed = (
+                seam[field, pl.ds(row - 1, STRIP), :]
+                + seam[field, here, :]
+                + seam[field, pl.ds(row + 1, STRIP), :]
             )
-            force[0, t, here, :] = step * (factor * along)
-            force[1, t, here, :] = step * (factor * across)
-            force[2, t, here, :] = step * (heat * contrast)
-            force[3, t, here, :] = step * force[3, t, here, :]
+            west, east = pltpu.roll(summed, 1, 1), pltpu.roll(summed, LANES - 1, 1)
+            filtered.append((west + summed + east) * (1.0 / 9.0))
+        result = wall_forcing(filtered, seam[3, here, :], seam[4, here, :])
+        for field in range(3):
+            first = step * result[field]
+            last = pltpu.roll(first, LANES // 2, 1)
+            force[field, TILES, here, :] = jnp.where(lanes < LANES // 2, last, first)
+            for t in range(TILES):
+                value = step * force_in[field, t, here, :]
+                if t == 0:
+                    value = jnp.where(lanes == 0, first, value)
+                if t == TILES - 1:
+                    value = jnp.where(lanes == LANES - 1, last, value)
+                force[field, t, here, :] = value
+        for t in range(TILES):
+            force[3, t, here, :] = step * force_in[3, t, here, :]
         return carry
 
-    grouped(3, 18, forcing_rows, 0)
+    grouped(6, 18, seam_rows, 0)
 
     half = 0.5 * step
 
-    def advance(source, row):
+    def advance(load, row):
         here = pl.ds(row, STRIP)
         centre, wests, easts, norths, souths = [], [], [], [], []
         for field in range(4):
-            middle = [source[field, t, here, :] for t in range(count)]
-            north = [source[field, t, pl.ds(row - 1, STRIP), :] for t in range(count)]
-            south = [source[field, t, pl.ds(row + 1, STRIP), :] for t in range(count)]
+            middle = [load(field, t, here) for t in range(count)]
+            north = [load(field, t, pl.ds(row - 1, STRIP)) for t in range(count)]
+            south = [load(field, t, pl.ds(row + 1, STRIP)) for t in range(count)]
             west, east = shifted_lanes(middle)
             centre.append(middle)
             wests.append(west)
@@ -276,13 +402,19 @@
 
         grouped(6, 18, body, 0)
 
-    middle_rows(ring_a, ring_b)
-    middle_rows(ring_b, ring_a)
-    middle_rows(ring_a, ring_b)
+    def first_load(field, t, rows):
+        return ring[field, t, rows, :] if t < TILES else halo[field, rows, :]
+
+    def load_from(source):
+        return lambda field, t, rows: source[field, t, rows, :]
+
+    middle_rows(first_load, ring_a)
+    middle_rows(load_from(ring_a), ring_b)
+    middle_rows(load_from(ring_b), ring_a)
 
     def last_rows(index, best):
         row = pl.multiple_of(8 + 8 * index, 8)
-        news = advance(ring_b, row)
+        news = advance(load_from(ring_a), row)
         place = owner_map[wall, index]
         for t in range(TILES):
             for field in range(4):
@@ -297,17 +429,18 @@
 
 
 def band_peak_kernel(pieces, peak):
-    best = pieces[0, 0]
+    best = pieces[0, 4 * TILES]
     for source in range(1, pieces.shape[0]):
-        best = jnp.maximum(best, pieces[source, 0])
+        best = jnp.maximum(best, pieces[source, 4 * TILES])
     peak[...] = best
 
 
 def strips_kernel(pieces, out):
+    first = pl.program_id(0) * TILES
     for source in range(pieces.shape[0]):
         for t in range(TILES):
             start = source * COLS + t * LANES
-            out[0, :, start : start + LANES] = pieces[source, t]
+            out[0, :, start : start + LANES] = pieces[source, first + t]
 
 
 def grouped(unroll, total, body, carry):
@@ -324,6 +457,10 @@
     return carry
 
 
+def in_hbm(*arrays):
+    return [pltpu.with_memory_space_constraint(a, pltpu.HBM) for a in arrays]
+
+
 def vmem(count):
     return [pl.BlockSpec(memory_space=pltpu.VMEM)] * count
 
@@ -334,6 +471,8 @@
 
 def coupling_step(gas_state, wall_flags, film_state, deposit, owner_map):
     params = pltpu.CompilerParams(vmem_limit_bytes=VMEM_LIMIT)
+    tail = pltpu.CompilerParams(vmem_limit_bytes=8 << 20)
+    flags = jnp.transpose(wall_flags)
     sampled, to_north, to_south, core_main, chip_main, peak = pl.pallas_call(
         edges_kernel,
         out_shape=(
@@ -344,11 +483,18 @@
             shape(ROWS + 8, LANES),
             shape(ROWS, LANES),
         ),
-        in_specs=vmem(4),
+        in_specs=[pl.BlockSpec(memory_space=pltpu.HBM)] * 4,
         out_specs=tuple(vmem(6)),
-        compiler_params=params,
+        scratch_shapes=[
+            pltpu.VMEM((4, ROWS, COLS), jnp.float32),
+            pltpu.VMEM((3, 4, ROWS, COLS), jnp.float32),
+            pltpu.VMEM((ROWS, COLS), jnp.float32),
+            pltpu.VMEM((TILES, ROWS), jnp.int32),
+            pltpu.SemaphoreType.DMA((6,)),
+        ],
+        compiler_params=pltpu.CompilerParams(vmem_limit_bytes=VMEM_LIMIT),
         name="edges",
-    )(gas_state, wall_flags, film_state, deposit)
+    )(*in_hbm(gas_state, flags, film_state, deposit))
 
     walls, gases = lax.axis_size("wall"), lax.axis_size("gas")
     both = ("wall", "gas")
@@ -370,41 +516,49 @@
     core_pack = lax.ppermute(core_pack, "gas", partner)
     chip_pack = lax.ppermute(chip_pack, "gas", outer)
 
-    ring = (4, TILES + 1, RING, LANES)
+    inner = (4, TILES, RING, LANES)
+    ring, force, seam = pl.pallas_call(
+        inside_kernel,
+        out_shape=(shape(*inner), shape(*inner), shape(5, RING, LANES)),
+        in_specs=vmem(1) + [pl.BlockSpec(memory_space=pltpu.HBM)] * 3 + vmem(2),
+        out_specs=tuple(vmem(3)),
+        scratch_shapes=[
+            pltpu.VMEM((3,) + inner[1:], jnp.float32),
+            pltpu.VMEM(inner[1:], jnp.float32),
+            pltpu.VMEM((4, ROWS, COLS), jnp.float32),
+            pltpu.VMEM((TILES, ROWS), jnp.int32),
+            pltpu.VMEM((ROWS, COLS), jnp.float32),
+            pltpu.SemaphoreType.DMA((3,)),
+        ],
+        compiler_params=pltpu.CompilerParams(vmem_limit_bytes=24 << 20),
+        cost_estimate=pl.CostEstimate(
+            flops=20 << 20, bytes_accessed=8 << 20, transcendentals=1 << 19
+        ),
+        name="inside",
+    )(sampled, *in_hbm(film_state, flags, deposit), from_north, from_south)
+    outer_ring = (4, TILES + 1, RING, LANES)
     pieces = pl.pallas_call(
         film_kernel,
         out_shape=shape(gases, 4 * TILES + 1, STRIP, LANES),
-        in_specs=[pl.BlockSpec(memory_space=pltpu.SMEM)] + vmem(9),
+        in_specs=[pl.BlockSpec(memory_space=pltpu.SMEM)] + vmem(6),
         out_specs=vmem(1)[0],
         scratch_shapes=[
-            pltpu.VMEM(ring, jnp.float32),
-            pltpu.VMEM(ring, jnp.float32),
-            pltpu.VMEM((3,) + ring[1:], jnp.float32),
-            pltpu.VMEM(ring, jnp.float32),
+            pltpu.VMEM((4, RING, LANES), jnp.float32),
+            pltpu.VMEM((5, RING, LANES), jnp.float32),
+            pltpu.VMEM(outer_ring, jnp.float32),
+            pltpu.VMEM(outer_ring, jnp.float32),
+            pltpu.VMEM(outer_ring, jnp.float32),
         ],
-        compiler_params=params,
+        compiler_params=pltpu.CompilerParams(vmem_limit_bytes=24 << 20),
         name="film",
-    )(
-        owner_map,
-        film_state,
-        sampled,
-        wall_flags,
-        deposit,
-        from_north,
-        from_south,
-        core_pack,
-        chip_pack,
-        peaks,
-    )
+    )(owner_map, ring, force, seam, core_pack, chip_pack, peaks)
     pieces = lax.all_to_all(pieces, "gas", split_axis=0, concat_axis=0, tiled=True)
     band_peak = pl.pallas_call(
         band_peak_kernel,
         out_shape=shape(STRIP, LANES),
-        grid=(1,),
-        in_specs=[
-            pl.BlockSpec((gases, 1, STRIP, LANES), lambda i: (0, 4 * TILES, 0, 0))
-        ],
-        out_specs=pl.BlockSpec((STRIP, LANES), lambda i: (0, 0)),
+        in_specs=vmem(1),
+        out_specs=vmem(1)[0],
+        compiler_params=tail,
         name="band_peak",
     )(pieces)
     cfl = jnp.max(
@@ -414,7 +568,8 @@
         strips_kernel,
         out_shape=shape(4, STRIP, gases * COLS),
         grid=(4,),
-        in_specs=[pl.BlockSpec((gases, TILES, STRIP, LANES), lambda i: (0, i, 0, 0))],
+        in_specs=vmem(1),
+        compiler_params=tail,
         out_specs=pl.BlockSpec((1, STRIP, gases * COLS), lambda i: (i, 0, 0)),
         cost_estimate=pl.CostEstimate(
             flops=0, bytes_accessed=2 << 20, transcendentals=0

time: 76.5 us -> 74 us (0.967)
  blocking collectives: 40 us -> 22.5 us
  starting transfers between devices: 13 us -> 21 us
  waiting for transfers between devices: 3.65 us -> 11.3 us
  local copies, waits for them, and re-layouts: 4.85 us -> 1.73 us
  Pallas kernels: 13.1 us -> 15.7 us
    all_to_all x1 -> x0, blocking collectives: 17.3 us -> none  [coupling_step(): peaks = lax.all_to_all(peak, both, split_axis=0, concat_axis=0, tiled=True)]
    all_to_all x0 -> x1, starting transfers between devices: none -> 8.12 us  [coupling_step(): peaks = lax.all_to_all(peak, both, split_axis=0, concat_axis=0, tiled=True)]
    all_to_all x0 -> x1, waiting for transfers between devices: none -> 5.77 us  [coupling_step(): peaks = lax.all_to_all(peak, both, split_axis=0, concat_axis=0, tiled=True)]
    unnamed x11 -> x6, local copies, waits for them, and re-layouts: 4.85 us -> 1.73 us
    pallas_call x1, Pallas kernels: 0.96 us -> 3.42 us  [coupling_step(): pl.pallas_call(edges_kernel, out_shape=(shape(3, ROWS, COLS), shape(4 * F...]
    pallas_call x1 -> x2, Pallas kernels: 1.45 us -> 3.56 us  [the longest x1 2.96 us: coupling_step(): pl.pallas_call(inside_kernel, out_shape=(shape(*inner), shape(*inner), sh...]
    all_to_all x1, waiting for transfers between devices: 1.58 us -> 3.41 us  [coupling_step(): lax.all_to_all(band_peak, 'wall', split_axis=0, concat_axis=0, tiled=True)]
    pallas_call x1, Pallas kernels: 3.38 us -> 1.55 us  [coupling_step(): pl.pallas_call(strips_kernel, out_shape=shape(4, STRIP, gases * COLS), gr...]
  transfers between devices with their start and end apart: 5 -> 6, of which waited for: 2 -> 3; matrix products, arithmetic and copies ran while one was open for 0% -> 0% of each run, Pallas kernels for 4% -> 6%
where the time goes in v3:
time: 74 us; the launch traced here: 73.5 us
  blocking collectives  22.5 us (30%)
  starting transfers between devices  21 us (28%)
  Pallas kernels  15.7 us (21%)
  waiting for transfers between devices  11.3 us (15%)
  local copies, waits for them, and re-layouts  1.73 us (2%)
    all_to_all x1, blocking collectives, coupling_step(): lax.all_to_all(pieces, 'gas', split_axis=0, concat_axis=0, tiled=True)  22.5 us
    all_to_all x1, starting transfers between devices, coupling_step(): peaks = lax.all_to_all(peak, both, split_axis=0, concat_axis=0, tiled=True)  8.12 us
    pallas_call x1, Pallas kernels, coupling_step(): pl.pallas_call(film_kernel, out_shape=shape(gases, 4 * TILES + 1, STRIP,...  6.36 us
    all_to_all x1, waiting for transfers between devices, coupling_step(): peaks = lax.all_to_all(peak, both, split_axis=0, concat_axis=0, tiled=True)  5.77 us
    pallas_call x1, Pallas kernels, coupling_step(): pl.pallas_call(edges_kernel, out_shape=(shape(3, ROWS, COLS), shape(4 * F...  3.42 us
    all_to_all x1, waiting for transfers between devices, coupling_step(): lax.all_to_all(band_peak, 'wall', split_axis=0, concat_axis=0, tiled=True)  3.41 us
    all_to_all x1, starting transfers between devices, coupling_step(): lax.all_to_all(band_peak, 'wall', split_axis=0, concat_axis=0, tiled=True)  3.32 us
    ppermute x1, starting transfers between devices, coupling_step(): chip_pack = lax.ppermute(chip_pack, 'gas', outer)  3.22 us
  transfers between devices with their start and end apart: 6, of which 3 were waited for; matrix products, arithmetic and copies ran while one was open for 0% of the time, Pallas kernels for 6%

profile of v3, /device:TPU:1, one launch (start us, length us, event | category | flops | bytes accessed | tf_op | source)
XLA Modules:
  0.0 73.5 jit_solution(11221220077224750083)
XLA Ops:
  0.6 3.4 %edges.1 = (f32[3,128,512]{2,1,0:T(8,128)S(1)}, f32[36,512]{1,0:T(8,128)S(1)}, f32[36,512]{1,0:T(8,128)S(1)}, f32[136,128]{1,0:T(8,128)S(1)}, f32[136,128]{1,0:T(8,128)S(1)}, /*index=5*/f32[128,128]{1,0:T(8,128)}) custom-call(f32[3,4,128,512]{3,2,1,0:T(8,128)} %gas_hbm.1, s32[4,128]{1,0:T(4,128)} %bitcast.9, f32[4,128,512]{2,1,0:T(8,128)} %film_hbm.3, ...), custom_call_target="tpu_custom_call" | custom-call | tf_op jit(solution)/shard_map/edges/pallas_call | solution.py:476
  4.1 2.2 %collective-permute-start = (f32[36,512]{1,0:T(8,128)S(1)}, f32[36,512]{1,0:T(8,128)S(1)}, u32[]{:S(2)}, u32[]{:S(2)}) collective-permute-start(f32[36,512]{1,0:T(8,128)S(1)} %get-tuple-element.14), channel_id=1, source_target_pairs={{0,16},{16,32},{32,48},{48,64},{64,80},{80,96},{96,112},{112,0},{1... | collective-permute-start | bytes 221192 | tf_op jit(solution)/shard_map/ppermute | solution.py:504
  6.2 2.9 %collective-permute-start.1 = (f32[36,512]{1,0:T(8,128)S(1)}, f32[36,512]{1,0:T(8,128)S(1)}, u32[]{:S(2)}, u32[]{:S(2)}) collective-permute-start(f32[36,512]{1,0:T(8,128)S(1)} %get-tuple-element.15), channel_id=1, source_target_pairs={{16,0},{32,16},{48,32},{64,48},{80,64},{96,80},{112,96},{0,112},{1... | collective-permute-start | bytes 221192 | tf_op jit(solution)/shard_map/ppermute | solution.py:505
  9.1 2.1 %collective-permute-done.from_north = f32[36,512]{1,0:T(8,128)S(1)} collective-permute-done((f32[36,512]{1,0:T(8,128)S(1)}, f32[36,512]{1,0:T(8,128)S(1)}, u32[]{:S(2)}, u32[]{:S(2)}) %collective-permute-start) | collective-permute-done | bytes 73760 | tf_op jit(solution)/shard_map/ppermute | solution.py:504
  11.2 0.0 collective-permute-done.1.from_south
  11.2 0.8 %corners.1 = (f32[136,128]{1,0:T(8,128)}, f32[136,128]{1,0:T(8,128)}) custom-call(f32[36,512]{1,0:T(8,128)S(1)} %collective-permute-done.from_north, f32[36,512]{1,0:T(8,128)S(1)} %collective-permute-done.1.from_south, f32[136,128]{1,0:T(8,128)S(1)} %get-tuple-element.19.core_in, f32[136,128]{1,0:T(8,128)S(1)} %get-tuple-element.20.chip_in), custom_call_target="tpu_custom_call" | custom-call | tf_op jit(solution)/shard_map/corners/pallas_call | solution.py:506
  11.9 0.0 copy-start.2
  12.0 1.3 %collective-permute-start.2 = (f32[136,128]{1,0:T(8,128)}, f32[136,128]{1,0:T(8,128)}, u32[]{:S(2)}, u32[]{:S(2)}) collective-permute-start(f32[136,128]{1,0:T(8,128)} %get-tuple-element.21), channel_id=1, source_target_pairs={{0,1},{1,0},{2,3},{3,2},{4,5},{5,4},{6,7},{7,6},{8,9},{9,8},{10,11... | collective-permute-start | bytes 208904 | tf_op jit(solution)/shard_map/ppermute | solution.py:516
  13.2 3.2 %collective-permute-start.3 = (f32[136,128]{1,0:T(8,128)}, f32[136,128]{1,0:T(8,128)}, u32[]{:S(2)}, u32[]{:S(2)}) collective-permute-start(f32[136,128]{1,0:T(8,128)} %get-tuple-element.22), channel_id=1, source_target_pairs={{0,15},{1,2},{2,1},{3,4},{4,3},{5,6},{6,5},{7,8},{8,7},{9,10},{10,... | collective-permute-start | bytes 208904 | tf_op jit(solution)/shard_map/ppermute | solution.py:517
  16.4 8.1 %all-to-all-start = ((f32[128,1,128]{2,1,0:T(1,128)}), f32[128,1,128]{2,1,0:T(1,128)S(1)}, u32[]{:S(2)}, u32[]{:S(2)}) async-start(f32[128,1,128]{2,1,0:T(1,128)} %bitcast.2), calls=%async_computation | async-start | bytes 131072 | tf_op jit(solution)/shard_map/all_to_all | solution.py:501
  24.6 3.0 %inside.1 = (f32[4,4,152,128]{3,2,1,0:T(8,128)S(1)}, f32[4,4,152,128]{3,2,1,0:T(8,128)S(1)}, f32[5,152,128]{2,1,0:T(8,128)S(1)}) custom-call(f32[3,128,512]{2,1,0:T(8,128)S(1)} %get-tuple-element.13.sampled, f32[4,128,512]{2,1,0:T(8,128)} %film_hbm.3, s32[4,128]{1,0:T(4,128)} %bitcast.10, f32[128,512]{1,0:T(8,128)} %deposit_hbm.3, ...), custom_call_target="tpu_custom_call" | custom-call | flops 20971520 | bytes 8388608 | tf_op jit(solution)/shard_map/inside/pallas_call | solution.py:520
  27.5 0.0 copy-start
  27.5 0.7 %copy-done = f32[5,152,128]{2,1,0:T(8,128)} copy-done((f32[5,152,128]{2,1,0:T(8,128)}, f32[5,152,128]{2,1,0:T(8,128)S(1)}, u32[]{:S(2)}) %copy-start) | copy-done | bytes 389144
  28.3 5.8 %all-to-all-done = f32[128,1,128]{2,1,0:T(1,128)S(1)} async-done(((f32[128,1,128]{2,1,0:T(1,128)}), f32[128,1,128]{2,1,0:T(1,128)S(1)}, u32[]{:S(2)}, u32[]{:S(2)}) %all-to-all-start) | async-done | bytes 65568 | tf_op jit(solution)/shard_map/all_to_all | solution.py:501
  34.0 0.0 collective-permute-done.2.core_pack
  34.0 0.0 collective-permute-done.3.chip_pack
  34.1 0.0 copy-done.2
  34.1 0.0 copy-start.1
  34.1 1.0 %copy-done.1 = f32[5,152,128]{2,1,0:T(8,128)S(1)} copy-done((f32[5,152,128]{2,1,0:T(8,128)S(1)}, f32[5,152,128]{2,1,0:T(8,128)}, u32[]{:S(2)}) %copy-start.1) | copy-done | bytes 389144
  35.1 6.4 %film.1 = f32[16,17,8,128]{3,2,1,0:T(8,128)S(1)} custom-call(s32[8,16]{1,0:T(8,128)S(1)} %copy-done.2, f32[4,4,152,128]{3,2,1,0:T(8,128)S(1)} %get-tuple-element.16.ring, f32[4,4,152,128]{3,2,1,0:T(8,128)S(1)} %get-tuple-element.17.force_in, f32[5,152,128]{2,1,0:T(8,128)S(1)} %copy-done.1, f32[136,128]{1,0:T(8,128)} %collective-permute-done.2.core_pack, ...), custom_call_target="tpu_custom_call" | custom-call | tf_op jit(solution)/shard_map/film/pallas_call | solution.py:540
  41.4 22.5 %all_to_all.25.pieces = f32[16,17,8,128]{3,2,1,0:T(8,128)S(1)} all-to-all(f32[16,17,8,128]{3,2,1,0:T(8,128)S(1)} %film.1), channel_id=1, replica_groups=mesh['wall'=8,'gas'=16] {'gas'}, dimensions={0} | all-to-all | bytes 2228224 | tf_op jit(solution)/shard_map/all_to_all | solution.py:555
  64.0 0.6 band_peak.1
  64.6 3.3 %all-to-all-start.2 = ((f32[8,1,128]{2,1,0:T(1,128)}), f32[8,1,128]{2,1,0:T(1,128)S(1)}, u32[]{:S(2)}, u32[]{:S(2)}) async-start(f32[8,1,128]{2,1,0:T(1,128)} %bitcast.5), calls=%async_computation.2 | async-start | bytes 8192 | tf_op jit(solution)/shard_map/all_to_all | solution.py:565
  67.9 1.5 %strips.1 = f32[4,8,8192]{2,1,0:T(8,128)} custom-call(f32[16,17,8,128]{3,2,1,0:T(8,128)S(1)} %all_to_all.25.pieces), custom_call_target="tpu_custom_call" | custom-call | bytes 2097152 | tf_op jit(solution)/shard_map/strips/pallas_call | solution.py:567
  69.4 3.4 %all-to-all-done.2 = f32[8,1,128]{2,1,0:T(1,128)S(1)} async-done(((f32[8,1,128]{2,1,0:T(1,128)}), f32[8,1,128]{2,1,0:T(1,128)S(1)}, u32[]{:S(2)}, u32[]{:S(2)}) %all-to-all-start.2) | async-done | bytes 4128 | tf_op jit(solution)/shard_map/all_to_all | solution.py:565
  72.9 0.6 reduce_max.9
Async XLA Ops:
  4.1 7.1 %collective-permute-start = (f32[36,512]{1,0:T(8,128)S(1)}, f32[36,512]{1,0:T(8,128)S(1)}, u32[]{:S(2)}, u32[]{:S(2)}) collective-permute-start(f32[36,512]{1,0:T(8,128)S(1)} %get-tuple-element.14), channel_id=1, source_target_pairs={{0,16},{16,32},{32,48},{48,64},{64,80},{80,96},{96,112},{112,0},{1... | collective-permute-start | bytes 221192 | tf_op jit(solution)/shard_map/ppermute | solution.py:504
  6.2 4.9 %collective-permute-start.1 = (f32[36,512]{1,0:T(8,128)S(1)}, f32[36,512]{1,0:T(8,128)S(1)}, u32[]{:S(2)}, u32[]{:S(2)}) collective-permute-start(f32[36,512]{1,0:T(8,128)S(1)} %get-tuple-element.15), channel_id=1, source_target_pairs={{16,0},{32,16},{48,32},{64,48},{80,64},{96,80},{112,96},{0,112},{1... | collective-permute-start | bytes 221192 | tf_op jit(solution)/shard_map/ppermute | solution.py:505
  11.9 22.1 %copy-start.2 = (s32[8,16]{1,0:T(8,128)S(1)}, s32[8,16]{1,0:T(8,128)}, u32[]{:S(2)}) copy-start(s32[8,16]{1,0:T(8,128)} %owner_map.1) | copy-start | bytes 1540
  12.0 22.1 %collective-permute-start.2 = (f32[136,128]{1,0:T(8,128)}, f32[136,128]{1,0:T(8,128)}, u32[]{:S(2)}, u32[]{:S(2)}) collective-permute-start(f32[136,128]{1,0:T(8,128)} %get-tuple-element.21), channel_id=1, source_target_pairs={{0,1},{1,0},{2,3},{3,2},{4,5},{5,4},{6,7},{7,6},{8,9},{9,8},{10,11... | collective-permute-start | bytes 208904 | tf_op jit(solution)/shard_map/ppermute | solution.py:516
  13.2 20.8 %collective-permute-start.3 = (f32[136,128]{1,0:T(8,128)}, f32[136,128]{1,0:T(8,128)}, u32[]{:S(2)}, u32[]{:S(2)}) collective-permute-start(f32[136,128]{1,0:T(8,128)} %get-tuple-element.22), channel_id=1, source_target_pairs={{0,15},{1,2},{2,1},{3,4},{4,3},{5,6},{6,5},{7,8},{8,7},{9,10},{10,... | collective-permute-start | bytes 208904 | tf_op jit(solution)/shard_map/ppermute | solution.py:517
  16.4 17.6 %all-to-all-start = ((f32[128,1,128]{2,1,0:T(1,128)}), f32[128,1,128]{2,1,0:T(1,128)S(1)}, u32[]{:S(2)}, u32[]{:S(2)}) async-start(f32[128,1,128]{2,1,0:T(1,128)} %bitcast.2), calls=%async_computation | async-start | bytes 131072 | tf_op jit(solution)/shard_map/all_to_all | solution.py:501
  27.5 0.7 %copy-start = (f32[5,152,128]{2,1,0:T(8,128)}, f32[5,152,128]{2,1,0:T(8,128)S(1)}, u32[]{:S(2)}) copy-start(f32[5,152,128]{2,1,0:T(8,128)S(1)} %get-tuple-element.18.seam_in) | copy-start | bytes 1167364
  34.1 1.0 %copy-start.1 = (f32[5,152,128]{2,1,0:T(8,128)S(1)}, f32[5,152,128]{2,1,0:T(8,128)}, u32[]{:S(2)}) copy-start(f32[5,152,128]{2,1,0:T(8,128)} %copy-done) | copy-start | bytes 1167364
  64.6 8.3 %all-to-all-start.2 = ((f32[8,1,128]{2,1,0:T(1,128)}), f32[8,1,128]{2,1,0:T(1,128)S(1)}, u32[]{:S(2)}, u32[]{:S(2)}) async-start(f32[8,1,128]{2,1,0:T(1,128)} %bitcast.5), calls=%async_computation.2 | async-start | bytes 8192 | tf_op jit(solution)/shard_map/all_to_all | solution.py:565

commit v4 on v3

--- a/solution.py
+++ b/solution.py
@@ -25,7 +25,8 @@
 TILES = COLS // LANES
 FIELDS = 9
 STRIP = 8
-RING = ROWS + 24
+RING = ROWS + 16
+AHEAD = 8
 VMEM_LIMIT = 24 << 20
 
 
@@ -75,7 +76,7 @@
     flags_hbm,
     film_hbm,
     deposit_hbm,
-    sampled,
+    gas_ring,
     to_north,
     to_south,
     core_pack,
@@ -89,15 +90,36 @@
 ):
     copies = [
         pltpu.make_async_copy(film_hbm, film, sems.at[0]),
-        pltpu.make_async_copy(gas_hbm.at[0], gas.at[0], sems.at[1]),
-        pltpu.make_async_copy(gas_hbm.at[1], gas.at[1], sems.at[2]),
-        pltpu.make_async_copy(gas_hbm.at[2], gas.at[2], sems.at[3]),
-        pltpu.make_async_copy(flags_hbm, flags, sems.at[4]),
-        pltpu.make_async_copy(deposit_hbm, deposit, sems.at[5]),
+        pltpu.make_async_copy(flags_hbm, flags, sems.at[1]),
+        pltpu.make_async_copy(deposit_hbm, deposit, sems.at[2]),
+        pltpu.make_async_copy(gas_hbm.at[0], gas.at[0], sems.at[3]),
+        pltpu.make_async_copy(gas_hbm.at[1], gas.at[1], sems.at[4]),
+        pltpu.make_async_copy(gas_hbm.at[2], gas.at[2], sems.at[5]),
     ]
     for copy in copies:
         copy.start()
     tiles = [slice(tile * LANES, (tile + 1) * LANES) for tile in range(TILES)]
+    every = slice(0, ROWS)
+    even = lax.rem(lax.axis_index("gas"), 2) == 0
+    lane = lane_iota((ROWS, LANES))
+
+    def send(field, value_of):
+        target = slice(4 * field, 4 * field + 4)
+        for tile, cols in enumerate(tiles):
+            to_north[target, cols] = value_of(slice(0, 4), tile)
+            to_south[target, cols] = value_of(slice(ROWS - 4, ROWS), tile)
+        west = value_of(every, 0)
+        if field:
+            west = pltpu.roll(west, 4 * field, 1)
+        east = pltpu.roll(value_of(every, TILES - 1), 4 * field + 4, 1)
+        here = (lane >= 4 * field) & (lane < 4 * field + 4)
+        for pack, value in (
+            (core_pack, jnp.where(even, east, west)),
+            (chip_pack, jnp.where(even, west, east)),
+        ):
+            old = pack[4 : 4 + ROWS, :] if field else jnp.zeros_like(value)
+            pack[4 : 4 + ROWS, :] = jnp.where(here, value, old)
+
     copies[0].wait()
     best = jnp.zeros((STRIP, LANES), jnp.float32)
     for cols in tiles:
@@ -105,35 +127,23 @@
         for row in range(0, ROWS, STRIP):
             best = jnp.maximum(best, speed[row : row + STRIP])
     peak[...] = jnp.broadcast_to(jnp.max(best, keepdims=True), (ROWS, LANES))
-    every = slice(0, ROWS)
+    for field in range(4):
+        send(field, lambda rows, tile, f=field: film[f, rows, tiles[tile]])
+    copies[1].wait()
+    columns = flag_columns(flags[...])
+    send(8, lambda rows, tile: attached_rows(columns, rows, tile))
+    copies[2].wait()
+    send(7, lambda rows, tile: deposit[rows, tiles[tile]])
     for field in range(3):
-        copies[1 + field].wait()
-        for cols in tiles:
-            sampled[field, :, cols] = sample(gas, field, every, cols)
-    copies[4].wait()
-    copies[5].wait()
-    columns = flag_columns(flags[...])
-
-    def value_of(field, rows, tile):
-        if field < 4:
-            return film[field, rows, tiles[tile]]
-        if field < 7:
-            return sampled[field - 4, rows, tiles[tile]]
-        if field == 7:
-            return deposit[rows, tiles[tile]]
-        return attached_rows(columns, rows, tile)
-
-    for field in range(FIELDS):
+        copies[3 + field].wait()
         for tile, cols in enumerate(tiles):
-            target = slice(4 * field, 4 * field + 4)
-            to_north[target, cols] = value_of(field, slice(0, 4), tile)
-            to_south[target, cols] = value_of(field, slice(ROWS - 4, ROWS), tile)
-
-    even = lax.rem(lax.axis_index("gas"), 2) == 0
-    west = pack_columns(lambda f: value_of(f, every, 0), ROWS, True)
-    east = pack_columns(lambda f: value_of(f, every, TILES - 1), ROWS, False)
-    core_pack[4 : 4 + ROWS, :] = jnp.where(even, east, west)
-    chip_pack[4 : 4 + ROWS, :] = jnp.where(even, west, east)
+            gas_ring[field, tile, 16 : 16 + ROWS, :] = sample(gas, field, every, cols)
+        send(
+            4 + field,
+            lambda rows, tile, f=field: gas_ring[
+                f, tile, 16 + rows.start : 16 + rows.stop, :
+            ],
+        )
 
 
 def corners_kernel(from_north, from_south, core_in, chip_in, core_pack, chip_pack):
@@ -183,63 +193,65 @@
 
 
 def inside_kernel(
-    sampled,
+    gas_in,
     film_hbm,
     flags_hbm,
     deposit_hbm,
     from_north,
     from_south,
     ring,
+    spray,
+    seam,
     force,
-    seam,
-    gas_ring,
     attached,
-    film,
     flags,
-    deposit,
     sems,
 ):
-    pairs = (
-        (flags_hbm, flags),
-        (film_hbm, film),
-        (deposit_hbm, deposit),
-    )
-    copies = [
-        pltpu.make_async_copy(source, target, sems.at[index])
-        for index, (source, target) in enumerate(pairs)
-    ]
-    for copy in copies:
-        copy.start()
-    for copy in copies:
-        copy.wait()
+    del gas_in
+    tiles = [slice(tile * LANES, (tile + 1) * LANES) for tile in range(TILES)]
     inner = slice(8, 8 + ROWS)
+    flags_copy = pltpu.make_async_copy(flags_hbm, flags, sems.at[5, 0])
+    flags_copy.start()
+    arriving = {}
+    for field in (3, 0, 1, 2, 4):
+        arriving[field] = []
+        for tile, cols in enumerate(tiles):
+            if field < 4:
+                source, target = film_hbm.at[field, :, cols], ring.at[field, tile, inner]
+            else:
+                source, target = deposit_hbm.at[:, cols], spray.at[tile, inner]
+            copy = pltpu.make_async_copy(source, target, sems.at[field, tile])
+            copy.start()
+            arriving[field].append(copy)
+
+    refs = [ring.at[f] for f in range(4)]
+    refs += [force.at[f, :, pl.ds(AHEAD, RING)] for f in range(3)]
+    refs += [spray, attached]
+    for field, ref in enumerate(refs):
+        target = slice(4 * field, 4 * field + 4)
+        for tile, cols in enumerate(tiles):
+            ref[tile, 4:8, :] = from_north[target, cols]
+            ref[tile, 8 + ROWS : 12 + ROWS, :] = from_south[target, cols]
+    flags_copy.wait()
     columns = flag_columns(flags[...])
-    refs = [ring.at[f] for f in range(4)] + [gas_ring.at[f] for f in range(3)]
-    refs += [force.at[3], attached]
-    for field in range(FIELDS):
-        ref = refs[field]
-        for tile in range(TILES):
-            cols = slice(tile * LANES, (tile + 1) * LANES)
-            if field < 4:
-                ref[tile, inner, :] = film[field, :, cols]
-            elif field < 7:
-                ref[tile, inner, :] = sampled[field - 4, :, cols]
-            elif field == 7:
-                ref[tile, inner, :] = deposit[:, cols]
-            else:
-                ref[tile, inner, :] = attached_rows(columns, slice(0, ROWS), tile)
-            ref[tile, 4:8, :] = from_north[4 * field : 4 * field + 4, cols]
-            ref[tile, 8 + ROWS : 12 + ROWS, :] = from_south[
-                4 * field : 4 * field + 4, cols
-            ]
+    for tile in range(TILES):
+        attached[tile, inner, :] = attached_rows(columns, slice(0, ROWS), tile)
     every = slice(4, 12 + ROWS)
     lane = lane_iota((ROWS + 8, LANES))
-    for index, ref in enumerate(refs[4:7] + [refs[3], attached]):
-        seam[index, every, :] = jnp.where(
-            lane < LANES // 4,
-            ref[0, every, :],
-            pltpu.roll(ref[TILES - 1, every, :], LANES // 2, 1),
-        )
+
+    def ends(ref, shift):
+        first, last = ref[0, every, :], ref[TILES - 1, every, :]
+        first = pltpu.roll(first, shift, 1) if shift else first
+        last = pltpu.roll(last, LANES // 2 + shift, 1)
+        return jnp.where(lane < shift + LANES // 4, first, last)
+
+    for index in range(2):
+        left = ends(refs[4 + 2 * index], 0)
+        right = ends(refs[5] if index == 0 else attached, LANES // 4)
+        inside = (lane < 8) | ((lane >= 48) & (lane < 72))
+        seam[index, every, :] = jnp.where(inside, left, right)
+    for copy in arriving[3]:
+        copy.wait()
 
     def forcing_rows(index, carry):
         row = 4 + 8 * index
@@ -247,9 +259,9 @@
         filtered = []
         for field in range(3):
             summed = [
-                gas_ring[field, t, pl.ds(row - 1, STRIP), :]
-                + gas_ring[field, t, here, :]
-                + gas_ring[field, t, pl.ds(row + 1, STRIP), :]
+                force[field, t, pl.ds(row + AHEAD - 1, STRIP), :]
+                + force[field, t, pl.ds(row + AHEAD, STRIP), :]
+                + force[field, t, pl.ds(row + AHEAD + 1, STRIP), :]
                 for t in range(TILES)
             ]
             west, east = shifted_lanes(summed)
@@ -266,14 +278,18 @@
                 force[field, t, here, :] = result[field]
         return carry
 
-    grouped(3, 18, forcing_rows, 0)
+    grouped(4, 17, forcing_rows, 0)
+    for field in (0, 1, 2, 4):
+        for copy in arriving[field]:
+            copy.wait()
 
 
 def film_kernel(
     owner_map,
     ring,
+    spray,
+    seam_in,
     force_in,
-    seam_in,
     core_pack,
     chip_pack,
     peaks,
@@ -304,11 +320,25 @@
             force[3, TILES, every, :] = step * value
         else:
             halo[field, every, :] = value
+    film_ends = jnp.where(
+        lane < LANES // 4,
+        ring[3, 0, every, :],
+        pltpu.roll(ring[3, TILES - 1, every, :], LANES // 2, 1),
+    )
+    first, second = seam_in[0, every, :], seam_in[1, every, :]
+    quarter = LANES - LANES // 4
+    own = (
+        first,
+        pltpu.roll(first, quarter, 1),
+        second,
+        film_ends,
+        pltpu.roll(second, quarter, 1),
+    )
     for index, field in enumerate((4, 5, 6, 3, 8)):
         east = pltpu.roll(east_side, (LANES // 2 - 4 * field) % LANES, 1)
         west = pltpu.roll(west_side, (LANES - 4 - 4 * field) % LANES, 1)
         value = jnp.where(
-            (lane >= LANES // 2) & (lane < LANES // 2 + 4), east, seam_in[index, every, :]
+            (lane >= LANES // 2) & (lane < LANES // 2 + 4), east, own[index]
         )
         seam[index, every, :] = jnp.where(lane >= LANES - 4, west, value)
 
@@ -338,10 +368,10 @@
                     value = jnp.where(lanes == LANES - 1, last, value)
                 force[field, t, here, :] = value
         for t in range(TILES):
-            force[3, t, here, :] = step * force_in[3, t, here, :]
+            force[3, t, here, :] = step * spray[t, here, :]
         return carry
 
-    grouped(6, 18, seam_rows, 0)
+    grouped(6, 17, seam_rows, 0)
 
     half = 0.5 * step
 
@@ -400,7 +430,7 @@
                     target[field, t, pl.ds(row, STRIP), :] = news[t][field]
             return carry
 
-        grouped(6, 18, body, 0)
+        grouped(6, 17, body, 0)
 
     def first_load(field, t, rows):
         return ring[field, t, rows, :] if t < TILES else halo[field, rows, :]
@@ -473,10 +503,10 @@
     params = pltpu.CompilerParams(vmem_limit_bytes=VMEM_LIMIT)
     tail = pltpu.CompilerParams(vmem_limit_bytes=8 << 20)
     flags = jnp.transpose(wall_flags)
-    sampled, to_north, to_south, core_main, chip_main, peak = pl.pallas_call(
+    gas_ring, to_north, to_south, core_main, chip_main, peak = pl.pallas_call(
         edges_kernel,
         out_shape=(
-            shape(3, ROWS, COLS),
+            shape(3, TILES, RING + AHEAD, LANES),
             shape(4 * FIELDS, COLS),
             shape(4 * FIELDS, COLS),
             shape(ROWS + 8, LANES),
@@ -517,30 +547,33 @@
     chip_pack = lax.ppermute(chip_pack, "gas", outer)
 
     inner = (4, TILES, RING, LANES)
-    ring, force, seam = pl.pallas_call(
+    ring, spray, seam, force = pl.pallas_call(
         inside_kernel,
-        out_shape=(shape(*inner), shape(*inner), shape(5, RING, LANES)),
+        out_shape=(
+            shape(*inner),
+            shape(*inner[1:]),
+            shape(2, RING, LANES),
+            shape(3, TILES, RING + AHEAD, LANES),
+        ),
         in_specs=vmem(1) + [pl.BlockSpec(memory_space=pltpu.HBM)] * 3 + vmem(2),
-        out_specs=tuple(vmem(3)),
+        out_specs=tuple(vmem(4)),
+        input_output_aliases={0: 3},
         scratch_shapes=[
-            pltpu.VMEM((3,) + inner[1:], jnp.float32),
             pltpu.VMEM(inner[1:], jnp.float32),
-            pltpu.VMEM((4, ROWS, COLS), jnp.float32),
             pltpu.VMEM((TILES, ROWS), jnp.int32),
-            pltpu.VMEM((ROWS, COLS), jnp.float32),
-            pltpu.SemaphoreType.DMA((3,)),
+            pltpu.SemaphoreType.DMA((6, TILES)),
         ],
         compiler_params=pltpu.CompilerParams(vmem_limit_bytes=24 << 20),
         cost_estimate=pl.CostEstimate(
             flops=20 << 20, bytes_accessed=8 << 20, transcendentals=1 << 19
         ),
         name="inside",
-    )(sampled, *in_hbm(film_state, flags, deposit), from_north, from_south)
+    )(gas_ring, *in_hbm(film_state, flags, deposit), from_north, from_south)
     outer_ring = (4, TILES + 1, RING, LANES)
     pieces = pl.pallas_call(
         film_kernel,
         out_shape=shape(gases, 4 * TILES + 1, STRIP, LANES),
-        in_specs=[pl.BlockSpec(memory_space=pltpu.SMEM)] + vmem(6),
+        in_specs=[pl.BlockSpec(memory_space=pltpu.SMEM)] + vmem(7),
         out_specs=vmem(1)[0],
         scratch_shapes=[
             pltpu.VMEM((4, RING, LANES), jnp.float32),
@@ -551,7 +584,7 @@
         ],
         compiler_params=pltpu.CompilerParams(vmem_limit_bytes=24 << 20),
         name="film",
-    )(owner_map, ring, force, seam, core_pack, chip_pack, peaks)
+    )(owner_map, ring, spray, seam, force, core_pack, chip_pack, peaks)
     pieces = lax.all_to_all(pieces, "gas", split_axis=0, concat_axis=0, tiled=True)
     band_peak = pl.pallas_call(
         band_peak_kernel,

time: 74 us -> 71.5 us (0.966)
  Pallas kernels: 15.7 us -> 13.6 us
  local copies, waits for them, and re-layouts: 1.73 us -> 0.01 us
  waiting for transfers between devices: 11.3 us -> 12.5 us
    unnamed x6 -> x2, local copies, waits for them, and re-layouts: 1.73 us -> 0.01 us
    all_to_all x1, waiting for transfers between devices: 5.77 us -> 7.06 us  [coupling_step(): peaks = lax.all_to_all(peak, both, split_axis=0, concat_axis=0, tiled=True)]
    pallas_call x2, Pallas kernels: 6.38 us -> 5.47 us  [the longest x1 3.14 us: coupling_step(): pl.pallas_call(edges_kernel, out_shape=(shape(3, TILES, RING + AHEAD, LAN...]
  transfers between devices with their start and end apart: 6 -> 6, of which waited for: 3 -> 3; matrix products, arithmetic and copies ran while one was open for 0% -> 0% of each run, Pallas kernels for 6% -> 5%
where the time goes in v4:
time: 71.5 us; the launch traced here: 71.1 us
  blocking collectives  22.6 us (32%)
  starting transfers between devices  21 us (29%)
  Pallas kernels  13.6 us (19%)
  waiting for transfers between devices  12.5 us (17%)
    all_to_all x1, blocking collectives, coupling_step(): lax.all_to_all(pieces, 'gas', split_axis=0, concat_axis=0, tiled=True)  22.6 us
    all_to_all x1, starting transfers between devices, coupling_step(): peaks = lax.all_to_all(peak, both, split_axis=0, concat_axis=0, tiled=True)  8.03 us
    all_to_all x1, waiting for transfers between devices, coupling_step(): peaks = lax.all_to_all(peak, both, split_axis=0, concat_axis=0, tiled=True)  7.06 us
    pallas_call x1, Pallas kernels, coupling_step(): pl.pallas_call(film_kernel, out_shape=shape(gases, 4 * TILES + 1, STRIP,...  5.89 us
    all_to_all x1, waiting for transfers between devices, coupling_step(): lax.all_to_all(band_peak, 'wall', split_axis=0, concat_axis=0, tiled=True)  3.41 us
    ppermute x1, starting transfers between devices, coupling_step(): chip_pack = lax.ppermute(chip_pack, 'gas', outer)  3.31 us
    all_to_all x1, starting transfers between devices, coupling_step(): lax.all_to_all(band_peak, 'wall', split_axis=0, concat_axis=0, tiled=True)  3.31 us
    pallas_call x1, Pallas kernels, coupling_step(): pl.pallas_call(edges_kernel, out_shape=(shape(3, TILES, RING + AHEAD, LAN...  3.14 us
  transfers between devices with their start and end apart: 6, of which 3 were waited for; matrix products, arithmetic and copies ran while one was open for 0% of the time, Pallas kernels for 5%

profile of v4, /device:TPU:1, one launch (start us, length us, event | category | flops | bytes accessed | tf_op | source)
XLA Modules:
  0.0 71.1 jit_solution(6303853047266076684)
XLA Ops:
  0.6 3.1 %edges.1 = (f32[3,4,152,128]{3,2,1,0:T(8,128)S(1)}, f32[36,512]{1,0:T(8,128)S(1)}, f32[36,512]{1,0:T(8,128)S(1)}, f32[136,128]{1,0:T(8,128)S(1)}, f32[136,128]{1,0:T(8,128)S(1)}, /*index=5*/f32[128,128]{1,0:T(8,128)}) custom-call(f32[3,4,128,512]{3,2,1,0:T(8,128)} %gas_hbm.1, s32[4,128]{1,0:T(4,128)} %bitcast.9, f32[4,128,512]{2,1,0:T(8,128)} %film_hbm.3, ...), custom_call_target="tpu_custom_call" | custom-call | tf_op jit(solution)/shard_map/edges/pallas_call | solution.py:506
  3.8 2.2 %collective-permute-start = (f32[36,512]{1,0:T(8,128)S(1)}, f32[36,512]{1,0:T(8,128)S(1)}, u32[]{:S(2)}, u32[]{:S(2)}) collective-permute-start(f32[36,512]{1,0:T(8,128)S(1)} %get-tuple-element.15), channel_id=1, source_target_pairs={{0,16},{16,32},{32,48},{48,64},{64,80},{80,96},{96,112},{112,0},{1... | collective-permute-start | bytes 221192 | tf_op jit(solution)/shard_map/ppermute | solution.py:534
  6.0 2.9 %collective-permute-start.1 = (f32[36,512]{1,0:T(8,128)S(1)}, f32[36,512]{1,0:T(8,128)S(1)}, u32[]{:S(2)}, u32[]{:S(2)}) collective-permute-start(f32[36,512]{1,0:T(8,128)S(1)} %get-tuple-element.16), channel_id=1, source_target_pairs={{16,0},{32,16},{48,32},{64,48},{80,64},{96,80},{112,96},{0,112},{1... | collective-permute-start | bytes 221192 | tf_op jit(solution)/shard_map/ppermute | solution.py:535
  8.8 2.1 %collective-permute-done.from_north = f32[36,512]{1,0:T(8,128)S(1)} collective-permute-done((f32[36,512]{1,0:T(8,128)S(1)}, f32[36,512]{1,0:T(8,128)S(1)}, u32[]{:S(2)}, u32[]{:S(2)}) %collective-permute-start) | collective-permute-done | bytes 73760 | tf_op jit(solution)/shard_map/ppermute | solution.py:534
  10.9 0.0 collective-permute-done.1.from_south
  10.9 0.1 corners.1
  11.0 1.3 %collective-permute-start.2 = (f32[136,128]{1,0:T(8,128)S(1)}, f32[136,128]{1,0:T(8,128)S(1)}, u32[]{:S(2)}, u32[]{:S(2)}) collective-permute-start(f32[136,128]{1,0:T(8,128)S(1)} %get-tuple-element.23), channel_id=1, source_target_pairs={{0,1},{1,0},{2,3},{3,2},{4,5},{5,4},{6,7},{7,6},{8,9},{9,8},{10,11... | collective-permute-start | bytes 208904 | tf_op jit(solution)/shard_map/ppermute | solution.py:546
  12.3 3.3 %collective-permute-start.3 = (f32[136,128]{1,0:T(8,128)S(1)}, f32[136,128]{1,0:T(8,128)S(1)}, u32[]{:S(2)}, u32[]{:S(2)}) collective-permute-start(f32[136,128]{1,0:T(8,128)S(1)} %get-tuple-element.24), channel_id=1, source_target_pairs={{0,15},{1,2},{2,1},{3,4},{4,3},{5,6},{6,5},{7,8},{8,7},{9,10},{10,... | collective-permute-start | bytes 208904 | tf_op jit(solution)/shard_map/ppermute | solution.py:547
  15.7 8.0 %all-to-all-start = ((f32[128,1,128]{2,1,0:T(1,128)}), f32[128,1,128]{2,1,0:T(1,128)S(1)}, u32[]{:S(2)}, u32[]{:S(2)}) async-start(f32[128,1,128]{2,1,0:T(1,128)} %bitcast.2), calls=%async_computation | async-start | bytes 131072 | tf_op jit(solution)/shard_map/all_to_all | solution.py:531
  23.7 0.0 copy-start
  23.7 2.3 %inside.1 = (f32[4,4,144,128]{3,2,1,0:T(8,128)S(1)}, f32[4,144,128]{2,1,0:T(8,128)S(1)}, f32[2,144,128]{2,1,0:T(8,128)S(1)}, f32[3,4,152,128]{3,2,1,0:T(8,128)S(1)}) custom-call(f32[3,4,152,128]{3,2,1,0:T(8,128)S(1)} %get-tuple-element.14.gas_in, f32[4,128,512]{2,1,0:T(8,128)} %film_hbm.3, s32[4,128]{1,0:T(4,128)} %bitcast.10, ...), custom_call_target="tpu_custom_call", output_to_operand_aliasing={{3}: (0, {})} | custom-call | flops 20971520 | bytes 8388608 | tf_op jit(solution)/shard_map/inside/pallas_call | solution.py:550
  26.1 7.1 %all-to-all-done = f32[128,1,128]{2,1,0:T(1,128)S(1)} async-done(((f32[128,1,128]{2,1,0:T(1,128)}), f32[128,1,128]{2,1,0:T(1,128)S(1)}, u32[]{:S(2)}, u32[]{:S(2)}) %all-to-all-start) | async-done | bytes 65568 | tf_op jit(solution)/shard_map/all_to_all | solution.py:531
  33.1 0.0 collective-permute-done.2.core_pack
  33.1 0.0 collective-permute-done.3.chip_pack
  33.1 0.0 copy-done
  33.1 5.9 %film.1 = f32[16,17,8,128]{3,2,1,0:T(8,128)S(1)} custom-call(s32[8,16]{1,0:T(8,128)S(1)} %copy-done, f32[4,4,144,128]{3,2,1,0:T(8,128)S(1)} %get-tuple-element.17.ring, f32[4,144,128]{2,1,0:T(8,128)S(1)} %get-tuple-element.18.spray, f32[2,144,128]{2,1,0:T(8,128)S(1)} %get-tuple-element.19.seam_in, f32[3,4,152,128]{3,2,1,0:T(8,128)S(1)} %get-tuple-element.20.force_in, ...), custom_call_target="tpu_custom_call" | custom-call | tf_op jit(solution)/shard_map/film/pallas_call | solution.py:573
  39.0 22.6 %all_to_all.25.pieces = f32[16,17,8,128]{3,2,1,0:T(8,128)S(1)} all-to-all(f32[16,17,8,128]{3,2,1,0:T(8,128)S(1)} %film.1), channel_id=1, replica_groups=mesh['wall'=8,'gas'=16] {'gas'}, dimensions={0} | all-to-all | bytes 2228224 | tf_op jit(solution)/shard_map/all_to_all | solution.py:588
  61.6 0.6 band_peak.1
  62.2 3.3 %all-to-all-start.2 = ((f32[8,1,128]{2,1,0:T(1,128)}), f32[8,1,128]{2,1,0:T(1,128)S(1)}, u32[]{:S(2)}, u32[]{:S(2)}) async-start(f32[8,1,128]{2,1,0:T(1,128)} %bitcast.5), calls=%async_computation.2 | async-start | bytes 8192 | tf_op jit(solution)/shard_map/all_to_all | solution.py:598
  65.5 1.5 %strips.1 = f32[4,8,8192]{2,1,0:T(8,128)} custom-call(f32[16,17,8,128]{3,2,1,0:T(8,128)S(1)} %all_to_all.25.pieces), custom_call_target="tpu_custom_call" | custom-call | bytes 2097152 | tf_op jit(solution)/shard_map/strips/pallas_call | solution.py:600
  67.1 3.4 %all-to-all-done.2 = f32[8,1,128]{2,1,0:T(1,128)S(1)} async-done(((f32[8,1,128]{2,1,0:T(1,128)}), f32[8,1,128]{2,1,0:T(1,128)S(1)}, u32[]{:S(2)}, u32[]{:S(2)}) %all-to-all-start.2) | async-done | bytes 4128 | tf_op jit(solution)/shard_map/all_to_all | solution.py:598
  70.5 0.6 reduce_max.9
Async XLA Ops:
  3.8 7.1 %collective-permute-start = (f32[36,512]{1,0:T(8,128)S(1)}, f32[36,512]{1,0:T(8,128)S(1)}, u32[]{:S(2)}, u32[]{:S(2)}) collective-permute-start(f32[36,512]{1,0:T(8,128)S(1)} %get-tuple-element.15), channel_id=1, source_target_pairs={{0,16},{16,32},{32,48},{48,64},{64,80},{80,96},{96,112},{112,0},{1... | collective-permute-start | bytes 221192 | tf_op jit(solution)/shard_map/ppermute | solution.py:534
  6.0 4.9 %collective-permute-start.1 = (f32[36,512]{1,0:T(8,128)S(1)}, f32[36,512]{1,0:T(8,128)S(1)}, u32[]{:S(2)}, u32[]{:S(2)}) collective-permute-start(f32[36,512]{1,0:T(8,128)S(1)} %get-tuple-element.16), channel_id=1, source_target_pairs={{16,0},{32,16},{48,32},{64,48},{80,64},{96,80},{112,96},{0,112},{1... | collective-permute-start | bytes 221192 | tf_op jit(solution)/shard_map/ppermute | solution.py:535
  11.0 22.1 %collective-permute-start.2 = (f32[136,128]{1,0:T(8,128)S(1)}, f32[136,128]{1,0:T(8,128)S(1)}, u32[]{:S(2)}, u32[]{:S(2)}) collective-permute-start(f32[136,128]{1,0:T(8,128)S(1)} %get-tuple-element.23), channel_id=1, source_target_pairs={{0,1},{1,0},{2,3},{3,2},{4,5},{5,4},{6,7},{7,6},{8,9},{9,8},{10,11... | collective-permute-start | bytes 208904 | tf_op jit(solution)/shard_map/ppermute | solution.py:546
  12.3 20.8 %collective-permute-start.3 = (f32[136,128]{1,0:T(8,128)S(1)}, f32[136,128]{1,0:T(8,128)S(1)}, u32[]{:S(2)}, u32[]{:S(2)}) collective-permute-start(f32[136,128]{1,0:T(8,128)S(1)} %get-tuple-element.24), channel_id=1, source_target_pairs={{0,15},{1,2},{2,1},{3,4},{4,3},{5,6},{6,5},{7,8},{8,7},{9,10},{10,... | collective-permute-start | bytes 208904 | tf_op jit(solution)/shard_map/ppermute | solution.py:547
  15.7 17.5 %all-to-all-start = ((f32[128,1,128]{2,1,0:T(1,128)}), f32[128,1,128]{2,1,0:T(1,128)S(1)}, u32[]{:S(2)}, u32[]{:S(2)}) async-start(f32[128,1,128]{2,1,0:T(1,128)} %bitcast.2), calls=%async_computation | async-start | bytes 131072 | tf_op jit(solution)/shard_map/all_to_all | solution.py:531
  23.7 9.4 %copy-start = (s32[8,16]{1,0:T(8,128)S(1)}, s32[8,16]{1,0:T(8,128)}, u32[]{:S(2)}) copy-start(s32[8,16]{1,0:T(8,128)} %owner_map.1) | copy-start | bytes 1540
  62.2 8.3 %all-to-all-start.2 = ((f32[8,1,128]{2,1,0:T(1,128)}), f32[8,1,128]{2,1,0:T(1,128)S(1)}, u32[]{:S(2)}, u32[]{:S(2)}) async-start(f32[8,1,128]{2,1,0:T(1,128)} %bitcast.5), calls=%async_computation.2 | async-start | bytes 8192 | tf_op jit(solution)/shard_map/all_to_all | solution.py:598

commit v5 on v4

--- a/solution.py
+++ b/solution.py
@@ -26,6 +26,7 @@
 FIELDS = 9
 STRIP = 8
 RING = ROWS + 16
+WIDE = COLS + LANES
 AHEAD = 8
 VMEM_LIMIT = 24 << 20
 
@@ -41,16 +42,18 @@
     return moving / thickness + jnp.sqrt(thickness)
 
 
-def pack_columns(rows_of, count, left):
-    lane = lane_iota((count, LANES))
-    packed = jnp.zeros((count, LANES), jnp.float32)
-    for field in range(FIELDS):
-        shift = (4 * field) if left else (4 * field + 4)
-        value = rows_of(field)
-        if shift:
-            value = pltpu.roll(value, shift, 1)
-        packed = jnp.where((lane >= 4 * field) & (lane < 4 * field + 4), value, packed)
-    return packed
+def halo_tile(east, west, field):
+    lane = lane_iota(east.shape)
+    return jnp.where(
+        lane < LANES // 2,
+        pltpu.roll(east, (LANES - 4 * field) % LANES, 1),
+        pltpu.roll(west, (LANES - 4 - 4 * field) % LANES, 1),
+    )
+
+
+def sides(core, chip):
+    even = lax.rem(lax.axis_index("gas"), 2) == 0
+    return jnp.where(even, core, chip), jnp.where(even, chip, core)
 
 
 def sample(gas, field, rows, cols):
@@ -117,8 +120,8 @@
             (core_pack, jnp.where(even, east, west)),
             (chip_pack, jnp.where(even, west, east)),
         ):
-            old = pack[4 : 4 + ROWS, :] if field else jnp.zeros_like(value)
-            pack[4 : 4 + ROWS, :] = jnp.where(here, value, old)
+            old = pack[...] if field else jnp.zeros_like(value)
+            pack[...] = jnp.where(here, value, old)
 
     copies[0].wait()
     best = jnp.zeros((STRIP, LANES), jnp.float32)
@@ -137,26 +140,26 @@
     for field in range(3):
         copies[3 + field].wait()
         for tile, cols in enumerate(tiles):
-            gas_ring[field, tile, 16 : 16 + ROWS, :] = sample(gas, field, every, cols)
+            gas_ring[field, tile, AHEAD : AHEAD + ROWS, :] = sample(gas, field, every, cols)
         send(
             4 + field,
             lambda rows, tile, f=field: gas_ring[
-                f, tile, 16 + rows.start : 16 + rows.stop, :
+                f, tile, AHEAD + rows.start : AHEAD + rows.stop, :
             ],
         )
 
 
-def corners_kernel(from_north, from_south, core_in, chip_in, core_pack, chip_pack):
-    even = lax.rem(lax.axis_index("gas"), 2) == 0
-    core_pack[4 : 4 + ROWS, :] = core_in[4 : 4 + ROWS, :]
-    chip_pack[4 : 4 + ROWS, :] = chip_in[4 : 4 + ROWS, :]
-    for source, start in ((from_north, 0), (from_south, 4 + ROWS)):
-        west = pack_columns(lambda f: source[4 * f : 4 * f + 4, 0:LANES], 4, True)
-        east = pack_columns(
-            lambda f: source[4 * f : 4 * f + 4, COLS - LANES : COLS], 4, False
-        )
-        core_pack[start : start + 4, :] = jnp.where(even, east, west)
-        chip_pack[start : start + 4, :] = jnp.where(even, west, east)
+def corners_kernel(core, chip, north_in, south_in, to_north, to_south):
+    for rows, source, target in (
+        (slice(0, 8), north_in, to_north),
+        (slice(ROWS - 8, ROWS), south_in, to_south),
+    ):
+        target[:, 0:COLS] = source[:, 0:COLS]
+        east, west = sides(core[rows, :], chip[rows, :])
+        for field in range(FIELDS):
+            value = halo_tile(east, west, field)
+            value = value[0:4] if rows.start == 0 else value[4:8]
+            target[4 * field : 4 * field + 4, COLS:WIDE] = value
 
 
 def shifted_lanes(tiles):
@@ -197,64 +200,49 @@
     film_hbm,
     flags_hbm,
     deposit_hbm,
-    from_north,
-    from_south,
+    core,
+    chip,
     ring,
     spray,
-    seam,
     force,
     attached,
     flags,
     sems,
 ):
     del gas_in
-    tiles = [slice(tile * LANES, (tile + 1) * LANES) for tile in range(TILES)]
+    count = TILES + 1
     inner = slice(8, 8 + ROWS)
     flags_copy = pltpu.make_async_copy(flags_hbm, flags, sems.at[5, 0])
     flags_copy.start()
     arriving = {}
     for field in (3, 0, 1, 2, 4):
         arriving[field] = []
-        for tile, cols in enumerate(tiles):
+        for tile in range(TILES):
+            cols = slice(tile * LANES, (tile + 1) * LANES)
             if field < 4:
                 source, target = film_hbm.at[field, :, cols], ring.at[field, tile, inner]
             else:
-                source, target = deposit_hbm.at[:, cols], spray.at[tile, inner]
+                source, target = deposit_hbm.at[:, cols], spray.at[tile]
             copy = pltpu.make_async_copy(source, target, sems.at[field, tile])
             copy.start()
             arriving[field].append(copy)
 
-    refs = [ring.at[f] for f in range(4)]
-    refs += [force.at[f, :, pl.ds(AHEAD, RING)] for f in range(3)]
-    refs += [spray, attached]
-    for field, ref in enumerate(refs):
-        target = slice(4 * field, 4 * field + 4)
-        for tile, cols in enumerate(tiles):
-            ref[tile, 4:8, :] = from_north[target, cols]
-            ref[tile, 8 + ROWS : 12 + ROWS, :] = from_south[target, cols]
+    east, west = sides(core[...], chip[...])
+    for field in range(4):
+        ring[field, TILES, inner, :] = halo_tile(east, west, field)
+    for field in range(3):
+        force[field, TILES, AHEAD : AHEAD + ROWS, :] = halo_tile(east, west, 4 + field)
+    spray[TILES] = halo_tile(east, west, 7)
+    attached[TILES, 0:ROWS, :] = halo_tile(east, west, 8)
     flags_copy.wait()
     columns = flag_columns(flags[...])
     for tile in range(TILES):
-        attached[tile, inner, :] = attached_rows(columns, slice(0, ROWS), tile)
-    every = slice(4, 12 + ROWS)
-    lane = lane_iota((ROWS + 8, LANES))
-
-    def ends(ref, shift):
-        first, last = ref[0, every, :], ref[TILES - 1, every, :]
-        first = pltpu.roll(first, shift, 1) if shift else first
-        last = pltpu.roll(last, LANES // 2 + shift, 1)
-        return jnp.where(lane < shift + LANES // 4, first, last)
-
-    for index in range(2):
-        left = ends(refs[4 + 2 * index], 0)
-        right = ends(refs[5] if index == 0 else attached, LANES // 4)
-        inside = (lane < 8) | ((lane >= 48) & (lane < 72))
-        seam[index, every, :] = jnp.where(inside, left, right)
+        attached[tile, 0:ROWS, :] = attached_rows(columns, slice(0, ROWS), tile)
     for copy in arriving[3]:
         copy.wait()
 
     def forcing_rows(index, carry):
-        row = 4 + 8 * index
+        row = 1 + 8 * index
         here = pl.ds(row, STRIP)
         filtered = []
         for field in range(3):
@@ -262,23 +250,23 @@
                 force[field, t, pl.ds(row + AHEAD - 1, STRIP), :]
                 + force[field, t, pl.ds(row + AHEAD, STRIP), :]
                 + force[field, t, pl.ds(row + AHEAD + 1, STRIP), :]
-                for t in range(TILES)
+                for t in range(count)
             ]
             west, east = shifted_lanes(summed)
             filtered.append(
-                [(west[t] + summed[t] + east[t]) * (1.0 / 9.0) for t in range(TILES)]
+                [(west[t] + summed[t] + east[t]) * (1.0 / 9.0) for t in range(count)]
             )
-        for t in range(TILES):
+        for t in range(count):
             result = wall_forcing(
                 [filtered[f][t] for f in range(3)],
-                ring[3, t, here, :],
+                ring[3, t, pl.ds(row + 8, STRIP), :],
                 attached[t, here, :],
             )
             for field in range(3):
                 force[field, t, here, :] = result[field]
         return carry
 
-    grouped(4, 17, forcing_rows, 0)
+    grouped(4, 16, forcing_rows, 0)
     for field in (0, 1, 2, 4):
         for copy in arriving[field]:
             copy.wait()
@@ -286,92 +274,76 @@
 
 def film_kernel(
     owner_map,
-    ring,
+    ring_in,
     spray,
-    seam_in,
     force_in,
-    core_pack,
-    chip_pack,
+    to_north,
+    to_south,
+    from_north,
+    from_south,
     peaks,
     out,
-    halo,
-    seam,
+    ring,
+    stack,
     ring_a,
     ring_b,
     force,
 ):
+    del ring_in
     count = TILES + 1
-    even = lax.rem(lax.axis_index("gas"), 2) == 0
     wall = lax.axis_index("wall")
     step = COURANT / jnp.max(peaks[...])
-
-    every = slice(4, 12 + ROWS)
-    lane = lane_iota((ROWS + 8, LANES))
-    core, chip = core_pack[...], chip_pack[...]
-    east_side = jnp.where(even, core, chip)
-    west_side = jnp.where(even, chip, core)
-    for field in (0, 1, 2, 3, 7):
-        value = jnp.where(
-            lane < LANES // 2,
-            pltpu.roll(east_side, (LANES - 4 * field) % LANES, 1),
-            pltpu.roll(west_side, (LANES - 4 - 4 * field) % LANES, 1),
-        )
-        if field == 7:
-            force[3, TILES, every, :] = step * value
-        else:
-            halo[field, every, :] = value
-    film_ends = jnp.where(
-        lane < LANES // 4,
-        ring[3, 0, every, :],
-        pltpu.roll(ring[3, TILES - 1, every, :], LANES // 2, 1),
-    )
-    first, second = seam_in[0, every, :], seam_in[1, every, :]
-    quarter = LANES - LANES // 4
-    own = (
-        first,
-        pltpu.roll(first, quarter, 1),
-        second,
-        film_ends,
-        pltpu.roll(second, quarter, 1),
-    )
-    for index, field in enumerate((4, 5, 6, 3, 8)):
-        east = pltpu.roll(east_side, (LANES // 2 - 4 * field) % LANES, 1)
-        west = pltpu.roll(west_side, (LANES - 4 - 4 * field) % LANES, 1)
-        value = jnp.where(
-            (lane >= LANES // 2) & (lane < LANES // 2 + 4), east, own[index]
-        )
-        seam[index, every, :] = jnp.where(lane >= LANES - 4, west, value)
-
-    def seam_rows(index, carry):
-        row = 4 + 8 * index
-        here = pl.ds(row, STRIP)
-        lanes = lane_iota((STRIP, LANES))
+    inner = slice(8, 8 + ROWS)
+    above, below = slice(4, 8), slice(8 + ROWS, 12 + ROWS)
+
+    for tile in range(count):
+        cols = slice(tile * LANES, (tile + 1) * LANES)
+        for field in range(4):
+            source = slice(4 * field, 4 * field + 4)
+            ring[field, tile, above, :] = from_north[source, cols]
+            ring[field, tile, below, :] = from_south[source, cols]
+        force[3, tile, above, :] = step * from_north[28:32, cols]
+        force[3, tile, inner, :] = step * spray[tile]
+        force[3, tile, below, :] = step * from_south[28:32, cols]
+        for index, field in enumerate((4, 5, 6, 3, 8)):
+            source = slice(4 * field, 4 * field + 4)
+            stack[index, tile, 0:4, :] = from_north[source, cols]
+            stack[index, tile, 4:8, :] = to_north[source, cols]
+            stack[index, tile, 8:12, :] = to_south[source, cols]
+            stack[index, tile, 12:16, :] = from_south[source, cols]
+
+    def scale_rows(index, carry):
+        row = 1 + 8 * index
+        for field in range(3):
+            for t in range(count):
+                force[field, t, pl.ds(row + 8, STRIP), :] = (
+                    step * force_in[field, t, pl.ds(row, STRIP), :]
+                )
+        return carry
+
+    grouped(4, 16, scale_rows, 0)
+    for start, first, target in ((1, 0, 5), (8, 3, 135)):
         filtered = []
         for field in range(3):
-            summed = (
-                seam[field, pl.ds(row - 1, STRIP), :]
-                + seam[field, here, :]
-                + seam[field, pl.ds(row + 1, STRIP), :]
+            summed = [
+                stack[field, t, start - 1 : start - 1 + STRIP, :]
+                + stack[field, t, start : start + STRIP, :]
+                + stack[field, t, start + 1 : start + 1 + STRIP, :]
+                for t in range(count)
+            ]
+            west, east = shifted_lanes(summed)
+            filtered.append(
+                [(west[t] + summed[t] + east[t]) * (1.0 / 9.0) for t in range(count)]
             )
-            west, east = pltpu.roll(summed, 1, 1), pltpu.roll(summed, LANES - 1, 1)
-            filtered.append((west + summed + east) * (1.0 / 9.0))
-        result = wall_forcing(filtered, seam[3, here, :], seam[4, here, :])
-        for field in range(3):
-            first = step * result[field]
-            last = pltpu.roll(first, LANES // 2, 1)
-            force[field, TILES, here, :] = jnp.where(lanes < LANES // 2, last, first)
-            for t in range(TILES):
-                value = step * force_in[field, t, here, :]
-                if t == 0:
-                    value = jnp.where(lanes == 0, first, value)
-                if t == TILES - 1:
-                    value = jnp.where(lanes == LANES - 1, last, value)
-                force[field, t, here, :] = value
-        for t in range(TILES):
-            force[3, t, here, :] = step * spray[t, here, :]
-        return carry
-
-    grouped(6, 17, seam_rows, 0)
+        for t in range(count):
+            rows = slice(start, start + STRIP)
+            result = wall_forcing(
+                [filtered[f][t] for f in range(3)], stack[3, t, rows, :], stack[4, t, rows, :]
+            )
+            for field in range(3):
+                force[field, t, target : target + 4, :] = (
+                    step * result[field][first : first + 4]
+                )
 
     half = 0.5 * step
 
@@ -432,13 +404,10 @@
 
         grouped(6, 17, body, 0)
 
-    def first_load(field, t, rows):
-        return ring[field, t, rows, :] if t < TILES else halo[field, rows, :]
-
     def load_from(source):
         return lambda field, t, rows: source[field, t, rows, :]
 
-    middle_rows(first_load, ring_a)
+    middle_rows(load_from(ring), ring_a)
     middle_rows(load_from(ring_a), ring_b)
     middle_rows(load_from(ring_b), ring_a)
 
@@ -503,14 +472,14 @@
     params = pltpu.CompilerParams(vmem_limit_bytes=VMEM_LIMIT)
     tail = pltpu.CompilerParams(vmem_limit_bytes=8 << 20)
     flags = jnp.transpose(wall_flags)
-    gas_ring, to_north, to_south, core_main, chip_main, peak = pl.pallas_call(
+    gas_ring, north_main, south_main, core_pack, chip_pack, peak = pl.pallas_call(
         edges_kernel,
         out_shape=(
-            shape(3, TILES, RING + AHEAD, LANES),
-            shape(4 * FIELDS, COLS),
-            shape(4 * FIELDS, COLS),
-            shape(ROWS + 8, LANES),
-            shape(ROWS + 8, LANES),
+            shape(3, TILES + 1, RING, LANES),
+            shape(4 * FIELDS, WIDE),
+            shape(4 * FIELDS, WIDE),
+            shape(ROWS, LANES),
+            shape(ROWS, LANES),
             shape(ROWS, LANES),
         ),
         in_specs=[pl.BlockSpec(memory_space=pltpu.HBM)] * 4,
@@ -527,64 +496,72 @@
     )(*in_hbm(gas_state, flags, film_state, deposit))
 
     walls, gases = lax.axis_size("wall"), lax.axis_size("gas")
+    partner = [(i, i ^ 1) for i in range(gases)]
+    outer = [(i, (i + 1) % gases if i % 2 else (i - 1) % gases) for i in range(gases)]
+    chip_side = lax.ppermute(chip_pack, "gas", outer)
+    core_side = lax.ppermute(core_pack, "gas", partner)
     both = ("wall", "gas")
     peaks = lax.all_to_all(peak, both, split_axis=0, concat_axis=0, tiled=True)
+    to_north, to_south = pl.pallas_call(
+        corners_kernel,
+        out_shape=(shape(4 * FIELDS, WIDE), shape(4 * FIELDS, WIDE)),
+        in_specs=vmem(4),
+        out_specs=tuple(vmem(2)),
+        compiler_params=params,
+        name="corners",
+    )(core_side, chip_side, north_main, south_main)
     down = [(i, (i + 1) % walls) for i in range(walls)]
     up = [(j, i) for i, j in down]
     from_north = lax.ppermute(to_south, "wall", down)
     from_south = lax.ppermute(to_north, "wall", up)
-    core_pack, chip_pack = pl.pallas_call(
-        corners_kernel,
-        out_shape=(shape(ROWS + 8, LANES), shape(ROWS + 8, LANES)),
-        in_specs=vmem(4),
-        out_specs=tuple(vmem(2)),
-        compiler_params=params,
-        name="corners",
-    )(from_north, from_south, core_main, chip_main)
-    partner = [(i, i ^ 1) for i in range(gases)]
-    outer = [(i, (i + 1) % gases if i % 2 else (i - 1) % gases) for i in range(gases)]
-    core_pack = lax.ppermute(core_pack, "gas", partner)
-    chip_pack = lax.ppermute(chip_pack, "gas", outer)
-
-    inner = (4, TILES, RING, LANES)
-    ring, spray, seam, force = pl.pallas_call(
+
+    ring_shape = (4, TILES + 1, RING, LANES)
+    ring, spray, force = pl.pallas_call(
         inside_kernel,
         out_shape=(
-            shape(*inner),
-            shape(*inner[1:]),
-            shape(2, RING, LANES),
-            shape(3, TILES, RING + AHEAD, LANES),
+            shape(*ring_shape),
+            shape(TILES + 1, ROWS, LANES),
+            shape(3, *ring_shape[1:]),
         ),
         in_specs=vmem(1) + [pl.BlockSpec(memory_space=pltpu.HBM)] * 3 + vmem(2),
-        out_specs=tuple(vmem(4)),
-        input_output_aliases={0: 3},
+        out_specs=tuple(vmem(3)),
+        input_output_aliases={0: 2},
         scratch_shapes=[
-            pltpu.VMEM(inner[1:], jnp.float32),
+            pltpu.VMEM(ring_shape[1:], jnp.float32),
             pltpu.VMEM((TILES, ROWS), jnp.int32),
             pltpu.SemaphoreType.DMA((6, TILES)),
         ],
-        compiler_params=pltpu.CompilerParams(vmem_limit_bytes=24 << 20),
+        compiler_params=params,
         cost_estimate=pl.CostEstimate(
             flops=20 << 20, bytes_accessed=8 << 20, transcendentals=1 << 19
         ),
         name="inside",
-    )(gas_ring, *in_hbm(film_state, flags, deposit), from_north, from_south)
-    outer_ring = (4, TILES + 1, RING, LANES)
-    pieces = pl.pallas_call(
+    )(gas_ring, *in_hbm(film_state, flags, deposit), core_side, chip_side)
+    pieces, _ = pl.pallas_call(
         film_kernel,
-        out_shape=shape(gases, 4 * TILES + 1, STRIP, LANES),
-        in_specs=[pl.BlockSpec(memory_space=pltpu.SMEM)] + vmem(7),
-        out_specs=vmem(1)[0],
+        out_shape=(shape(gases, 4 * TILES + 1, STRIP, LANES), shape(*ring_shape)),
+        in_specs=[pl.BlockSpec(memory_space=pltpu.SMEM)] + vmem(8),
+        out_specs=tuple(vmem(2)),
+        input_output_aliases={1: 1},
         scratch_shapes=[
-            pltpu.VMEM((4, RING, LANES), jnp.float32),
-            pltpu.VMEM((5, RING, LANES), jnp.float32),
-            pltpu.VMEM(outer_ring, jnp.float32),
-            pltpu.VMEM(outer_ring, jnp.float32),
-            pltpu.VMEM(outer_ring, jnp.float32),
+            pltpu.VMEM((5, TILES + 1, 24, LANES), jnp.float32),
+            pltpu.VMEM(ring_shape, jnp.float32),
+            pltpu.VMEM(ring_shape, jnp.float32),
+            pltpu.VMEM(ring_shape, jnp.float32),
         ],
-        compiler_params=pltpu.CompilerParams(vmem_limit_bytes=24 << 20),
+        compiler_params=params,
         name="film",
-    )(owner_map, ring, spray, seam, force, core_pack, chip_pack, peaks)
+    )(
+        owner_map,
+        ring,
+        spray,
+        force,
+        to_north,
+        to_south,
+        from_north,
+        from_south,
+        peaks,
+    )
     pieces = lax.all_to_all(pieces, "gas", split_axis=0, concat_axis=0, tiled=True)
     band_peak = pl.pallas_call(
         band_peak_kernel,

time: 71.5 us -> 73.2 us (1.024)
  starting transfers between devices: 21 us -> 23.5 us
    all_to_all x1, starting transfers between devices: 8.03 us -> 11.3 us  [coupling_step(): peaks = lax.all_to_all(peak, both, split_axis=0, concat_axis=0, tiled=True)]
    ppermute x1, starting transfers between devices: 2.18 us -> 0.01 us  [coupling_step(): from_north = lax.ppermute(to_south, 'wall', down)]
    ppermute x1, waiting for transfers between devices: 2.07 us -> 0.01 us  [coupling_step(): from_north = lax.ppermute(to_south, 'wall', down)]
    ppermute x2, waiting for transfers between devices: 0.01 us -> 1.95 us  [the longest x1 1.95 us: coupling_step(): chip_side = lax.ppermute(chip_pack, 'gas', outer)]
    ppermute x1, starting transfers between devices: 2.87 us -> 3.83 us  [coupling_step(): from_south = lax.ppermute(to_north, 'wall', up)]
    pallas_call x4, Pallas kernels: 11.5 us -> 10.7 us  [the longest x1 5.21 us: coupling_step(): pl.pallas_call(film_kernel, out_shape=(shape(gases, 4 * TILES + 1, STRIP,...]
where the time goes in v5:
time: 73.2 us; the launch traced here: 72.8 us
  starting transfers between devices  23.5 us (32%)
  blocking collectives  22.6 us (31%)
  Pallas kernels  12.9 us (18%)
  waiting for transfers between devices  12.5 us (17%)
    all_to_all x1, blocking collectives, coupling_step(): lax.all_to_all(pieces, 'gas', split_axis=0, concat_axis=0, tiled=True)  22.6 us
    all_to_all x1, starting transfers between devices, coupling_step(): peaks = lax.all_to_all(peak, both, split_axis=0, concat_axis=0, tiled=True)  11.3 us
    all_to_all x1, waiting for transfers between devices, coupling_step(): peaks = lax.all_to_all(peak, both, split_axis=0, concat_axis=0, tiled=True)  7.15 us
    pallas_call x1, Pallas kernels, coupling_step(): pl.pallas_call(film_kernel, out_shape=(shape(gases, 4 * TILES + 1, STRIP,...  5.21 us
    ppermute x1, starting transfers between devices, coupling_step(): from_south = lax.ppermute(to_north, 'wall', up)  3.83 us
    ppermute x1, starting transfers between devices, coupling_step(): chip_side = lax.ppermute(chip_pack, 'gas', outer)  3.69 us
    all_to_all x1, waiting for transfers between devices, coupling_step(): lax.all_to_all(band_peak, 'wall', split_axis=0, concat_axis=0, tiled=True)  3.41 us
    all_to_all x1, starting transfers between devices, coupling_step(): lax.all_to_all(band_peak, 'wall', split_axis=0, concat_axis=0, tiled=True)  3.28 us
  transfers between devices with their start and end apart: 6, of which 3 were waited for; matrix products, arithmetic and copies ran while one was open for 0% of the time, Pallas kernels for 5%

profile of v5, /device:TPU:1, one launch (start us, length us, event | category | flops | bytes accessed | tf_op | source)
XLA Modules:
  0.0 72.8 jit_solution(16154045984660386694)
XLA Ops:
  0.6 3.1 %edges.1 = (f32[3,5,144,128]{3,2,1,0:T(8,128)S(1)}, f32[36,640]{1,0:T(8,128)S(1)}, f32[36,640]{1,0:T(8,128)S(1)}, f32[128,128]{1,0:T(8,128)S(1)}, f32[128,128]{1,0:T(8,128)S(1)}, /*index=5*/f32[128,128]{1,0:T(8,128)}) custom-call(f32[3,4,128,512]{3,2,1,0:T(8,128)} %gas_hbm.1, s32[4,128]{1,0:T(4,128)} %bitcast.9, f32[4,128,512]{2,1,0:T(8,128)} %film_hbm.3, ...), custom_call_target="tpu_custom_call" | custom-call | tf_op jit(solution)/shard_map/edges/pallas_call | solution.py:475
  3.8 1.5 %collective-permute-start = (f32[128,128]{1,0:T(8,128)S(1)}, f32[128,128]{1,0:T(8,128)S(1)}, u32[]{:S(2)}, u32[]{:S(2)}) collective-permute-start(f32[128,128]{1,0:T(8,128)S(1)} %get-tuple-element.15), channel_id=1, source_target_pairs={{0,1},{1,0},{2,3},{3,2},{4,5},{5,4},{6,7},{7,6},{8,9},{9,8},{10,11... | collective-permute-start | bytes 196616 | tf_op jit(solution)/shard_map/ppermute | solution.py:502
  5.2 3.7 %collective-permute-start.1 = (f32[128,128]{1,0:T(8,128)S(1)}, f32[128,128]{1,0:T(8,128)S(1)}, u32[]{:S(2)}, u32[]{:S(2)}) collective-permute-start(f32[128,128]{1,0:T(8,128)S(1)} %get-tuple-element.16), channel_id=1, source_target_pairs={{0,15},{1,2},{2,1},{3,4},{4,3},{5,6},{6,5},{7,8},{8,7},{9,10},{10,... | collective-permute-start | bytes 196616 | tf_op jit(solution)/shard_map/ppermute | solution.py:501
  8.9 0.0 collective-permute-done.core
  8.9 1.9 %collective-permute-done.1.chip = f32[128,128]{1,0:T(8,128)S(1)} collective-permute-done((f32[128,128]{1,0:T(8,128)S(1)}, f32[128,128]{1,0:T(8,128)S(1)}, u32[]{:S(2)}, u32[]{:S(2)}) %collective-permute-start.1) | collective-permute-done | bytes 65568 | tf_op jit(solution)/shard_map/ppermute | solution.py:501
  10.9 0.1 corners.1
  11.0 3.8 %collective-permute-start.3 = (f32[36,640]{1,0:T(8,128)S(1)}, f32[36,640]{1,0:T(8,128)S(1)}, u32[]{:S(2)}, u32[]{:S(2)}) collective-permute-start(f32[36,640]{1,0:T(8,128)S(1)} %get-tuple-element.22.to_north), channel_id=1, source_target_pairs={{16,0},{32,16},{48,32},{64,48},{80,64},{96,80},{112,96},{0,112},{1... | collective-permute-start | bytes 276488 | tf_op jit(solution)/shard_map/ppermute | solution.py:516
  14.8 0.0 collective-permute-start.2
  14.8 11.3 %all-to-all-start = ((f32[128,1,128]{2,1,0:T(1,128)}), f32[128,1,128]{2,1,0:T(1,128)S(1)}, u32[]{:S(2)}, u32[]{:S(2)}) async-start(f32[128,1,128]{2,1,0:T(1,128)} %bitcast.2), calls=%async_computation | async-start | bytes 131072 | tf_op jit(solution)/shard_map/all_to_all | solution.py:504
  26.1 0.0 copy-start
  26.1 2.2 %inside.1 = (f32[4,5,144,128]{3,2,1,0:T(8,128)S(1)}, f32[5,128,128]{2,1,0:T(8,128)S(1)}, f32[3,5,144,128]{3,2,1,0:T(8,128)S(1)}) custom-call(f32[3,5,144,128]{3,2,1,0:T(8,128)S(1)} %get-tuple-element.14.gas_in, f32[4,128,512]{2,1,0:T(8,128)} %film_hbm.3, s32[4,128]{1,0:T(4,128)} %bitcast.10, ...), custom_call_target="tpu_custom_call", output_to_operand_aliasing={{2}: (0, {})} | custom-call | flops 20971520 | bytes 8388608 | tf_op jit(solution)/shard_map/inside/pallas_call | solution.py:519
  28.4 7.2 %all-to-all-done = f32[128,1,128]{2,1,0:T(1,128)S(1)} async-done(((f32[128,1,128]{2,1,0:T(1,128)}), f32[128,1,128]{2,1,0:T(1,128)S(1)}, u32[]{:S(2)}, u32[]{:S(2)}) %all-to-all-start) | async-done | bytes 65568 | tf_op jit(solution)/shard_map/all_to_all | solution.py:504
  35.5 0.0 collective-permute-done.3.from_south
  35.5 0.0 collective-permute-done.2.from_north
  35.5 0.0 copy-done
  35.5 5.2 %film.1 = (f32[16,17,8,128]{3,2,1,0:T(8,128)S(1)}, f32[4,5,144,128]{3,2,1,0:T(8,128)S(1)}) custom-call(s32[8,16]{1,0:T(8,128)S(1)} %copy-done, f32[4,5,144,128]{3,2,1,0:T(8,128)S(1)} %get-tuple-element.17.ring_in, f32[5,128,128]{2,1,0:T(8,128)S(1)} %get-tuple-element.18.spray, ...), custom_call_target="tpu_custom_call", output_to_operand_aliasing={{1}: (1, {})} | custom-call | tf_op jit(solution)/shard_map/film/pallas_call | solution.py:540
  40.7 22.6 %all_to_all.25.pieces = f32[16,17,8,128]{3,2,1,0:T(8,128)S(1)} all-to-all(f32[16,17,8,128]{3,2,1,0:T(8,128)S(1)} %get-tuple-element.25), channel_id=1, replica_groups=mesh['wall'=8,'gas'=16] {'gas'}, dimensions={0} | all-to-all | bytes 2228224 | tf_op jit(solution)/shard_map/all_to_all | solution.py:565
  63.3 0.6 band_peak.1
  63.9 3.3 %all-to-all-start.2 = ((f32[8,1,128]{2,1,0:T(1,128)}), f32[8,1,128]{2,1,0:T(1,128)S(1)}, u32[]{:S(2)}, u32[]{:S(2)}) async-start(f32[8,1,128]{2,1,0:T(1,128)} %bitcast.5), calls=%async_computation.2 | async-start | bytes 8192 | tf_op jit(solution)/shard_map/all_to_all | solution.py:575
  67.2 1.5 %strips.1 = f32[4,8,8192]{2,1,0:T(8,128)} custom-call(f32[16,17,8,128]{3,2,1,0:T(8,128)S(1)} %all_to_all.25.pieces), custom_call_target="tpu_custom_call" | custom-call | bytes 2097152 | tf_op jit(solution)/shard_map/strips/pallas_call | solution.py:577
  68.8 3.4 %all-to-all-done.2 = f32[8,1,128]{2,1,0:T(1,128)S(1)} async-done(((f32[8,1,128]{2,1,0:T(1,128)}), f32[8,1,128]{2,1,0:T(1,128)S(1)}, u32[]{:S(2)}, u32[]{:S(2)}) %all-to-all-start.2) | async-done | bytes 4128 | tf_op jit(solution)/shard_map/all_to_all | solution.py:575
  72.2 0.6 reduce_max.9
Async XLA Ops:
  3.8 5.2 %collective-permute-start = (f32[128,128]{1,0:T(8,128)S(1)}, f32[128,128]{1,0:T(8,128)S(1)}, u32[]{:S(2)}, u32[]{:S(2)}) collective-permute-start(f32[128,128]{1,0:T(8,128)S(1)} %get-tuple-element.15), channel_id=1, source_target_pairs={{0,1},{1,0},{2,3},{3,2},{4,5},{5,4},{6,7},{7,6},{8,9},{9,8},{10,11... | collective-permute-start | bytes 196616 | tf_op jit(solution)/shard_map/ppermute | solution.py:502
  5.2 5.6 %collective-permute-start.1 = (f32[128,128]{1,0:T(8,128)S(1)}, f32[128,128]{1,0:T(8,128)S(1)}, u32[]{:S(2)}, u32[]{:S(2)}) collective-permute-start(f32[128,128]{1,0:T(8,128)S(1)} %get-tuple-element.16), channel_id=1, source_target_pairs={{0,15},{1,2},{2,1},{3,4},{4,3},{5,6},{6,5},{7,8},{8,7},{9,10},{10,... | collective-permute-start | bytes 196616 | tf_op jit(solution)/shard_map/ppermute | solution.py:501
  11.0 24.5 %collective-permute-start.3 = (f32[36,640]{1,0:T(8,128)S(1)}, f32[36,640]{1,0:T(8,128)S(1)}, u32[]{:S(2)}, u32[]{:S(2)}) collective-permute-start(f32[36,640]{1,0:T(8,128)S(1)} %get-tuple-element.22.to_north), channel_id=1, source_target_pairs={{16,0},{32,16},{48,32},{64,48},{80,64},{96,80},{112,96},{0,112},{1... | collective-permute-start | bytes 276488 | tf_op jit(solution)/shard_map/ppermute | solution.py:516
  14.8 20.7 %collective-permute-start.2 = (f32[36,640]{1,0:T(8,128)S(1)}, f32[36,640]{1,0:T(8,128)S(1)}, u32[]{:S(2)}, u32[]{:S(2)}) collective-permute-start(f32[36,640]{1,0:T(8,128)S(1)} %get-tuple-element.23.to_south), channel_id=1, source_target_pairs={{0,16},{16,32},{32,48},{48,64},{64,80},{80,96},{96,112},{112,0},{1... | collective-permute-start | bytes 276488 | tf_op jit(solution)/shard_map/ppermute | solution.py:515
  14.8 20.7 %all-to-all-start = ((f32[128,1,128]{2,1,0:T(1,128)}), f32[128,1,128]{2,1,0:T(1,128)S(1)}, u32[]{:S(2)}, u32[]{:S(2)}) async-start(f32[128,1,128]{2,1,0:T(1,128)} %bitcast.2), calls=%async_computation | async-start | bytes 131072 | tf_op jit(solution)/shard_map/all_to_all | solution.py:504
  26.1 9.4 %copy-start = (s32[8,16]{1,0:T(8,128)S(1)}, s32[8,16]{1,0:T(8,128)}, u32[]{:S(2)}) copy-start(s32[8,16]{1,0:T(8,128)} %owner_map.1) | copy-start | bytes 1540
  63.9 8.2 %all-to-all-start.2 = ((f32[8,1,128]{2,1,0:T(1,128)}), f32[8,1,128]{2,1,0:T(1,128)S(1)}, u32[]{:S(2)}, u32[]{:S(2)}) async-start(f32[8,1,128]{2,1,0:T(1,128)} %bitcast.5), calls=%async_computation.2 | async-start | bytes 8192 | tf_op jit(solution)/shard_map/all_to_all | solution.py:575

commit v6 on v5

--- a/solution.py
+++ b/solution.py
@@ -149,17 +149,24 @@
         )
 
 
-def corners_kernel(core, chip, north_in, south_in, to_north, to_south):
-    for rows, source, target in (
-        (slice(0, 8), north_in, to_north),
-        (slice(ROWS - 8, ROWS), south_in, to_south),
-    ):
-        target[:, 0:COLS] = source[:, 0:COLS]
-        east, west = sides(core[rows, :], chip[rows, :])
-        for field in range(FIELDS):
-            value = halo_tile(east, west, field)
-            value = value[0:4] if rows.start == 0 else value[4:8]
-            target[4 * field : 4 * field + 4, COLS:WIDE] = value
+def even_wall():
+    return lax.rem(lax.axis_index("wall"), 2) == 0
+
+
+def corners_kernel(core, chip, north_in, south_in, near, far):
+    even = even_wall()
+    north, south = north_in[:, 0:COLS], south_in[:, 0:COLS]
+    near[:, 0:COLS] = jnp.where(even, south, north)
+    far[:, 0:COLS] = jnp.where(even, north, south)
+    top, bottom = slice(0, 8), slice(ROWS - 8, ROWS)
+    upper = sides(core[top, :], chip[top, :])
+    lower = sides(core[bottom, :], chip[bottom, :])
+    for field in range(FIELDS):
+        target = slice(4 * field, 4 * field + 4)
+        north = halo_tile(*upper, field)[0:4]
+        south = halo_tile(*lower, field)[4:8]
+        near[target, COLS:WIDE] = jnp.where(even, south, north)
+        far[target, COLS:WIDE] = jnp.where(even, north, south)
 
 
 def shifted_lanes(tiles):
@@ -277,10 +284,10 @@
     ring_in,
     spray,
     force_in,
-    to_north,
-    to_south,
-    from_north,
-    from_south,
+    near_sent,
+    far_sent,
+    near,
+    far,
     peaks,
     out,
     ring,
@@ -296,21 +303,27 @@
     inner = slice(8, 8 + ROWS)
     above, below = slice(4, 8), slice(8 + ROWS, 12 + ROWS)
 
+    even = even_wall()
+
+    def pair(field, cols, close, distant):
+        rows = slice(4 * field, 4 * field + 4)
+        one, two = close[rows, cols], distant[rows, cols]
+        return jnp.where(even, two, one), jnp.where(even, one, two)
+
     for tile in range(count):
         cols = slice(tile * LANES, (tile + 1) * LANES)
+        arrived = [pair(field, cols, near, far) for field in range(FIELDS)]
         for field in range(4):
-            source = slice(4 * field, 4 * field + 4)
-            ring[field, tile, above, :] = from_north[source, cols]
-            ring[field, tile, below, :] = from_south[source, cols]
-        force[3, tile, above, :] = step * from_north[28:32, cols]
+            ring[field, tile, above, :], ring[field, tile, below, :] = arrived[field]
+        force[3, tile, above, :] = step * arrived[7][0]
         force[3, tile, inner, :] = step * spray[tile]
-        force[3, tile, below, :] = step * from_south[28:32, cols]
+        force[3, tile, below, :] = step * arrived[7][1]
         for index, field in enumerate((4, 5, 6, 3, 8)):
-            source = slice(4 * field, 4 * field + 4)
-            stack[index, tile, 0:4, :] = from_north[source, cols]
-            stack[index, tile, 4:8, :] = to_north[source, cols]
-            stack[index, tile, 8:12, :] = to_south[source, cols]
-            stack[index, tile, 12:16, :] = from_south[source, cols]
+            own = pair(field, cols, near_sent, far_sent)
+            stack[index, tile, 0:4, :] = arrived[field][0]
+            stack[index, tile, 4:8, :] = own[0]
+            stack[index, tile, 8:12, :] = own[1]
+            stack[index, tile, 12:16, :] = arrived[field][1]
 
     def scale_rows(index, carry):
         row = 1 + 8 * index
@@ -502,7 +515,7 @@
     core_side = lax.ppermute(core_pack, "gas", partner)
     both = ("wall", "gas")
     peaks = lax.all_to_all(peak, both, split_axis=0, concat_axis=0, tiled=True)
-    to_north, to_south = pl.pallas_call(
+    near, far = pl.pallas_call(
         corners_kernel,
         out_shape=(shape(4 * FIELDS, WIDE), shape(4 * FIELDS, WIDE)),
         in_specs=vmem(4),
@@ -510,10 +523,10 @@
         compiler_params=params,
         name="corners",
     )(core_side, chip_side, north_main, south_main)
-    down = [(i, (i + 1) % walls) for i in range(walls)]
-    up = [(j, i) for i, j in down]
-    from_north = lax.ppermute(to_south, "wall", down)
-    from_south = lax.ppermute(to_north, "wall", up)
+    close = [(i, i ^ 1) for i in range(walls)]
+    distant = [(i, (i + 1) % walls if i % 2 else (i - 1) % walls) for i in range(walls)]
+    from_near = lax.ppermute(near, "wall", close)
+    from_far = lax.ppermute(far, "wall", distant)
 
     ring_shape = (4, TILES + 1, RING, LANES)
     ring, spray, force = pl.pallas_call(
@@ -556,10 +569,10 @@
         ring,
         spray,
         force,
-        to_north,
-        to_south,
-        from_north,
-        from_south,
+        near,
+        far,
+        from_near,
+        from_far,
         peaks,
     )
     pieces = lax.all_to_all(pieces, "gas", split_axis=0, concat_axis=0, tiled=True)

time: 73.2 us -> 71.8 us (0.981)
  starting transfers between devices: 23.5 us -> 22.1 us
    all_to_all x1, starting transfers between devices: 11.3 us -> 9.36 us  [coupling_step(): peaks = lax.all_to_all(peak, both, split_axis=0, concat_axis=0, tiled=True)]
where the time goes in v6:
time: 71.8 us; the launch traced here: 71.4 us
  blocking collectives  22.6 us (31%)
  starting transfers between devices  22.1 us (31%)
  Pallas kernels  12.9 us (18%)
  waiting for transfers between devices  12.5 us (17%)
    all_to_all x1, blocking collectives, coupling_step(): lax.all_to_all(pieces, 'gas', split_axis=0, concat_axis=0, tiled=True)  22.6 us
    all_to_all x1, starting transfers between devices, coupling_step(): peaks = lax.all_to_all(peak, both, split_axis=0, concat_axis=0, tiled=True)  9.36 us
    all_to_all x1, waiting for transfers between devices, coupling_step(): peaks = lax.all_to_all(peak, both, split_axis=0, concat_axis=0, tiled=True)  7.15 us
    pallas_call x1, Pallas kernels, coupling_step(): pl.pallas_call(film_kernel, out_shape=(shape(gases, 4 * TILES + 1, STRIP,...  5.22 us
    ppermute x1, starting transfers between devices, coupling_step(): chip_side = lax.ppermute(chip_pack, 'gas', outer)  3.69 us
    all_to_all x1, waiting for transfers between devices, coupling_step(): lax.all_to_all(band_peak, 'wall', split_axis=0, concat_axis=0, tiled=True)  3.41 us
    all_to_all x1, starting transfers between devices, coupling_step(): lax.all_to_all(band_peak, 'wall', split_axis=0, concat_axis=0, tiled=True)  3.28 us
    pallas_call x1, Pallas kernels, coupling_step(): pl.pallas_call(edges_kernel, out_shape=(shape(3, TILES + 1, RING, LANES),...  3.15 us
  transfers between devices with their start and end apart: 6, of which 3 were waited for; matrix products, arithmetic and copies ran while one was open for 0% of the time, Pallas kernels for 5%

profile of v6, /device:TPU:1, one launch (start us, length us, event | category | flops | bytes accessed | tf_op | source)
XLA Modules:
  0.0 71.4 jit_solution(14833596034349346520)
XLA Ops:
  0.6 3.1 %edges.1 = (f32[3,5,144,128]{3,2,1,0:T(8,128)S(1)}, f32[36,640]{1,0:T(8,128)S(1)}, f32[36,640]{1,0:T(8,128)S(1)}, f32[128,128]{1,0:T(8,128)S(1)}, f32[128,128]{1,0:T(8,128)S(1)}, /*index=5*/f32[128,128]{1,0:T(8,128)}) custom-call(f32[3,4,128,512]{3,2,1,0:T(8,128)} %gas_hbm.1, s32[4,128]{1,0:T(4,128)} %bitcast.9, f32[4,128,512]{2,1,0:T(8,128)} %film_hbm.3, ...), custom_call_target="tpu_custom_call" | custom-call | tf_op jit(solution)/shard_map/edges/pallas_call | solution.py:488
  3.8 1.5 %collective-permute-start = (f32[128,128]{1,0:T(8,128)S(1)}, f32[128,128]{1,0:T(8,128)S(1)}, u32[]{:S(2)}, u32[]{:S(2)}) collective-permute-start(f32[128,128]{1,0:T(8,128)S(1)} %get-tuple-element.15), channel_id=1, source_target_pairs={{0,1},{1,0},{2,3},{3,2},{4,5},{5,4},{6,7},{7,6},{8,9},{9,8},{10,11... | collective-permute-start | bytes 196616 | tf_op jit(solution)/shard_map/ppermute | solution.py:515
  5.2 3.7 %collective-permute-start.1 = (f32[128,128]{1,0:T(8,128)S(1)}, f32[128,128]{1,0:T(8,128)S(1)}, u32[]{:S(2)}, u32[]{:S(2)}) collective-permute-start(f32[128,128]{1,0:T(8,128)S(1)} %get-tuple-element.16), channel_id=1, source_target_pairs={{0,15},{1,2},{2,1},{3,4},{4,3},{5,6},{6,5},{7,8},{8,7},{9,10},{10,... | collective-permute-start | bytes 196616 | tf_op jit(solution)/shard_map/ppermute | solution.py:514
  8.9 0.0 collective-permute-done.core
  8.9 1.9 %collective-permute-done.1.chip = f32[128,128]{1,0:T(8,128)S(1)} collective-permute-done((f32[128,128]{1,0:T(8,128)S(1)}, f32[128,128]{1,0:T(8,128)S(1)}, u32[]{:S(2)}, u32[]{:S(2)}) %collective-permute-start.1) | collective-permute-done | bytes 65568 | tf_op jit(solution)/shard_map/ppermute | solution.py:514
  10.9 0.1 corners.1
  11.0 1.4 %collective-permute-start.2 = (f32[36,640]{1,0:T(8,128)S(1)}, f32[36,640]{1,0:T(8,128)S(1)}, u32[]{:S(2)}, u32[]{:S(2)}) collective-permute-start(f32[36,640]{1,0:T(8,128)S(1)} %get-tuple-element.22.near_sent), channel_id=1, source_target_pairs={{0,16},{16,0},{32,48},{48,32},{64,80},{80,64},{96,112},{112,96},{1... | collective-permute-start | bytes 276488 | tf_op jit(solution)/shard_map/ppermute | solution.py:528
  12.4 2.9 %collective-permute-start.3 = (f32[36,640]{1,0:T(8,128)S(1)}, f32[36,640]{1,0:T(8,128)S(1)}, u32[]{:S(2)}, u32[]{:S(2)}) collective-permute-start(f32[36,640]{1,0:T(8,128)S(1)} %get-tuple-element.23.far_sent), channel_id=1, source_target_pairs={{0,112},{16,32},{32,16},{48,64},{64,48},{80,96},{96,80},{112,0},{1... | collective-permute-start | bytes 276488 | tf_op jit(solution)/shard_map/ppermute | solution.py:529
  15.3 9.4 %all-to-all-start = ((f32[128,1,128]{2,1,0:T(1,128)}), f32[128,1,128]{2,1,0:T(1,128)S(1)}, u32[]{:S(2)}, u32[]{:S(2)}) async-start(f32[128,1,128]{2,1,0:T(1,128)} %bitcast.2), calls=%async_computation | async-start | bytes 131072 | tf_op jit(solution)/shard_map/all_to_all | solution.py:517
  24.7 0.0 copy-start
  24.7 2.2 %inside.1 = (f32[4,5,144,128]{3,2,1,0:T(8,128)S(1)}, f32[5,128,128]{2,1,0:T(8,128)S(1)}, f32[3,5,144,128]{3,2,1,0:T(8,128)S(1)}) custom-call(f32[3,5,144,128]{3,2,1,0:T(8,128)S(1)} %get-tuple-element.14.gas_in, f32[4,128,512]{2,1,0:T(8,128)} %film_hbm.3, s32[4,128]{1,0:T(4,128)} %bitcast.10, ...), custom_call_target="tpu_custom_call", output_to_operand_aliasing={{2}: (0, {})} | custom-call | flops 20971520 | bytes 8388608 | tf_op jit(solution)/shard_map/inside/pallas_call | solution.py:532
  26.9 7.2 %all-to-all-done = f32[128,1,128]{2,1,0:T(1,128)S(1)} async-done(((f32[128,1,128]{2,1,0:T(1,128)}), f32[128,1,128]{2,1,0:T(1,128)S(1)}, u32[]{:S(2)}, u32[]{:S(2)}) %all-to-all-start) | async-done | bytes 65568 | tf_op jit(solution)/shard_map/all_to_all | solution.py:517
  34.1 0.0 collective-permute-done.2.near
  34.1 0.0 collective-permute-done.3.far
  34.1 0.0 copy-done
  34.1 5.2 %film.1 = (f32[16,17,8,128]{3,2,1,0:T(8,128)S(1)}, f32[4,5,144,128]{3,2,1,0:T(8,128)S(1)}) custom-call(s32[8,16]{1,0:T(8,128)S(1)} %copy-done, f32[4,5,144,128]{3,2,1,0:T(8,128)S(1)} %get-tuple-element.17.ring_in, f32[5,128,128]{2,1,0:T(8,128)S(1)} %get-tuple-element.18.spray, ...), custom_call_target="tpu_custom_call", output_to_operand_aliasing={{1}: (1, {})} | custom-call | tf_op jit(solution)/shard_map/film/pallas_call | solution.py:553
  39.3 22.6 %all_to_all.25.pieces = f32[16,17,8,128]{3,2,1,0:T(8,128)S(1)} all-to-all(f32[16,17,8,128]{3,2,1,0:T(8,128)S(1)} %get-tuple-element.25), channel_id=1, replica_groups=mesh['wall'=8,'gas'=16] {'gas'}, dimensions={0} | all-to-all | bytes 2228224 | tf_op jit(solution)/shard_map/all_to_all | solution.py:578
  61.9 0.6 band_peak.1
  62.5 3.3 %all-to-all-start.2 = ((f32[8,1,128]{2,1,0:T(1,128)}), f32[8,1,128]{2,1,0:T(1,128)S(1)}, u32[]{:S(2)}, u32[]{:S(2)}) async-start(f32[8,1,128]{2,1,0:T(1,128)} %bitcast.5), calls=%async_computation.2 | async-start | bytes 8192 | tf_op jit(solution)/shard_map/all_to_all | solution.py:588
  65.8 1.5 %strips.1 = f32[4,8,8192]{2,1,0:T(8,128)} custom-call(f32[16,17,8,128]{3,2,1,0:T(8,128)S(1)} %all_to_all.25.pieces), custom_call_target="tpu_custom_call" | custom-call | bytes 2097152 | tf_op jit(solution)/shard_map/strips/pallas_call | solution.py:590
  67.3 3.4 %all-to-all-done.2 = f32[8,1,128]{2,1,0:T(1,128)S(1)} async-done(((f32[8,1,128]{2,1,0:T(1,128)}), f32[8,1,128]{2,1,0:T(1,128)S(1)}, u32[]{:S(2)}, u32[]{:S(2)}) %all-to-all-start.2) | async-done | bytes 4128 | tf_op jit(solution)/shard_map/all_to_all | solution.py:588
  70.8 0.6 reduce_max.9
Async XLA Ops:
  3.8 5.2 %collective-permute-start = (f32[128,128]{1,0:T(8,128)S(1)}, f32[128,128]{1,0:T(8,128)S(1)}, u32[]{:S(2)}, u32[]{:S(2)}) collective-permute-start(f32[128,128]{1,0:T(8,128)S(1)} %get-tuple-element.15), channel_id=1, source_target_pairs={{0,1},{1,0},{2,3},{3,2},{4,5},{5,4},{6,7},{7,6},{8,9},{9,8},{10,11... | collective-permute-start | bytes 196616 | tf_op jit(solution)/shard_map/ppermute | solution.py:515
  5.2 5.6 %collective-permute-start.1 = (f32[128,128]{1,0:T(8,128)S(1)}, f32[128,128]{1,0:T(8,128)S(1)}, u32[]{:S(2)}, u32[]{:S(2)}) collective-permute-start(f32[128,128]{1,0:T(8,128)S(1)} %get-tuple-element.16), channel_id=1, source_target_pairs={{0,15},{1,2},{2,1},{3,4},{4,3},{5,6},{6,5},{7,8},{8,7},{9,10},{10,... | collective-permute-start | bytes 196616 | tf_op jit(solution)/shard_map/ppermute | solution.py:514
  11.0 23.1 %collective-permute-start.2 = (f32[36,640]{1,0:T(8,128)S(1)}, f32[36,640]{1,0:T(8,128)S(1)}, u32[]{:S(2)}, u32[]{:S(2)}) collective-permute-start(f32[36,640]{1,0:T(8,128)S(1)} %get-tuple-element.22.near_sent), channel_id=1, source_target_pairs={{0,16},{16,0},{32,48},{48,32},{64,80},{80,64},{96,112},{112,96},{1... | collective-permute-start | bytes 276488 | tf_op jit(solution)/shard_map/ppermute | solution.py:528
  12.4 21.7 %collective-permute-start.3 = (f32[36,640]{1,0:T(8,128)S(1)}, f32[36,640]{1,0:T(8,128)S(1)}, u32[]{:S(2)}, u32[]{:S(2)}) collective-permute-start(f32[36,640]{1,0:T(8,128)S(1)} %get-tuple-element.23.far_sent), channel_id=1, source_target_pairs={{0,112},{16,32},{32,16},{48,64},{64,48},{80,96},{96,80},{112,0},{1... | collective-permute-start | bytes 276488 | tf_op jit(solution)/shard_map/ppermute | solution.py:529
  15.3 18.8 %all-to-all-start = ((f32[128,1,128]{2,1,0:T(1,128)}), f32[128,1,128]{2,1,0:T(1,128)S(1)}, u32[]{:S(2)}, u32[]{:S(2)}) async-start(f32[128,1,128]{2,1,0:T(1,128)} %bitcast.2), calls=%async_computation | async-start | bytes 131072 | tf_op jit(solution)/shard_map/all_to_all | solution.py:517
  24.7 9.4 %copy-start = (s32[8,16]{1,0:T(8,128)S(1)}, s32[8,16]{1,0:T(8,128)}, u32[]{:S(2)}) copy-start(s32[8,16]{1,0:T(8,128)} %owner_map.1) | copy-start | bytes 1540
  62.5 8.2 %all-to-all-start.2 = ((f32[8,1,128]{2,1,0:T(1,128)}), f32[8,1,128]{2,1,0:T(1,128)S(1)}, u32[]{:S(2)}, u32[]{:S(2)}) async-start(f32[8,1,128]{2,1,0:T(1,128)} %bitcast.5), calls=%async_computation.2 | async-start | bytes 8192 | tf_op jit(solution)/shard_map/all_to_all | solution.py:588

commit v7 on v6

--- a/solution.py
+++ b/solution.py
@@ -374,35 +374,38 @@
             norths.append(north)
             souths.append(south)
         news = []
+        keep = 1.0 - 4.0 * FILM_SPREAD
         for t in range(count):
-            spread = [
-                (1.0 - 4.0 * FILM_SPREAD) * centre[f][t]
-                + FILM_SPREAD
+            mixed = [
+                FILM_SPREAD
                 * ((norths[f][t] + souths[f][t]) + (wests[f][t] + easts[f][t]))
                 for f in range(4)
             ]
             height = centre[0][t]
             inverse = lax.rsqrt(height * height + FILM_FLOOR * FILM_FLOOR)
-            drag = (FRICTION * step) * inverse
+            keep_moving = keep - (FRICTION * step) * inverse
             slope = half * height
             height_new = (
-                spread[0]
+                keep * height
+                + mixed[0]
                 + force[3, t, here, :]
                 - half * ((easts[1][t] - wests[1][t]) + (souths[2][t] - norths[2][t]))
             )
             along_new = (
-                spread[1]
+                keep_moving * centre[1][t]
+                + mixed[1]
                 + force[0, t, here, :]
-                - drag * centre[1][t]
                 - slope * (easts[0][t] - wests[0][t])
             )
             across_new = (
-                spread[2]
+                keep_moving * centre[2][t]
+                + mixed[2]
                 + force[1, t, here, :]
-                - drag * centre[2][t]
                 - slope * (souths[0][t] - norths[0][t])
             )
-            heat_new = spread[3] + force[2, t, here, :] * inverse
+            heat_new = (
+                keep * centre[3][t] + mixed[3] + force[2, t, here, :] * inverse
+            )
             news.append((height_new, along_new, across_new, heat_new))
         return news
 
@@ -415,7 +418,7 @@
                     target[field, t, pl.ds(row, STRIP), :] = news[t][field]
             return carry
 
-        grouped(6, 17, body, 0)
+        grouped(17, 17, body, 0)
 
     def load_from(source):
         return lambda field, t, rows: source[field, t, rows, :]
@@ -434,7 +437,7 @@
             best = jnp.maximum(best, film_speed(*news[t][:3]))
         return best
 
-    best = grouped(4, 16, last_rows, jnp.zeros((STRIP, LANES), jnp.float32))
+    best = grouped(16, 16, last_rows, jnp.zeros((STRIP, LANES), jnp.float32))
     top = jnp.broadcast_to(step * jnp.max(best, keepdims=True), (STRIP, LANES))
     for owner in range(ROWS // STRIP):
         out[owner, 4 * TILES] = top

time: 71.8 us -> 70.8 us (0.986)
  Pallas kernels: 12.9 us -> 11.9 us
    pallas_call x1, Pallas kernels: 5.22 us -> 4.2 us  [coupling_step(): pl.pallas_call(film_kernel, out_shape=(shape(gases, 4 * TILES + 1, STRIP,...]
where the time goes in v7:
time: 70.8 us; the launch traced here: 70.3 us
  blocking collectives  22.6 us (32%)
  starting transfers between devices  22.1 us (31%)
  waiting for transfers between devices  12.5 us (18%)
  Pallas kernels  11.9 us (17%)
    all_to_all x1, blocking collectives, coupling_step(): lax.all_to_all(pieces, 'gas', split_axis=0, concat_axis=0, tiled=True)  22.6 us
    all_to_all x1, starting transfers between devices, coupling_step(): peaks = lax.all_to_all(peak, both, split_axis=0, concat_axis=0, tiled=True)  9.36 us
    all_to_all x1, waiting for transfers between devices, coupling_step(): peaks = lax.all_to_all(peak, both, split_axis=0, concat_axis=0, tiled=True)  7.15 us
    pallas_call x1, Pallas kernels, coupling_step(): pl.pallas_call(film_kernel, out_shape=(shape(gases, 4 * TILES + 1, STRIP,...  4.2 us
    ppermute x1, starting transfers between devices, coupling_step(): chip_side = lax.ppermute(chip_pack, 'gas', outer)  3.69 us
    all_to_all x1, waiting for transfers between devices, coupling_step(): lax.all_to_all(band_peak, 'wall', split_axis=0, concat_axis=0, tiled=True)  3.41 us
    all_to_all x1, starting transfers between devices, coupling_step(): lax.all_to_all(band_peak, 'wall', split_axis=0, concat_axis=0, tiled=True)  3.28 us
    pallas_call x1, Pallas kernels, coupling_step(): pl.pallas_call(edges_kernel, out_shape=(shape(3, TILES + 1, RING, LANES),...  3.15 us
  transfers between devices with their start and end apart: 6, of which 3 were waited for; matrix products, arithmetic and copies ran while one was open for 0% of the time, Pallas kernels for 5%

profile of v7, /device:TPU:1, one launch (start us, length us, event | category | flops | bytes accessed | tf_op | source)
XLA Modules:
  0.0 70.3 jit_solution(4490281193944655083)
XLA Ops:
  0.6 3.1 %edges.1 = (f32[3,5,144,128]{3,2,1,0:T(8,128)S(1)}, f32[36,640]{1,0:T(8,128)S(1)}, f32[36,640]{1,0:T(8,128)S(1)}, f32[128,128]{1,0:T(8,128)S(1)}, f32[128,128]{1,0:T(8,128)S(1)}, /*index=5*/f32[128,128]{1,0:T(8,128)}) custom-call(f32[3,4,128,512]{3,2,1,0:T(8,128)} %gas_hbm.1, s32[4,128]{1,0:T(4,128)} %bitcast.9, f32[4,128,512]{2,1,0:T(8,128)} %film_hbm.3, ...), custom_call_target="tpu_custom_call" | custom-call | tf_op jit(solution)/shard_map/edges/pallas_call | solution.py:491
  3.8 1.5 %collective-permute-start = (f32[128,128]{1,0:T(8,128)S(1)}, f32[128,128]{1,0:T(8,128)S(1)}, u32[]{:S(2)}, u32[]{:S(2)}) collective-permute-start(f32[128,128]{1,0:T(8,128)S(1)} %get-tuple-element.15), channel_id=1, source_target_pairs={{0,1},{1,0},{2,3},{3,2},{4,5},{5,4},{6,7},{7,6},{8,9},{9,8},{10,11... | collective-permute-start | bytes 196616 | tf_op jit(solution)/shard_map/ppermute | solution.py:518
  5.2 3.7 %collective-permute-start.1 = (f32[128,128]{1,0:T(8,128)S(1)}, f32[128,128]{1,0:T(8,128)S(1)}, u32[]{:S(2)}, u32[]{:S(2)}) collective-permute-start(f32[128,128]{1,0:T(8,128)S(1)} %get-tuple-element.16), channel_id=1, source_target_pairs={{0,15},{1,2},{2,1},{3,4},{4,3},{5,6},{6,5},{7,8},{8,7},{9,10},{10,... | collective-permute-start | bytes 196616 | tf_op jit(solution)/shard_map/ppermute | solution.py:517
  8.9 0.0 collective-permute-done.core
  8.9 1.9 %collective-permute-done.1.chip = f32[128,128]{1,0:T(8,128)S(1)} collective-permute-done((f32[128,128]{1,0:T(8,128)S(1)}, f32[128,128]{1,0:T(8,128)S(1)}, u32[]{:S(2)}, u32[]{:S(2)}) %collective-permute-start.1) | collective-permute-done | bytes 65568 | tf_op jit(solution)/shard_map/ppermute | solution.py:517
  10.9 0.1 corners.1
  11.0 1.4 %collective-permute-start.2 = (f32[36,640]{1,0:T(8,128)S(1)}, f32[36,640]{1,0:T(8,128)S(1)}, u32[]{:S(2)}, u32[]{:S(2)}) collective-permute-start(f32[36,640]{1,0:T(8,128)S(1)} %get-tuple-element.22.near_sent), channel_id=1, source_target_pairs={{0,16},{16,0},{32,48},{48,32},{64,80},{80,64},{96,112},{112,96},{1... | collective-permute-start | bytes 276488 | tf_op jit(solution)/shard_map/ppermute | solution.py:531
  12.4 2.9 %collective-permute-start.3 = (f32[36,640]{1,0:T(8,128)S(1)}, f32[36,640]{1,0:T(8,128)S(1)}, u32[]{:S(2)}, u32[]{:S(2)}) collective-permute-start(f32[36,640]{1,0:T(8,128)S(1)} %get-tuple-element.23.far_sent), channel_id=1, source_target_pairs={{0,112},{16,32},{32,16},{48,64},{64,48},{80,96},{96,80},{112,0},{1... | collective-permute-start | bytes 276488 | tf_op jit(solution)/shard_map/ppermute | solution.py:532
  15.3 9.4 %all-to-all-start = ((f32[128,1,128]{2,1,0:T(1,128)}), f32[128,1,128]{2,1,0:T(1,128)S(1)}, u32[]{:S(2)}, u32[]{:S(2)}) async-start(f32[128,1,128]{2,1,0:T(1,128)} %bitcast.2), calls=%async_computation | async-start | bytes 131072 | tf_op jit(solution)/shard_map/all_to_all | solution.py:520
  24.7 0.0 copy-start
  24.7 2.2 %inside.1 = (f32[4,5,144,128]{3,2,1,0:T(8,128)S(1)}, f32[5,128,128]{2,1,0:T(8,128)S(1)}, f32[3,5,144,128]{3,2,1,0:T(8,128)S(1)}) custom-call(f32[3,5,144,128]{3,2,1,0:T(8,128)S(1)} %get-tuple-element.14.gas_in, f32[4,128,512]{2,1,0:T(8,128)} %film_hbm.3, s32[4,128]{1,0:T(4,128)} %bitcast.10, ...), custom_call_target="tpu_custom_call", output_to_operand_aliasing={{2}: (0, {})} | custom-call | flops 20971520 | bytes 8388608 | tf_op jit(solution)/shard_map/inside/pallas_call | solution.py:535
  26.9 7.2 %all-to-all-done = f32[128,1,128]{2,1,0:T(1,128)S(1)} async-done(((f32[128,1,128]{2,1,0:T(1,128)}), f32[128,1,128]{2,1,0:T(1,128)S(1)}, u32[]{:S(2)}, u32[]{:S(2)}) %all-to-all-start) | async-done | bytes 65568 | tf_op jit(solution)/shard_map/all_to_all | solution.py:520
  34.1 0.0 collective-permute-done.2.near
  34.1 0.0 collective-permute-done.3.far
  34.1 0.0 copy-done
  34.1 4.2 %film.1 = (f32[16,17,8,128]{3,2,1,0:T(8,128)S(1)}, f32[4,5,144,128]{3,2,1,0:T(8,128)S(1)}) custom-call(s32[8,16]{1,0:T(8,128)S(1)} %copy-done, f32[4,5,144,128]{3,2,1,0:T(8,128)S(1)} %get-tuple-element.17.ring_in, f32[5,128,128]{2,1,0:T(8,128)S(1)} %get-tuple-element.18.spray, ...), custom_call_target="tpu_custom_call", output_to_operand_aliasing={{1}: (1, {})} | custom-call | tf_op jit(solution)/shard_map/film/pallas_call | solution.py:556
  38.3 22.6 %all_to_all.25.pieces = f32[16,17,8,128]{3,2,1,0:T(8,128)S(1)} all-to-all(f32[16,17,8,128]{3,2,1,0:T(8,128)S(1)} %get-tuple-element.25), channel_id=1, replica_groups=mesh['wall'=8,'gas'=16] {'gas'}, dimensions={0} | all-to-all | bytes 2228224 | tf_op jit(solution)/shard_map/all_to_all | solution.py:581
  60.9 0.6 band_peak.1
  61.5 3.3 %all-to-all-start.2 = ((f32[8,1,128]{2,1,0:T(1,128)}), f32[8,1,128]{2,1,0:T(1,128)S(1)}, u32[]{:S(2)}, u32[]{:S(2)}) async-start(f32[8,1,128]{2,1,0:T(1,128)} %bitcast.5), calls=%async_computation.2 | async-start | bytes 8192 | tf_op jit(solution)/shard_map/all_to_all | solution.py:591
  64.8 1.5 %strips.1 = f32[4,8,8192]{2,1,0:T(8,128)} custom-call(f32[16,17,8,128]{3,2,1,0:T(8,128)S(1)} %all_to_all.25.pieces), custom_call_target="tpu_custom_call" | custom-call | bytes 2097152 | tf_op jit(solution)/shard_map/strips/pallas_call | solution.py:593
  66.3 3.4 %all-to-all-done.2 = f32[8,1,128]{2,1,0:T(1,128)S(1)} async-done(((f32[8,1,128]{2,1,0:T(1,128)}), f32[8,1,128]{2,1,0:T(1,128)S(1)}, u32[]{:S(2)}, u32[]{:S(2)}) %all-to-all-start.2) | async-done | bytes 4128 | tf_op jit(solution)/shard_map/all_to_all | solution.py:591
  69.7 0.6 reduce_max.9
Async XLA Ops:
  3.8 5.2 %collective-permute-start = (f32[128,128]{1,0:T(8,128)S(1)}, f32[128,128]{1,0:T(8,128)S(1)}, u32[]{:S(2)}, u32[]{:S(2)}) collective-permute-start(f32[128,128]{1,0:T(8,128)S(1)} %get-tuple-element.15), channel_id=1, source_target_pairs={{0,1},{1,0},{2,3},{3,2},{4,5},{5,4},{6,7},{7,6},{8,9},{9,8},{10,11... | collective-permute-start | bytes 196616 | tf_op jit(solution)/shard_map/ppermute | solution.py:518
  5.2 5.6 %collective-permute-start.1 = (f32[128,128]{1,0:T(8,128)S(1)}, f32[128,128]{1,0:T(8,128)S(1)}, u32[]{:S(2)}, u32[]{:S(2)}) collective-permute-start(f32[128,128]{1,0:T(8,128)S(1)} %get-tuple-element.16), channel_id=1, source_target_pairs={{0,15},{1,2},{2,1},{3,4},{4,3},{5,6},{6,5},{7,8},{8,7},{9,10},{10,... | collective-permute-start | bytes 196616 | tf_op jit(solution)/shard_map/ppermute | solution.py:517
  11.0 23.1 %collective-permute-start.2 = (f32[36,640]{1,0:T(8,128)S(1)}, f32[36,640]{1,0:T(8,128)S(1)}, u32[]{:S(2)}, u32[]{:S(2)}) collective-permute-start(f32[36,640]{1,0:T(8,128)S(1)} %get-tuple-element.22.near_sent), channel_id=1, source_target_pairs={{0,16},{16,0},{32,48},{48,32},{64,80},{80,64},{96,112},{112,96},{1... | collective-permute-start | bytes 276488 | tf_op jit(solution)/shard_map/ppermute | solution.py:531
  12.4 21.7 %collective-permute-start.3 = (f32[36,640]{1,0:T(8,128)S(1)}, f32[36,640]{1,0:T(8,128)S(1)}, u32[]{:S(2)}, u32[]{:S(2)}) collective-permute-start(f32[36,640]{1,0:T(8,128)S(1)} %get-tuple-element.23.far_sent), channel_id=1, source_target_pairs={{0,112},{16,32},{32,16},{48,64},{64,48},{80,96},{96,80},{112,0},{1... | collective-permute-start | bytes 276488 | tf_op jit(solution)/shard_map/ppermute | solution.py:532
  15.3 18.8 %all-to-all-start = ((f32[128,1,128]{2,1,0:T(1,128)}), f32[128,1,128]{2,1,0:T(1,128)S(1)}, u32[]{:S(2)}, u32[]{:S(2)}) async-start(f32[128,1,128]{2,1,0:T(1,128)} %bitcast.2), calls=%async_computation | async-start | bytes 131072 | tf_op jit(solution)/shard_map/all_to_all | solution.py:520
  24.7 9.4 %copy-start = (s32[8,16]{1,0:T(8,128)S(1)}, s32[8,16]{1,0:T(8,128)}, u32[]{:S(2)}) copy-start(s32[8,16]{1,0:T(8,128)} %owner_map.1) | copy-start | bytes 1540
  61.5 8.2 %all-to-all-start.2 = ((f32[8,1,128]{2,1,0:T(1,128)}), f32[8,1,128]{2,1,0:T(1,128)S(1)}, u32[]{:S(2)}, u32[]{:S(2)}) async-start(f32[8,1,128]{2,1,0:T(1,128)} %bitcast.5), calls=%async_computation.2 | async-start | bytes 8192 | tf_op jit(solution)/shard_map/all_to_all | solution.py:591

commit v8 on v7

--- a/solution.py
+++ b/solution.py
@@ -37,9 +37,10 @@
 
 def film_speed(height, along, across):
     square = height * height + FILM_FLOOR * FILM_FLOOR
-    thickness = jnp.sqrt(square)
+    inverse = lax.rsqrt(square)
+    thickness = square * inverse
     moving = jnp.sqrt(along * along + across * across)
-    return moving / thickness + jnp.sqrt(thickness)
+    return moving * inverse + thickness * lax.rsqrt(thickness)
 
 
 def halo_tile(east, west, field):
@@ -91,13 +92,12 @@
     flags,
     sems,
 ):
+    pairs = [(flags_hbm, flags), (deposit_hbm, deposit)]
+    pairs += [(film_hbm.at[field], film.at[field]) for field in range(4)]
+    pairs += [(gas_hbm.at[field], gas.at[field]) for field in range(3)]
     copies = [
-        pltpu.make_async_copy(film_hbm, film, sems.at[0]),
-        pltpu.make_async_copy(flags_hbm, flags, sems.at[1]),
-        pltpu.make_async_copy(deposit_hbm, deposit, sems.at[2]),
-        pltpu.make_async_copy(gas_hbm.at[0], gas.at[0], sems.at[3]),
-        pltpu.make_async_copy(gas_hbm.at[1], gas.at[1], sems.at[4]),
-        pltpu.make_async_copy(gas_hbm.at[2], gas.at[2], sems.at[5]),
+        pltpu.make_async_copy(source, target, sems.at[index])
+        for index, (source, target) in enumerate(pairs)
     ]
     for copy in copies:
         copy.start()
@@ -106,7 +106,7 @@
     even = lax.rem(lax.axis_index("gas"), 2) == 0
     lane = lane_iota((ROWS, LANES))
 
-    def send(field, value_of):
+    def send(field, value_of, fresh=False):
         target = slice(4 * field, 4 * field + 4)
         for tile, cols in enumerate(tiles):
             to_north[target, cols] = value_of(slice(0, 4), tile)
@@ -120,27 +120,30 @@
             (core_pack, jnp.where(even, east, west)),
             (chip_pack, jnp.where(even, west, east)),
         ):
-            old = pack[...] if field else jnp.zeros_like(value)
+            old = jnp.zeros_like(value) if fresh else pack[...]
             pack[...] = jnp.where(here, value, old)
 
     copies[0].wait()
-    best = jnp.zeros((STRIP, LANES), jnp.float32)
-    for cols in tiles:
-        speed = film_speed(film[0, :, cols], film[1, :, cols], film[2, :, cols])
-        for row in range(0, ROWS, STRIP):
-            best = jnp.maximum(best, speed[row : row + STRIP])
-    peak[...] = jnp.broadcast_to(jnp.max(best, keepdims=True), (ROWS, LANES))
+    columns = flag_columns(flags[...])
+    send(8, lambda rows, tile: attached_rows(columns, rows, tile), True)
+    copies[1].wait()
+    send(7, lambda rows, tile: deposit[rows, tiles[tile]])
     for field in range(4):
+        copies[2 + field].wait()
         send(field, lambda rows, tile, f=field: film[f, rows, tiles[tile]])
-    copies[1].wait()
-    columns = flag_columns(flags[...])
-    send(8, lambda rows, tile: attached_rows(columns, rows, tile))
-    copies[2].wait()
-    send(7, lambda rows, tile: deposit[rows, tiles[tile]])
+        if field == 2:
+            best = jnp.zeros((STRIP, LANES), jnp.float32)
+            for cols in tiles:
+                speed = film_speed(film[0, :, cols], film[1, :, cols], film[2, :, cols])
+                for row in range(0, ROWS, STRIP):
+                    best = jnp.maximum(best, speed[row : row + STRIP])
+            peak[...] = jnp.broadcast_to(jnp.max(best, keepdims=True), (ROWS, LANES))
     for field in range(3):
-        copies[3 + field].wait()
+        copies[6 + field].wait()
         for tile, cols in enumerate(tiles):
-            gas_ring[field, tile, AHEAD : AHEAD + ROWS, :] = sample(gas, field, every, cols)
+            gas_ring[field, tile, AHEAD : AHEAD + ROWS, :] = sample(
+                gas, field, every, cols
+            )
         send(
             4 + field,
             lambda rows, tile, f=field: gas_ring[
@@ -505,7 +508,7 @@
             pltpu.VMEM((3, 4, ROWS, COLS), jnp.float32),
             pltpu.VMEM((ROWS, COLS), jnp.float32),
             pltpu.VMEM((TILES, ROWS), jnp.int32),
-            pltpu.SemaphoreType.DMA((6,)),
+            pltpu.SemaphoreType.DMA((9,)),
         ],
         compiler_params=pltpu.CompilerParams(vmem_limit_bytes=VMEM_LIMIT),
         name="edges",

time: 70.8 us -> 70.5 us (level)
  no operation moved by 1% of the time
where the time goes in v8:
time: 70.5 us; the launch traced here: 70.1 us
  blocking collectives  22.6 us (32%)
  starting transfers between devices  22.1 us (31%)
  waiting for transfers between devices  12.5 us (18%)
  Pallas kernels  11.6 us (16%)
    all_to_all x1, blocking collectives, coupling_step(): lax.all_to_all(pieces, 'gas', split_axis=0, concat_axis=0, tiled=True)  22.6 us
    all_to_all x1, starting transfers between devices, coupling_step(): peaks = lax.all_to_all(peak, both, split_axis=0, concat_axis=0, tiled=True)  9.36 us
    all_to_all x1, waiting for transfers between devices, coupling_step(): peaks = lax.all_to_all(peak, both, split_axis=0, concat_axis=0, tiled=True)  7.15 us
    pallas_call x1, Pallas kernels, coupling_step(): pl.pallas_call(film_kernel, out_shape=(shape(gases, 4 * TILES + 1, STRIP,...  4.09 us
    ppermute x1, starting transfers between devices, coupling_step(): chip_side = lax.ppermute(chip_pack, 'gas', outer)  3.69 us
    all_to_all x1, waiting for transfers between devices, coupling_step(): lax.all_to_all(band_peak, 'wall', split_axis=0, concat_axis=0, tiled=True)  3.41 us
    all_to_all x1, starting transfers between devices, coupling_step(): lax.all_to_all(band_peak, 'wall', split_axis=0, concat_axis=0, tiled=True)  3.28 us
    pallas_call x1, Pallas kernels, coupling_step(): pl.pallas_call(edges_kernel, out_shape=(shape(3, TILES + 1, RING, LANES),...  2.98 us
  transfers between devices with their start and end apart: 6, of which 3 were waited for; matrix products, arithmetic and copies ran while one was open for 0% of the time, Pallas kernels for 5%

profile of v8, /device:TPU:1, one launch (start us, length us, event | category | flops | bytes accessed | tf_op | source)
XLA Modules:
  0.0 70.1 jit_solution(8253511754798042244)
XLA Ops:
  0.6 3.0 %edges.1 = (f32[3,5,144,128]{3,2,1,0:T(8,128)S(1)}, f32[36,640]{1,0:T(8,128)S(1)}, f32[36,640]{1,0:T(8,128)S(1)}, f32[128,128]{1,0:T(8,128)S(1)}, f32[128,128]{1,0:T(8,128)S(1)}, /*index=5*/f32[128,128]{1,0:T(8,128)}) custom-call(f32[3,4,128,512]{3,2,1,0:T(8,128)} %gas_hbm.1, s32[4,128]{1,0:T(4,128)} %bitcast.9, f32[4,128,512]{2,1,0:T(8,128)} %film_hbm.3, ...), custom_call_target="tpu_custom_call" | custom-call | tf_op jit(solution)/shard_map/edges/pallas_call | solution.py:494
  3.6 1.5 %collective-permute-start = (f32[128,128]{1,0:T(8,128)S(1)}, f32[128,128]{1,0:T(8,128)S(1)}, u32[]{:S(2)}, u32[]{:S(2)}) collective-permute-start(f32[128,128]{1,0:T(8,128)S(1)} %get-tuple-element.15), channel_id=1, source_target_pairs={{0,1},{1,0},{2,3},{3,2},{4,5},{5,4},{6,7},{7,6},{8,9},{9,8},{10,11... | collective-permute-start | bytes 196616 | tf_op jit(solution)/shard_map/ppermute | solution.py:521
  5.1 3.7 %collective-permute-start.1 = (f32[128,128]{1,0:T(8,128)S(1)}, f32[128,128]{1,0:T(8,128)S(1)}, u32[]{:S(2)}, u32[]{:S(2)}) collective-permute-start(f32[128,128]{1,0:T(8,128)S(1)} %get-tuple-element.16), channel_id=1, source_target_pairs={{0,15},{1,2},{2,1},{3,4},{4,3},{5,6},{6,5},{7,8},{8,7},{9,10},{10,... | collective-permute-start | bytes 196616 | tf_op jit(solution)/shard_map/ppermute | solution.py:520
  8.8 0.0 collective-permute-done.core
  8.8 1.9 %collective-permute-done.1.chip = f32[128,128]{1,0:T(8,128)S(1)} collective-permute-done((f32[128,128]{1,0:T(8,128)S(1)}, f32[128,128]{1,0:T(8,128)S(1)}, u32[]{:S(2)}, u32[]{:S(2)}) %collective-permute-start.1) | collective-permute-done | bytes 65568 | tf_op jit(solution)/shard_map/ppermute | solution.py:520
  10.7 0.1 corners.1
  10.8 1.4 %collective-permute-start.2 = (f32[36,640]{1,0:T(8,128)S(1)}, f32[36,640]{1,0:T(8,128)S(1)}, u32[]{:S(2)}, u32[]{:S(2)}) collective-permute-start(f32[36,640]{1,0:T(8,128)S(1)} %get-tuple-element.22.near_sent), channel_id=1, source_target_pairs={{0,16},{16,0},{32,48},{48,32},{64,80},{80,64},{96,112},{112,96},{1... | collective-permute-start | bytes 276488 | tf_op jit(solution)/shard_map/ppermute | solution.py:534
  12.2 2.9 %collective-permute-start.3 = (f32[36,640]{1,0:T(8,128)S(1)}, f32[36,640]{1,0:T(8,128)S(1)}, u32[]{:S(2)}, u32[]{:S(2)}) collective-permute-start(f32[36,640]{1,0:T(8,128)S(1)} %get-tuple-element.23.far_sent), channel_id=1, source_target_pairs={{0,112},{16,32},{32,16},{48,64},{64,48},{80,96},{96,80},{112,0},{1... | collective-permute-start | bytes 276488 | tf_op jit(solution)/shard_map/ppermute | solution.py:535
  15.1 9.4 %all-to-all-start = ((f32[128,1,128]{2,1,0:T(1,128)}), f32[128,1,128]{2,1,0:T(1,128)S(1)}, u32[]{:S(2)}, u32[]{:S(2)}) async-start(f32[128,1,128]{2,1,0:T(1,128)} %bitcast.2), calls=%async_computation | async-start | bytes 131072 | tf_op jit(solution)/shard_map/all_to_all | solution.py:523
  24.5 0.0 copy-start
  24.5 2.2 %inside.1 = (f32[4,5,144,128]{3,2,1,0:T(8,128)S(1)}, f32[5,128,128]{2,1,0:T(8,128)S(1)}, f32[3,5,144,128]{3,2,1,0:T(8,128)S(1)}) custom-call(f32[3,5,144,128]{3,2,1,0:T(8,128)S(1)} %get-tuple-element.14.gas_in, f32[4,128,512]{2,1,0:T(8,128)} %film_hbm.3, s32[4,128]{1,0:T(4,128)} %bitcast.10, ...), custom_call_target="tpu_custom_call", output_to_operand_aliasing={{2}: (0, {})} | custom-call | flops 20971520 | bytes 8388608 | tf_op jit(solution)/shard_map/inside/pallas_call | solution.py:538
  26.8 7.2 %all-to-all-done = f32[128,1,128]{2,1,0:T(1,128)S(1)} async-done(((f32[128,1,128]{2,1,0:T(1,128)}), f32[128,1,128]{2,1,0:T(1,128)S(1)}, u32[]{:S(2)}, u32[]{:S(2)}) %all-to-all-start) | async-done | bytes 65568 | tf_op jit(solution)/shard_map/all_to_all | solution.py:523
  33.9 0.0 collective-permute-done.2.near
  33.9 0.0 collective-permute-done.3.far
  33.9 0.0 copy-done
  33.9 4.1 %film.1 = (f32[16,17,8,128]{3,2,1,0:T(8,128)S(1)}, f32[4,5,144,128]{3,2,1,0:T(8,128)S(1)}) custom-call(s32[8,16]{1,0:T(8,128)S(1)} %copy-done, f32[4,5,144,128]{3,2,1,0:T(8,128)S(1)} %get-tuple-element.17.ring_in, f32[5,128,128]{2,1,0:T(8,128)S(1)} %get-tuple-element.18.spray, ...), custom_call_target="tpu_custom_call", output_to_operand_aliasing={{1}: (1, {})} | custom-call | tf_op jit(solution)/shard_map/film/pallas_call | solution.py:559
  38.0 22.6 %all_to_all.25.pieces = f32[16,17,8,128]{3,2,1,0:T(8,128)S(1)} all-to-all(f32[16,17,8,128]{3,2,1,0:T(8,128)S(1)} %get-tuple-element.25), channel_id=1, replica_groups=mesh['wall'=8,'gas'=16] {'gas'}, dimensions={0} | all-to-all | bytes 2228224 | tf_op jit(solution)/shard_map/all_to_all | solution.py:584
  60.6 0.6 band_peak.1
  61.2 3.3 %all-to-all-start.2 = ((f32[8,1,128]{2,1,0:T(1,128)}), f32[8,1,128]{2,1,0:T(1,128)S(1)}, u32[]{:S(2)}, u32[]{:S(2)}) async-start(f32[8,1,128]{2,1,0:T(1,128)} %bitcast.5), calls=%async_computation.2 | async-start | bytes 8192 | tf_op jit(solution)/shard_map/all_to_all | solution.py:594
  64.5 1.5 %strips.1 = f32[4,8,8192]{2,1,0:T(8,128)} custom-call(f32[16,17,8,128]{3,2,1,0:T(8,128)S(1)} %all_to_all.25.pieces), custom_call_target="tpu_custom_call" | custom-call | bytes 2097152 | tf_op jit(solution)/shard_map/strips/pallas_call | solution.py:596
  66.0 3.4 %all-to-all-done.2 = f32[8,1,128]{2,1,0:T(1,128)S(1)} async-done(((f32[8,1,128]{2,1,0:T(1,128)}), f32[8,1,128]{2,1,0:T(1,128)S(1)}, u32[]{:S(2)}, u32[]{:S(2)}) %all-to-all-start.2) | async-done | bytes 4128 | tf_op jit(solution)/shard_map/all_to_all | solution.py:594
  69.5 0.6 reduce_max.9
Async XLA Ops:
  3.6 5.2 %collective-permute-start = (f32[128,128]{1,0:T(8,128)S(1)}, f32[128,128]{1,0:T(8,128)S(1)}, u32[]{:S(2)}, u32[]{:S(2)}) collective-permute-start(f32[128,128]{1,0:T(8,128)S(1)} %get-tuple-element.15), channel_id=1, source_target_pairs={{0,1},{1,0},{2,3},{3,2},{4,5},{5,4},{6,7},{7,6},{8,9},{9,8},{10,11... | collective-permute-start | bytes 196616 | tf_op jit(solution)/shard_map/ppermute | solution.py:521
  5.1 5.6 %collective-permute-start.1 = (f32[128,128]{1,0:T(8,128)S(1)}, f32[128,128]{1,0:T(8,128)S(1)}, u32[]{:S(2)}, u32[]{:S(2)}) collective-permute-start(f32[128,128]{1,0:T(8,128)S(1)} %get-tuple-element.16), channel_id=1, source_target_pairs={{0,15},{1,2},{2,1},{3,4},{4,3},{5,6},{6,5},{7,8},{8,7},{9,10},{10,... | collective-permute-start | bytes 196616 | tf_op jit(solution)/shard_map/ppermute | solution.py:520
  10.8 23.1 %collective-permute-start.2 = (f32[36,640]{1,0:T(8,128)S(1)}, f32[36,640]{1,0:T(8,128)S(1)}, u32[]{:S(2)}, u32[]{:S(2)}) collective-permute-start(f32[36,640]{1,0:T(8,128)S(1)} %get-tuple-element.22.near_sent), channel_id=1, source_target_pairs={{0,16},{16,0},{32,48},{48,32},{64,80},{80,64},{96,112},{112,96},{1... | collective-permute-start | bytes 276488 | tf_op jit(solution)/shard_map/ppermute | solution.py:534
  12.2 21.7 %collective-permute-start.3 = (f32[36,640]{1,0:T(8,128)S(1)}, f32[36,640]{1,0:T(8,128)S(1)}, u32[]{:S(2)}, u32[]{:S(2)}) collective-permute-start(f32[36,640]{1,0:T(8,128)S(1)} %get-tuple-element.23.far_sent), channel_id=1, source_target_pairs={{0,112},{16,32},{32,16},{48,64},{64,48},{80,96},{96,80},{112,0},{1... | collective-permute-start | bytes 276488 | tf_op jit(solution)/shard_map/ppermute | solution.py:535
  15.1 18.8 %all-to-all-start = ((f32[128,1,128]{2,1,0:T(1,128)}), f32[128,1,128]{2,1,0:T(1,128)S(1)}, u32[]{:S(2)}, u32[]{:S(2)}) async-start(f32[128,1,128]{2,1,0:T(1,128)} %bitcast.2), calls=%async_computation | async-start | bytes 131072 | tf_op jit(solution)/shard_map/all_to_all | solution.py:523
  24.5 9.4 %copy-start = (s32[8,16]{1,0:T(8,128)S(1)}, s32[8,16]{1,0:T(8,128)}, u32[]{:S(2)}) copy-start(s32[8,16]{1,0:T(8,128)} %owner_map.1) | copy-start | bytes 1540
  61.2 8.2 %all-to-all-start.2 = ((f32[8,1,128]{2,1,0:T(1,128)}), f32[8,1,128]{2,1,0:T(1,128)S(1)}, u32[]{:S(2)}, u32[]{:S(2)}) async-start(f32[8,1,128]{2,1,0:T(1,128)} %bitcast.5), calls=%async_computation.2 | async-start | bytes 8192 | tf_op jit(solution)/shard_map/all_to_all | solution.py:594

commit v9 on v8

--- a/solution.py
+++ b/solution.py
@@ -85,11 +85,12 @@
     to_south,
     core_pack,
     chip_pack,
-    peak,
+    peak_hbm,
     film,
     gas,
     deposit,
     flags,
+    peak,
     sems,
 ):
     pairs = [(flags_hbm, flags), (deposit_hbm, deposit)]
@@ -138,6 +139,8 @@
                 for row in range(0, ROWS, STRIP):
                     best = jnp.maximum(best, speed[row : row + STRIP])
             peak[...] = jnp.broadcast_to(jnp.max(best, keepdims=True), (ROWS, LANES))
+            leaving = pltpu.make_async_copy(peak, peak_hbm, sems.at[9])
+            leaving.start()
     for field in range(3):
         copies[6 + field].wait()
         for tile, cols in enumerate(tiles):
@@ -150,6 +153,7 @@
                 f, tile, AHEAD + rows.start : AHEAD + rows.stop, :
             ],
         )
+    leaving.wait()
 
 
 def even_wall():
@@ -502,13 +506,14 @@
             shape(ROWS, LANES),
         ),
         in_specs=[pl.BlockSpec(memory_space=pltpu.HBM)] * 4,
-        out_specs=tuple(vmem(6)),
+        out_specs=(*vmem(5), pl.BlockSpec(memory_space=pltpu.HBM)),
         scratch_shapes=[
             pltpu.VMEM((4, ROWS, COLS), jnp.float32),
             pltpu.VMEM((3, 4, ROWS, COLS), jnp.float32),
             pltpu.VMEM((ROWS, COLS), jnp.float32),
             pltpu.VMEM((TILES, ROWS), jnp.int32),
-            pltpu.SemaphoreType.DMA((9,)),
+            pltpu.VMEM((ROWS, LANES), jnp.float32),
+            pltpu.SemaphoreType.DMA((10,)),
         ],
         compiler_params=pltpu.CompilerParams(vmem_limit_bytes=VMEM_LIMIT),
         name="edges",

time: 70.5 us -> 70.1 us (level)
  no operation moved by 1% of the time
where the time goes in v9:
time: 70.1 us; the launch traced here: 69.6 us
  blocking collectives  22.6 us (32%)
  starting transfers between devices  22.1 us (32%)
  waiting for transfers between devices  12.5 us (18%)
  Pallas kernels  11.2 us (16%)
    all_to_all x1, blocking collectives, coupling_step(): lax.all_to_all(pieces, 'gas', split_axis=0, concat_axis=0, tiled=True)  22.6 us
    all_to_all x1, starting transfers between devices, coupling_step(): peaks = lax.all_to_all(peak, both, split_axis=0, concat_axis=0, tiled=True)  9.36 us
    all_to_all x1, waiting for transfers between devices, coupling_step(): peaks = lax.all_to_all(peak, both, split_axis=0, concat_axis=0, tiled=True)  7.15 us
    pallas_call x1, Pallas kernels, coupling_step(): pl.pallas_call(film_kernel, out_shape=(shape(gases, 4 * TILES + 1, STRIP,...  4.09 us
    ppermute x1, starting transfers between devices, coupling_step(): chip_side = lax.ppermute(chip_pack, 'gas', outer)  3.69 us
    all_to_all x1, waiting for transfers between devices, coupling_step(): lax.all_to_all(band_peak, 'wall', split_axis=0, concat_axis=0, tiled=True)  3.41 us
    all_to_all x1, starting transfers between devices, coupling_step(): lax.all_to_all(band_peak, 'wall', split_axis=0, concat_axis=0, tiled=True)  3.28 us
    ppermute x1, starting transfers between devices, coupling_step(): from_far = lax.ppermute(far, 'wall', distant)  2.92 us
  transfers between devices with their start and end apart: 6, of which 3 were waited for; matrix products, arithmetic and copies ran while one was open for 0% of the time, Pallas kernels for 5%

profile of v9, /device:TPU:1, one launch (start us, length us, event | category | flops | bytes accessed | tf_op | source)
XLA Modules:
  0.0 69.6 jit_solution(5094578092678214007)
XLA Ops:
  0.6 2.6 %edges.1 = (f32[3,5,144,128]{3,2,1,0:T(8,128)S(1)}, f32[36,640]{1,0:T(8,128)S(1)}, f32[36,640]{1,0:T(8,128)S(1)}, f32[128,128]{1,0:T(8,128)S(1)}, f32[128,128]{1,0:T(8,128)S(1)}, /*index=5*/f32[128,128]{1,0:T(8,128)}) custom-call(f32[3,4,128,512]{3,2,1,0:T(8,128)} %gas_hbm.1, s32[4,128]{1,0:T(4,128)} %bitcast.9, f32[4,128,512]{2,1,0:T(8,128)} %film_hbm.3, ...), custom_call_target="tpu_custom_call" | custom-call | tf_op jit(solution)/shard_map/edges/pallas_call | solution.py:498
  3.2 1.5 %collective-permute-start = (f32[128,128]{1,0:T(8,128)S(1)}, f32[128,128]{1,0:T(8,128)S(1)}, u32[]{:S(2)}, u32[]{:S(2)}) collective-permute-start(f32[128,128]{1,0:T(8,128)S(1)} %get-tuple-element.15), channel_id=1, source_target_pairs={{0,1},{1,0},{2,3},{3,2},{4,5},{5,4},{6,7},{7,6},{8,9},{9,8},{10,11... | collective-permute-start | bytes 196616 | tf_op jit(solution)/shard_map/ppermute | solution.py:526
  4.7 3.7 %collective-permute-start.1 = (f32[128,128]{1,0:T(8,128)S(1)}, f32[128,128]{1,0:T(8,128)S(1)}, u32[]{:S(2)}, u32[]{:S(2)}) collective-permute-start(f32[128,128]{1,0:T(8,128)S(1)} %get-tuple-element.16), channel_id=1, source_target_pairs={{0,15},{1,2},{2,1},{3,4},{4,3},{5,6},{6,5},{7,8},{8,7},{9,10},{10,... | collective-permute-start | bytes 196616 | tf_op jit(solution)/shard_map/ppermute | solution.py:525
  8.3 0.0 collective-permute-done.core
  8.3 1.9 %collective-permute-done.1.chip = f32[128,128]{1,0:T(8,128)S(1)} collective-permute-done((f32[128,128]{1,0:T(8,128)S(1)}, f32[128,128]{1,0:T(8,128)S(1)}, u32[]{:S(2)}, u32[]{:S(2)}) %collective-permute-start.1) | collective-permute-done | bytes 65568 | tf_op jit(solution)/shard_map/ppermute | solution.py:525
  10.3 0.1 corners.1
  10.4 1.4 %collective-permute-start.2 = (f32[36,640]{1,0:T(8,128)S(1)}, f32[36,640]{1,0:T(8,128)S(1)}, u32[]{:S(2)}, u32[]{:S(2)}) collective-permute-start(f32[36,640]{1,0:T(8,128)S(1)} %get-tuple-element.22.near_sent), channel_id=1, source_target_pairs={{0,16},{16,0},{32,48},{48,32},{64,80},{80,64},{96,112},{112,96},{1... | collective-permute-start | bytes 276488 | tf_op jit(solution)/shard_map/ppermute | solution.py:539
  11.8 2.9 %collective-permute-start.3 = (f32[36,640]{1,0:T(8,128)S(1)}, f32[36,640]{1,0:T(8,128)S(1)}, u32[]{:S(2)}, u32[]{:S(2)}) collective-permute-start(f32[36,640]{1,0:T(8,128)S(1)} %get-tuple-element.23.far_sent), channel_id=1, source_target_pairs={{0,112},{16,32},{32,16},{48,64},{64,48},{80,96},{96,80},{112,0},{1... | collective-permute-start | bytes 276488 | tf_op jit(solution)/shard_map/ppermute | solution.py:540
  14.7 9.4 %all-to-all-start = ((f32[128,1,128]{2,1,0:T(1,128)}), f32[128,1,128]{2,1,0:T(1,128)S(1)}, u32[]{:S(2)}, u32[]{:S(2)}) async-start(f32[128,1,128]{2,1,0:T(1,128)} %bitcast.2), calls=%async_computation | async-start | bytes 131072 | tf_op jit(solution)/shard_map/all_to_all | solution.py:528
  24.1 0.0 copy-start
  24.1 2.2 %inside.1 = (f32[4,5,144,128]{3,2,1,0:T(8,128)S(1)}, f32[5,128,128]{2,1,0:T(8,128)S(1)}, f32[3,5,144,128]{3,2,1,0:T(8,128)S(1)}) custom-call(f32[3,5,144,128]{3,2,1,0:T(8,128)S(1)} %get-tuple-element.14.gas_in, f32[4,128,512]{2,1,0:T(8,128)} %film_hbm.3, s32[4,128]{1,0:T(4,128)} %bitcast.10, ...), custom_call_target="tpu_custom_call", output_to_operand_aliasing={{2}: (0, {})} | custom-call | flops 20971520 | bytes 8388608 | tf_op jit(solution)/shard_map/inside/pallas_call | solution.py:543
  26.3 7.2 %all-to-all-done = f32[128,1,128]{2,1,0:T(1,128)S(1)} async-done(((f32[128,1,128]{2,1,0:T(1,128)}), f32[128,1,128]{2,1,0:T(1,128)S(1)}, u32[]{:S(2)}, u32[]{:S(2)}) %all-to-all-start) | async-done | bytes 65568 | tf_op jit(solution)/shard_map/all_to_all | solution.py:528
  33.5 0.0 collective-permute-done.2.near
  33.5 0.0 collective-permute-done.3.far
  33.5 0.0 copy-done
  33.5 4.1 %film.1 = (f32[16,17,8,128]{3,2,1,0:T(8,128)S(1)}, f32[4,5,144,128]{3,2,1,0:T(8,128)S(1)}) custom-call(s32[8,16]{1,0:T(8,128)S(1)} %copy-done, f32[4,5,144,128]{3,2,1,0:T(8,128)S(1)} %get-tuple-element.17.ring_in, f32[5,128,128]{2,1,0:T(8,128)S(1)} %get-tuple-element.18.spray, ...), custom_call_target="tpu_custom_call", output_to_operand_aliasing={{1}: (1, {})} | custom-call | tf_op jit(solution)/shard_map/film/pallas_call | solution.py:564
  37.6 22.6 %all_to_all.25.pieces = f32[16,17,8,128]{3,2,1,0:T(8,128)S(1)} all-to-all(f32[16,17,8,128]{3,2,1,0:T(8,128)S(1)} %get-tuple-element.25), channel_id=1, replica_groups=mesh['wall'=8,'gas'=16] {'gas'}, dimensions={0} | all-to-all | bytes 2228224 | tf_op jit(solution)/shard_map/all_to_all | solution.py:589
  60.2 0.6 band_peak.1
  60.8 3.3 %all-to-all-start.2 = ((f32[8,1,128]{2,1,0:T(1,128)}), f32[8,1,128]{2,1,0:T(1,128)S(1)}, u32[]{:S(2)}, u32[]{:S(2)}) async-start(f32[8,1,128]{2,1,0:T(1,128)} %bitcast.5), calls=%async_computation.2 | async-start | bytes 8192 | tf_op jit(solution)/shard_map/all_to_all | solution.py:599
  64.1 1.5 %strips.1 = f32[4,8,8192]{2,1,0:T(8,128)} custom-call(f32[16,17,8,128]{3,2,1,0:T(8,128)S(1)} %all_to_all.25.pieces), custom_call_target="tpu_custom_call" | custom-call | bytes 2097152 | tf_op jit(solution)/shard_map/strips/pallas_call | solution.py:601
  65.6 3.4 %all-to-all-done.2 = f32[8,1,128]{2,1,0:T(1,128)S(1)} async-done(((f32[8,1,128]{2,1,0:T(1,128)}), f32[8,1,128]{2,1,0:T(1,128)S(1)}, u32[]{:S(2)}, u32[]{:S(2)}) %all-to-all-start.2) | async-done | bytes 4128 | tf_op jit(solution)/shard_map/all_to_all | solution.py:599
  69.0 0.6 reduce_max.9
Async XLA Ops:
  3.2 5.2 %collective-permute-start = (f32[128,128]{1,0:T(8,128)S(1)}, f32[128,128]{1,0:T(8,128)S(1)}, u32[]{:S(2)}, u32[]{:S(2)}) collective-permute-start(f32[128,128]{1,0:T(8,128)S(1)} %get-tuple-element.15), channel_id=1, source_target_pairs={{0,1},{1,0},{2,3},{3,2},{4,5},{5,4},{6,7},{7,6},{8,9},{9,8},{10,11... | collective-permute-start | bytes 196616 | tf_op jit(solution)/shard_map/ppermute | solution.py:526
  4.7 5.6 %collective-permute-start.1 = (f32[128,128]{1,0:T(8,128)S(1)}, f32[128,128]{1,0:T(8,128)S(1)}, u32[]{:S(2)}, u32[]{:S(2)}) collective-permute-start(f32[128,128]{1,0:T(8,128)S(1)} %get-tuple-element.16), channel_id=1, source_target_pairs={{0,15},{1,2},{2,1},{3,4},{4,3},{5,6},{6,5},{7,8},{8,7},{9,10},{10,... | collective-permute-start | bytes 196616 | tf_op jit(solution)/shard_map/ppermute | solution.py:525
  10.4 23.1 %collective-permute-start.2 = (f32[36,640]{1,0:T(8,128)S(1)}, f32[36,640]{1,0:T(8,128)S(1)}, u32[]{:S(2)}, u32[]{:S(2)}) collective-permute-start(f32[36,640]{1,0:T(8,128)S(1)} %get-tuple-element.22.near_sent), channel_id=1, source_target_pairs={{0,16},{16,0},{32,48},{48,32},{64,80},{80,64},{96,112},{112,96},{1... | collective-permute-start | bytes 276488 | tf_op jit(solution)/shard_map/ppermute | solution.py:539
  11.8 21.7 %collective-permute-start.3 = (f32[36,640]{1,0:T(8,128)S(1)}, f32[36,640]{1,0:T(8,128)S(1)}, u32[]{:S(2)}, u32[]{:S(2)}) collective-permute-start(f32[36,640]{1,0:T(8,128)S(1)} %get-tuple-element.23.far_sent), channel_id=1, source_target_pairs={{0,112},{16,32},{32,16},{48,64},{64,48},{80,96},{96,80},{112,0},{1... | collective-permute-start | bytes 276488 | tf_op jit(solution)/shard_map/ppermute | solution.py:540
  14.7 18.8 %all-to-all-start = ((f32[128,1,128]{2,1,0:T(1,128)}), f32[128,1,128]{2,1,0:T(1,128)S(1)}, u32[]{:S(2)}, u32[]{:S(2)}) async-start(f32[128,1,128]{2,1,0:T(1,128)} %bitcast.2), calls=%async_computation | async-start | bytes 131072 | tf_op jit(solution)/shard_map/all_to_all | solution.py:528
  24.1 9.4 %copy-start = (s32[8,16]{1,0:T(8,128)S(1)}, s32[8,16]{1,0:T(8,128)}, u32[]{:S(2)}) copy-start(s32[8,16]{1,0:T(8,128)} %owner_map.1) | copy-start | bytes 1540
  60.8 8.2 %all-to-all-start.2 = ((f32[8,1,128]{2,1,0:T(1,128)}), f32[8,1,128]{2,1,0:T(1,128)S(1)}, u32[]{:S(2)}, u32[]{:S(2)}) async-start(f32[8,1,128]{2,1,0:T(1,128)} %bitcast.5), calls=%async_computation.2 | async-start | bytes 8192 | tf_op jit(solution)/shard_map/all_to_all | solution.py:599
